TPU v7x, 256 devices: a whole 4x4x8 slice. The times are simulated.
256 devices in a mesh: comp: 2 (over core), gx: 32 (over z, y), gy: 4 (over x).
Axes of the slice: x: 4, y: 4, z: 8, core: 2. Of those that a mesh axis runs over, the one named last changes fastest.
Arguments:
- atm_state: float32 [2, 72, 128, 4096], P('comp', None, 'gy', 'gx'), may hold values from -6 to 6
- atm_mass: float32 [128, 4096], P('gy', 'gx'), may hold values from 0.5 to 2
- coupler: float32 [16, 72], replicated, may hold values from -0.75 to 0.75
- flux_dest: int32 [4, 2048, 1], P('gy', 'gx'), may hold values from 0 to 31; in each aligned block of 64 rows (0 to 63, 64 to 127, ..., all dimensions but the last counted through in order) at most 6 rows name the same one
- flux_dst_blk: int32 [4, 2048], P('gy', 'gx'), may hold values from 0 to 15
- flux_src_blk: int32 [4, 2048], P('gy', 'gx'), may hold values from 0 to 31
- conservative_flux_weights: bfloat16 [4, 2048, 128, 128], P('gy', 'gx'), may hold values from -0.25 to 0.25
- ocn_tracers: float32 [2, 2, 80, 64, 4096], P('comp', None, None, 'gy', 'gx'), may hold values from -6 to 6
- ocean_neighbour_codes: int32 [6, 64, 4096], P(None, 'gy', 'gx'), may hold values from 0 to 7, as said below
- ocn_rates: float32 [6, 64, 4096], P(None, 'gy', 'gx'), may hold values from 0.03 to 0.15
- lev_speed: float32 [80], replicated, may hold values from 0.3 to 1
- profile: float32 [2, 80, 16], replicated, may hold values from -0.6 to 0.6
- back_owner: int32 [4, 2048], P('gy', 'gx'), may hold values from 0 to 31
- back_src_blk: int32 [4, 2048], P('gy', 'gx'), may hold values from 0 to 15
- back_dst_blk: int32 [4, 2048], P('gy', 'gx'), may hold values from 0 to 31
- return_remap_weights: bfloat16 [4, 2048, 128, 128], P('gy', 'gx'), may hold values from -0.375 to 0.375
Outputs:
- dss_out: float32 [2, 72, 128, 4096], P('comp', None, 'gy', 'gx')
- sfc_out: float32 [2, 2, 128, 4096], P('comp', None, 'gy', 'gx')
- ocn_out: float32 [2, 2, 80, 64, 4096], P('comp', None, None, 'gy', 'gx')
Inputs may be any that keep to these rules, and one draw needn't show every extreme that they name: `flux_dest`: the 64 rows of one holder name one ocean owner at most 6 times, and 6 times in some holder. `ocean_neighbour_codes`: the 6 codes of a cell are distinct.
All inputs are finite; a program needn't handle non-finite values.
Results may differ from a plain program's by a relative error of at most 0.0037.
Values may be sent and summed in bfloat16 or wider, within the bound.
No kernel may reach another device: no remote copies, remote signals or barrier semaphores. Data moves between devices by JAX's collectives and lax.ppermute only.
A program may use at most 128 MiB of HBM per device.

v0:
```python
import functools

import jax
import jax.numpy as jnp
from jax import lax
from jax.experimental import pallas as pl
from jax.experimental.pallas import tpu as pltpu
from jax.sharding import PartitionSpec as P

F32 = jnp.float32
BF16 = jnp.bfloat16
ADV = 4
W = 128
PR = 176
EXT = 24
SLOTS = 6
TILES_PER_PEER = 9


def lanes(rows):
    return lax.broadcasted_iota(jnp.int32, (rows, W), 1)


def fetch(src, dst, sem):
    copy = pltpu.make_async_copy(src, dst, sem)
    copy.start()
    copy.wait()


def split(value):
    hi = value.astype(BF16)
    return hi, (value - hi.astype(F32)).astype(BF16)


def params():
    return pltpu.CompilerParams(vmem_limit_bytes=60 * 1024 * 1024)


def call(body, out_shape, n_smem, n_any, n_vmem, scratch):
    specs = (
        [pl.BlockSpec(memory_space=pltpu.SMEM)] * n_smem
        + [pl.BlockSpec(memory_space=pl.ANY)] * n_any
        + [pl.BlockSpec(memory_space=pltpu.VMEM)] * n_vmem
    )
    return pl.pallas_call(
        body,
        out_shape=out_shape,
        in_specs=specs,
        out_specs=[pl.BlockSpec(memory_space=pltpu.VMEM)] * len(out_shape),
        scratch_shapes=scratch,
        compiler_params=params(),
        name=body.__name__,
    )


def pack_rows(comp, state, tracer, mass, codes, rates, up, down, rate8, buf, sem):
    @pl.when(comp[0] == 0)
    def _():
        fetch(state, buf.at[pl.ds(0, 2304)], sem)
        for dst, y in ((up, 0), (down, 31)):
            m = jnp.broadcast_to(mass[y : y + 1, :], (8, W))
            parts = [buf[pl.ds(g * 256 + y, 8, stride=32), :] * m for g in range(9)] + [m]
            for p in range(5):
                hi, lo = split(jnp.concatenate(parts[2 * p : 2 * p + 2], axis=0))
                dst[16 * p : 16 * p + 16, :] = hi
                dst[80 + 16 * p : 96 + 16 * p, :] = lo

    @pl.when(comp[0] == 1)
    def _():
        fetch(tracer, buf, sem)
        for o in range(8):
            acc = jnp.zeros((16, W), F32)
            for k in range(6):
                rows = slice(16 * k, 16 * k + 16)
                acc = acc + jnp.where(codes[rows, :] == o, rates[rows, :], 0.0)
            rate8[16 * o : 16 * o + 16, :] = acc
        for dst, first in ((up, 0), (down, 12)):
            for j in range(ADV):
                y = first + j
                for p in range(10):
                    both = jnp.concatenate(
                        [buf[pl.ds(g * 128 + y, 8, stride=16), :] for g in (2 * p, 2 * p + 1)],
                        axis=0,
                    )
                    dst[j * PR + 16 * p : j * PR + 16 * p + 16, :] = both.astype(BF16)
                r = rate8[pl.ds(y, 8, stride=16), :]
                dst[j * PR + 160 : j * PR + 176, :] = jnp.concatenate([r, r], axis=0).astype(BF16)


def pack_columns(comp, state, tracer, mass, rate8, left, right, turned, buf, sem):
    lane = lanes(8)

    @pl.when(comp[0] == 0)
    def _():
        fetch(state, buf.at[pl.ds(0, 2304)], sem)
        for g in range(10):
            to_left = jnp.zeros((8, W), F32)
            to_right = jnp.zeros((8, W), F32)
            for y in range(32):
                v = jnp.broadcast_to(mass[y : y + 1, :], (8, W))
                if g < 9:
                    v = v * buf[pl.ds(g * 256 + y, 8, stride=32), :]
                turned[80 * y + 8 * g : 80 * y + 8 * g + 8, :] = v
                v = pltpu.roll(v, y, 1)
                to_left = jnp.where(lane == y, v, to_left)
                to_right = jnp.where(lane == (y - 1) % W, v, to_right)
            left[8 * g : 8 * g + 8, :] = to_left
            right[8 * g : 8 * g + 8, :] = to_right

    @pl.when(comp[0] == 1)
    def _():
        fetch(tracer, buf, sem)
        for g in range(21):
            to_left = jnp.zeros((8, W), F32)
            to_right = jnp.zeros((8, W), F32)
            for y in range(16):
                i = y + ADV
                if g < 20:
                    v = buf[pl.ds(g * 128 + y, 8, stride=16), :]
                    turned[160 * y + 8 * g : 160 * y + 8 * g + 8, :] = v
                else:
                    v = rate8[pl.ds(y, 8, stride=16), :]
                v = pltpu.roll(v, 4 * i, 1)
                to_left = jnp.where(lane // 4 == i, v, to_left)
                to_right = jnp.where(lane // 4 == i - 1, v, to_right)
            left[8 * g : 8 * g + 8, :] = to_left
            right[8 * g : 8 * g + 8, :] = to_right
        left[168:176, :] = jnp.zeros((8, W), F32)
        right[168:176, :] = jnp.zeros((8, W), F32)


def finish_columns(comp, raw_left, raw_right, above, below, left, right):
    lane = lanes(16)

    @pl.when(comp[0] == 0)
    def _():
        for p in range(5):
            rows = slice(16 * p, 16 * p + 16)
            low = slice(80 + 16 * p, 96 + 16 * p)
            up = above[rows, :].astype(F32) + above[low, :].astype(F32)
            down = below[rows, :].astype(F32) + below[low, :].astype(F32)
            down = pltpu.roll(down, 31, 1)
            for src, dst, at in ((raw_left, left, 0), (raw_right, right, 1)):
                v = src[rows, :]
                pos = (lane + at) % 4
                before = jnp.where(lane == (W - at) % W, up, pltpu.roll(v, 1, 1))
                after = jnp.where(lane == 31 - at, down, pltpu.roll(v, W - 1, 1))
                v = v + jnp.where(pos == 0, before, 0.0) + jnp.where(pos == 3, after, 0.0)
                hi, lo = split(v)
                dst[rows, :] = hi
                dst[low, :] = lo

    @pl.when(comp[0] == 1)
    def _():
        for p in range(11):
            rows = slice(16 * p, 16 * p + 16)
            to_left = raw_left[rows, :]
            to_right = raw_right[rows, :]
            for src, first in ((above, 0), (below, 20)):
                for j in range(ADV):
                    i = first + j
                    v = src[j * PR + 16 * p : j * PR + 16 * p + 16, :].astype(F32)
                    v = pltpu.roll(v, 4 * i, 1)
                    to_left = jnp.where(lane // 4 == i, v, to_left)
                    to_right = jnp.where(lane // 4 == (i - 1) % 32, v, to_right)
            left[rows, :] = to_left.astype(BF16)
            right[rows, :] = to_right.astype(BF16)


def swap_left(a, b):
    lane = lanes(a.shape[0])
    ra, rb = pltpu.roll(a, W - 1, 1), pltpu.roll(b, W - 1, 1)
    return jnp.where(lane == W - 1, rb, ra), jnp.where(lane == W - 1, ra, rb)


def swap_right(a, b):
    lane = lanes(a.shape[0])
    ra, rb = pltpu.roll(a, 1, 1), pltpu.roll(b, 1, 1)
    return jnp.where(lane == 0, rb, ra), jnp.where(lane == 0, ra, rb)


def halo_tile(from_right, from_left, i):
    lane = lanes(8)
    v = jnp.where(lane // 4 == i, from_right, from_left)
    v = pltpu.roll(v, (W - 4 * i) % W, 1)
    return jnp.where((lane < 4) | (lane >= W - 4), v, 0.0)


def extended(g, i, main, above, below, halo_l, halo_r):
    rows = slice(8 * g, 8 * g + 8)
    half = slice(8 * (g % 2), 8 * (g % 2) + 8)
    pair = 16 * (g // 2)

    def wide(ref, at):
        return ref[at : at + 16, :].astype(F32)[half]

    if i < ADV:
        a = wide(above, i * PR + pair)
    elif i >= EXT - ADV:
        a = wide(below, (i - EXT + ADV) * PR + pair)
    else:
        a = main(g, i - ADV)
    b = halo_tile(wide(halo_r, pair), wide(halo_l, pair), i)
    return a, b


RIGHTWARD = (2, 4, 7)
LEFTWARD = (0, 3, 5)


def prepare_rates(coef_a, coef_b, rate8, above, below, halo_l, halo_r):
    sub = lax.broadcasted_iota(jnp.int32, (8, W), 0)
    right = (sub == 2) | (sub == 4) | (sub == 7)
    left = (sub == 0) | (sub == 3) | (sub == 5)

    def main(g, y):
        return rate8[pl.ds(y, 8, stride=16), :]

    for i in range(EXT):
        a, b = extended(20, i, main, above, below, halo_l, halo_r)
        la, lb = swap_left(a, b)
        ra, rb = swap_right(a, b)
        coef_a[i * 16 : i * 16 + 8, :] = jnp.where(right, ra, jnp.where(left, la, a))
        coef_b[i * 16 : i * 16 + 8, :] = jnp.where(right, rb, jnp.where(left, lb, b))
        coef_a[i * 16 + 8 : i * 16 + 16, :] = jnp.broadcast_to(
            jnp.sum(a, axis=0, keepdims=True), (8, W)
        )
        coef_b[i * 16 + 8 : i * 16 + 16, :] = jnp.broadcast_to(
            jnp.sum(b, axis=0, keepdims=True), (8, W)
        )


def level_speeds(lev_speed, groups):
    sub = lax.broadcasted_iota(jnp.int32, (8, W), 0)
    speeds = []
    for g in groups:
        v = jnp.zeros((8, W), F32)
        for k in range(8):
            v = jnp.where(sub == k, lev_speed[(8 * g + k) % 80], v)
        speeds.append(v)
    return speeds


def fill(groups, ta, tb, main, above, below, halo_l, halo_r):
    wide = 8 * len(groups)
    for n, g in enumerate(groups):
        for part in range(3):
            span = range(8 * part, 8 * part + 8)
            pairs = [extended(g, i, main, above, below, halo_l, halo_r) for i in span]
            for i, (a, b) in zip(span, pairs):
                ta[i * wide + 8 * n : i * wide + 8 * n + 8, :] = a
                tb[i * wide + 8 * n : i * wide + 8 * n + 8, :] = b


def advect_cell(cells, coefs, speed):
    outs = []
    for (t0, t1, t2), c in zip(cells, coefs):
        to_r = c[2] * t0 + c[4] * t1 + c[7] * t2
        to_l = c[0] * t0 + c[3] * t1 + c[5] * t2
        mid = c[1] * t0 + c[6] * t2 - c[8] * t1
        outs.append((t1, to_r, to_l, mid))
    (a1, ar, al, am), (b1, br, bl, bm) = outs
    ua, ub = swap_left(ar, br)
    va, vb = swap_right(al, bl)
    return a1 + speed * (am + ua + va), b1 + speed * (bm + ub + vb)


def advect(pairs, coef_a, coef_b, speed, count, chunk, result):
    wide = count * 8

    def at(i, n):
        return pl.ds(pl.multiple_of(i * wide + 8 * n, 8), 8)

    for step in range(ADV):
        now, later = pairs[step % 2], pairs[(step + 1) % 2]
        last = step == ADV - 1

        def row(i, carry, now=now, later=later, last=last):
            def coef(ref, o):
                return jnp.broadcast_to(ref[pl.ds(i * 16 + o, 1), :], (8, W))

            coefs = [[coef(ref, o) for o in range(9)] for ref in (coef_a, coef_b)]
            for base in range(0, count, chunk):
                span = range(base, base + chunk)
                news = []
                for n in span:
                    cells = [[t[at(k, n), :] for k in (i - 1, i, i + 1)] for t in now]
                    news.append(advect_cell(cells, coefs, speed[8 * n : 8 * n + 8, :]))
                for n, (new_a, new_b) in zip(span, news):
                    if last:
                        place = pl.multiple_of((i - ADV) * wide + 8 * n, 8)
                        result[pl.ds(place, 8), :] = new_a
                    else:
                        later[0][at(i, n), :] = new_a
                        later[1][at(i, n), :] = new_b
            return carry

        lax.fori_loop(step + 1, EXT - 1 - step, row, 0)


def assemble(
    comp, lev_speed, turned, rate8, above, below, halo_l, halo_r, lhs,
    dss, own, flux, top, coef_a, coef_b,
    buf, sem, edge, high, low, far_l, far_r, ta, tb, tc, td,
):
    lane = lanes(8)

    @pl.when(comp[0] == 0)
    def _():
        copy = pltpu.make_async_copy(turned, buf.at[pl.ds(80, 2560)], sem)
        copy.start()
        for p in range(5):
            rows = slice(16 * p, 16 * p + 16)
            rest = slice(80 + 16 * p, 96 + 16 * p)
            v = halo_l[rows, :].astype(F32) + halo_l[rest, :].astype(F32)
            far_l[rows, :] = pltpu.roll(v, 2, 1)
            far_r[rows, :] = halo_r[rows, :].astype(F32) + halo_r[rest, :].astype(F32)
            v = above[rows, :].astype(F32) + above[rest, :].astype(F32)
            buf[16 * p : 16 * p + 16, :] = v
            v = below[rows, :].astype(F32) + below[rest, :].astype(F32)
            buf[2640 + 16 * p : 2656 + 16 * p, :] = v
        for g in range(10):
            rows = slice(8 * g, 8 * g + 8)
            from_l, from_r = far_l[rows, :], far_r[rows, :]
            for y in range(32):
                v = jnp.where(lane == y, from_r, from_l)
                at = 80 * y + 8 * g
                edge[at : at + 8, :] = pltpu.roll(v, (W - 1 - y) % W, 1)
        copy.wait()

        def quad(q, carry):
            first = lane % 4 == 0
            final = lane % 4 == 3
            outer = (lane == 0) | (lane == W - 1)

            def at(row, g, wide=80):
                return pl.ds(pl.multiple_of(row * wide + 8 * g, 8), 8)

            for r in range(4):
                y = 4 * q + r
                values = []
                for g in (9, 0, 1, 2, 3, 4, 5, 6, 7, 8):
                    v = buf[at(y + 1, g), :]
                    if r == 0:
                        v = v + buf[at(y, g), :]
                    if r == 3:
                        v = v + buf[at(y + 2, g), :]
                    near = jnp.where(first, pltpu.roll(v, 1, 1), pltpu.roll(v, W - 1, 1))
                    near = jnp.where(outer, edge[at(y, g), :], near)
                    v = v + jnp.where(first | final, near, 0.0)
                    if g == 9:
                        inverse = 1.0 / v
                    else:
                        values.append(v * inverse)
                for g, v in enumerate(values):
                    dss[at(y, g, 72), :] = v
                hi, lo = split(jnp.concatenate(values + [jnp.zeros((8, W), F32)], axis=0))
                high[y] = hi
                low[y] = lo
            return carry

        lax.fori_loop(0, 8, quad, 0)
        for y in range(32):
            first = jnp.dot(lhs[...], high[y], preferred_element_type=F32)
            second = jnp.dot(lhs[0:32, :], low[y], preferred_element_type=F32)
            total = first[0:32] + first[32:64] + second
            flux[y] = total[0:16].astype(BF16)
            hi, lo = split(total[16:32])
            own[y, 0:16] = hi
            own[y, 16:32] = lo

    @pl.when(comp[0] == 1)
    def _():
        copy = pltpu.make_async_copy(turned, buf.at[pl.ds(80, 2560)], sem)
        copy.start()
        prepare_rates(coef_a, coef_b, rate8, above, below, halo_l, halo_r)
        copy.wait()

        def main(g, y):
            return buf[80 + 160 * y + 8 * g : 88 + 160 * y + 8 * g, :]

        sub = lax.broadcasted_iota(jnp.int32, (8, W), 0)
        for i in range(EXT):
            first = extended(0, i, main, above, below, halo_l, halo_r)
            second = extended(10, i, main, above, below, halo_l, halo_r)
            for ref, u, v in zip((ta, tb), first, second):
                ref[8 * i : 8 * i + 8, :] = jnp.where(sub == 0, u, pltpu.roll(v, 1, 0))
        pairs = ((ta, tb), (tc, td))
        speed = lev_speed[0]
        for step in range(ADV):
            now, later = pairs[step % 2], pairs[(step + 1) % 2]
            for i in range(step + 1, EXT - 1 - step):
                new_a, new_b = advect_cell(
                    [[t[8 * k : 8 * k + 8, :] for k in (i - 1, i, i + 1)] for t in now],
                    [
                        [
                            jnp.broadcast_to(ref[16 * i + o : 16 * i + o + 1, :], (8, W))
                            for o in range(9)
                        ]
                        for ref in (coef_a, coef_b)
                    ],
                    speed,
                )
                later[0][8 * i : 8 * i + 8, :] = new_a
                later[1][8 * i : 8 * i + 8, :] = new_b
        for v in range(2):
            rows = [ta[pl.ds((ADV + y) * 8 + v, 8, stride=8), :] for y in (0, 8)]
            top[v] = jnp.concatenate(rows, axis=0).astype(BF16)


def tile_products(
    comp, me, src, dest, dst, own, arrived, weights, top, send, count, meta, parts
):
    band = send.shape[0] // TILES_PER_PEER
    tiles = weights.shape[0]

    lane8 = lanes(8)
    sub8 = lax.broadcasted_iota(jnp.int32, (8, W), 0)

    def product(lhs, t):
        return lax.dot_general(
            lhs[src[0, t]], weights[t], (((1,), (1,)), ((), ())), preferred_element_type=F32
        )

    @pl.when(comp[0] == 0)
    def _():
        for t in range(tiles):
            both = product(own, t)
            parts[8 * t : 8 * t + 8, :] = both[0:8] + both[16:24]
        pieces = []
        for v in range(2):
            for p in range(4):
                rows = [parts[pl.ds(128 * p + 64 * q + v, 8, stride=8), :] for q in range(2)]
                pieces.append(jnp.concatenate(rows, axis=0).astype(BF16))
        ids = jnp.zeros((8, W), F32)
        for t in range(tiles):
            named = jnp.where(sub8 == 0, dest[0, t], dst[0, t]).astype(F32)
            ids = jnp.where(lane8 % tiles == t, named, ids)
        pieces.append(jnp.concatenate([ids, ids], axis=0).astype(BF16))

        def spread(h, carry):
            for j, piece in enumerate(pieces):
                send[h * TILES_PER_PEER + j] = piece
            return carry

        lax.fori_loop(0, band, spread, 0)

    @pl.when(comp[0] == 1)
    def _():
        ids = jnp.where(sub8 == 0, me[0], lane8 % 16).astype(F32)
        ids = jnp.where((sub8 == 2) | (lane8 % tiles >= 16), -1.0, ids)

        def clear(h, carry):
            for j in range(TILES_PER_PEER):
                if j in (0, 4):
                    send[h * TILES_PER_PEER + j] = top[j // 4]
                else:
                    send[h * TILES_PER_PEER + j] = jnp.zeros((16, W), BF16)
            count[h] = 0
            meta[h] = ids
            return carry

        lax.fori_loop(0, band, clear, 0)
        for t in range(tiles):
            owner = dest[0, t]
            slot = count[owner]
            count[owner] = slot + 1
            place = slot + 1 + jnp.where(slot >= SLOTS // 2, 1, 0)
            send[owner * TILES_PER_PEER + place] = product(arrived, t).astype(BF16)
            named = jnp.where(
                (lane8 // 16 == place) & (sub8 == 2), dst[0, t].astype(F32), meta[owner]
            )
            meta[owner] = named

        def finish(h, carry):
            m = meta[h]
            send[h * TILES_PER_PEER + 8] = jnp.concatenate([m, m], axis=0).astype(BF16)
            return carry

        lax.fori_loop(0, band, finish, 0)


def advect_all(
    comp, lev_speed, turned, fields, above, below, halo_l, halo_r, coef_a, coef_b,
    result, dss, buf, sem, ta, tb, tc, td, speed,
):
    @pl.when(comp[0] == 0)
    def _():
        fetch(fields, buf.at[pl.ds(0, 2304)], sem)
        for f in range(72):
            for p in range(4):
                dss[32 * f + 8 * p : 32 * f + 8 * p + 8, :] = buf[
                    pl.ds(72 * 8 * p + f, 8, stride=72), :
                ]

    @pl.when(comp[0] == 1)
    def _():
        fetch(turned, buf, sem)
        dss[...] = jnp.zeros(dss.shape, F32)

        def main(g, y):
            return buf[160 * y + 8 * g : 160 * y + 8 * g + 8, :]

        groups = tuple(range(20))
        fill(groups, ta, tb, main, above, below, halo_l, halo_r)
        for n, v in enumerate(level_speeds(lev_speed, groups[:10])):
            speed[8 * n : 8 * n + 8, :] = v
            speed[80 + 8 * n : 88 + 8 * n, :] = v
        advect(((ta, tb), (tc, td)), coef_a, coef_b, speed, 20, 4, result)


def surface_select(back_owner, back_src, received, out):
    band = received.shape[0] // TILES_PER_PEER
    lane = lanes(1)
    sub8 = lax.broadcasted_iota(jnp.int32, (8, W), 0)
    wants = []
    for p in range(8):
        v = jnp.zeros((8, W), jnp.int32)
        for k in range(8):
            v = jnp.where(sub8 == k, back_owner[0, 8 * p + k] * 16 + back_src[0, 8 * p + k], v)
        wants.append(v)
    want = jnp.concatenate(wants, axis=0).astype(F32)

    def pair(q, carry):
        h = 2 * q
        ids = [
            received[(h + d) * TILES_PER_PEER + 8].astype(F32) for d in range(2)
        ]
        named = [v[0:1, :] * 16.0 + v[1:2, :] for v in ids]
        row = jnp.where(lane < 64, named[0], named[1])
        hot = jnp.where(jnp.broadcast_to(row, (64, W)) == want, 1.0, 0.0).astype(BF16)
        totals = []
        for v in range(2):
            rhs = jnp.concatenate(
                [
                    received[(h + d) * TILES_PER_PEER + 4 * v + j]
                    for d in range(2)
                    for j in range(4)
                ],
                axis=0,
            )
            totals.append(carry[v] + jnp.dot(hot, rhs, preferred_element_type=F32))
        return tuple(totals)

    zero = jnp.zeros((64, W), F32)
    sums = lax.fori_loop(0, band // 2, pair, (zero, zero), unroll=4)
    for v in range(2):
        out[64 * v : 64 * v + 64, :] = sums[v]


def surface_product(comp, back_dst, weights, mine, other, out, store, sem, table, parts, acc):
    tiles = weights.shape[0]

    @pl.when(comp[0] == 1)
    def _():
        out[...] = jnp.zeros(out.shape, F32)

    @pl.when(comp[0] == 0)
    def _():
        copy = pltpu.make_async_copy(weights, store, sem)
        copy.start()
        for v in range(2):
            rows = slice(64 * v, 64 * v + 64)
            hi, lo = split(mine[rows, :] + other[rows, :])
            for at, part in ((v, hi.astype(F32)), (2 + v, lo.astype(F32))):
                for p in range(8):
                    table[pl.ds(64 * p + at, 8, stride=8), :] = part[8 * p : 8 * p + 8]
        acc[...] = jnp.zeros(acc.shape, F32)
        copy.wait()
        for t in range(tiles):
            parts[8 * t : 8 * t + 8, :] = lax.dot_general(
                table[8 * t : 8 * t + 8, :].astype(BF16),
                store[t],
                (((1,), (1,)), ((), ())),
                preferred_element_type=F32,
            )
        for t in range(tiles):
            at = pl.ds(pl.multiple_of(back_dst[0, t] * 8, 8), 8)
            acc[at, :] = acc[at, :] + parts[8 * t : 8 * t + 8, :]
        for v in range(2):
            for p in range(4):
                out[32 * v + 8 * p : 32 * v + 8 * p + 8, :] = (
                    acc[pl.ds(64 * p + v, 8, stride=8), :]
                    + acc[pl.ds(64 * p + 2 + v, 8, stride=8), :]
                )


def force(comp, advected_ref, received_ref, profile, out, advected, received, sem, sem2):
    band = received.shape[0] // TILES_PER_PEER

    @pl.when(comp[0] == 0)
    def _():
        out[...] = jnp.zeros(out.shape, F32)

    @pl.when(comp[0] == 1)
    def _():
        late = pltpu.make_async_copy(advected_ref, advected, sem2)
        late.start()
        fetch(received_ref, received, sem)
        row = lax.broadcasted_iota(jnp.int32, (256, W), 0)
        point = jnp.where(row % 16 == lanes(256) % 16, row // 16, -2).astype(F32)

        def add(h, total):
            named = received[h * TILES_PER_PEER + 8].astype(F32)[2:3, :]
            hot = jnp.where(jnp.broadcast_to(named, (256, W)) == point, 1.0, 0.0)
            rhs = jnp.concatenate(
                [received[h * TILES_PER_PEER + j] for j in range(8)], axis=0
            )
            return total + jnp.dot(hot.astype(BF16), rhs, preferred_element_type=F32)

        total = lax.fori_loop(0, band, add, jnp.zeros((256, W), F32), unroll=4)
        level_hi, level_lo = split(profile[...])
        late.wait()
        for y in range(16):
            hi, lo = split(total[16 * y : 16 * y + 16, :])
            more = (
                jnp.dot(level_hi, hi, preferred_element_type=F32)
                + jnp.dot(level_hi, lo, preferred_element_type=F32)
                + jnp.dot(level_lo, hi, preferred_element_type=F32)
            )
            new = advected[160 * y : 160 * y + 160, :] + more
            for g in range(20):
                out[pl.ds(g * 128 + y, 8, stride=16), :] = new[8 * g : 8 * g + 8]


def shifted(array, axis, by):
    peers = lax.axis_size(axis)
    pairs = [(i, i + by) for i in range(peers) if 0 <= i + by < peers]
    return lax.ppermute(array, axis, pairs)


def shape(*dims, dtype=F32):
    return jax.ShapeDtypeStruct(dims, dtype)


def shards(
    atm_state,
    atm_mass,
    coupler,
    flux_dest,
    flux_dst_blk,
    flux_src_blk,
    conservative_flux_weights,
    ocn_tracers,
    ocean_neighbour_codes,
    ocn_rates,
    lev_speed,
    profile,
    back_owner,
    back_src_blk,
    back_dst_blk,
    return_remap_weights,
):
    comp = lax.axis_index("comp").astype(jnp.int32).reshape(1)
    band = lax.axis_size("gx")
    state = atm_state.reshape(72 * 32, W)
    tracer = ocn_tracers.reshape(2 * 80 * 16, W)
    codes = ocean_neighbour_codes.reshape(96, W)
    rates = ocn_rates.reshape(96, W)
    dma = pltpu.SemaphoreType.DMA
    buf = pltpu.VMEM((2560, W), F32)

    up, down, rate8 = call(
        pack_rows,
        [shape(4 * PR, W, dtype=BF16), shape(4 * PR, W, dtype=BF16), shape(128, W)],
        1, 2, 3,
        [buf, dma],
    )(comp, state, tracer, atm_mass, codes, rates)
    below = shifted(up, "gy", -1)
    above = shifted(down, "gy", 1)
    raw_left, raw_right, turned = call(
        pack_columns, [shape(PR, W), shape(PR, W), shape(2560, W)], 1, 2, 2, [buf, dma]
    )(comp, state, tracer, atm_mass, rate8)
    left, right = call(
        finish_columns,
        [shape(PR, W, dtype=BF16), shape(PR, W, dtype=BF16)],
        1, 0, 4,
        [],
    )(comp, raw_left, raw_right, above, below)
    halo_r = shifted(left, "gx", -1)
    halo_l = shifted(right, "gx", 1)

    top_profile = jnp.dot(profile[:, 0], coupler, precision=lax.Precision.HIGHEST)
    lhs = jnp.pad(jnp.concatenate([coupler, top_profile], axis=0), ((0, 14), (0, 8)))
    lhs_hi, lhs_lo = split(lhs)
    lhs = jnp.concatenate([lhs_hi, lhs_lo], axis=0)
    me = lax.axis_index("gx").astype(jnp.int32).reshape(1)
    small = pltpu.VMEM((EXT * 8, W), F32)

    fields, own, flux, top, coef_a, coef_b = call(
        assemble,
        [
            shape(72 * 32, W),
            shape(32, 32, W, dtype=BF16),
            shape(32, 16, W, dtype=BF16),
            shape(2, 16, W, dtype=BF16),
            shape(EXT * 16, W),
            shape(EXT * 16, W),
        ],
        2, 1, 6,
        [
            pltpu.VMEM((34 * 80, W), F32), dma, buf,
            pltpu.VMEM((32, 80, W), BF16), pltpu.VMEM((32, 80, W), BF16),
            pltpu.VMEM((80, W), F32), pltpu.VMEM((80, W), F32),
            small, small, small, small,
        ],
    )(comp, lev_speed, turned, rate8, above, below, halo_l, halo_r, lhs)
    arrived = shifted(flux, "comp", 1)
    send, = call(
        tile_products,
        [shape(band * TILES_PER_PEER, 16, W, dtype=BF16)],
        5, 0, 4,
        [
            pltpu.SMEM((band,), jnp.int32),
            pltpu.VMEM((band, 8, W), F32),
            pltpu.VMEM((512, W), F32),
        ],
    )(
        comp, me, flux_src_blk, flux_dest.reshape(1, 64), flux_dst_blk,
        own, arrived, conservative_flux_weights[0], top,
    )
    send, coef_a, coef_b = lax.optimization_barrier((send, coef_a, coef_b))
    received = lax.all_to_all(
        send.reshape(band, TILES_PER_PEER, 16, W), "gx", 0, 0, tiled=True
    ).reshape(band * TILES_PER_PEER, 16, W)
    grid = pltpu.VMEM((EXT * 160, W), F32)
    advected, dss = call(
        advect_all,
        [shape(16 * 160, W), shape(72 * 32, W)],
        2, 2, 6,
        [buf, dma, grid, grid, grid, grid, pltpu.VMEM((160, W), F32)],
    )(comp, lev_speed, turned, fields, above, below, halo_l, halo_r, coef_a, coef_b)
    levels = profile.reshape(160, 16)
    received, advected, levels = lax.optimization_barrier((received, advected, levels))
    mine, = call(surface_select, [shape(128, W)], 2, 0, 1, [])(
        back_owner, back_src_blk, received
    )
    other = shifted(mine, "comp", -1)
    ocean, = call(force, [shape(2560, W)], 1, 2, 1, [
        buf, pltpu.VMEM((band * TILES_PER_PEER, 16, W), BF16), dma, dma,
    ])(comp, advected, received, levels)
    tile_store = pltpu.VMEM(return_remap_weights.shape[1:], BF16)
    surface, = call(surface_product, [shape(64, W)], 2, 1, 2, [
        tile_store, dma,
        pltpu.VMEM((512, W), F32), pltpu.VMEM((512, W), F32), pltpu.VMEM((256, W), F32),
    ])(comp, back_dst_blk, return_remap_weights[0], mine, other)
    return (
        dss.reshape(1, 72, 32, W),
        surface.reshape(1, 2, 32, W),
        ocean.reshape(1, 2, 80, 16, W),
    )


def solution(mesh):
    placed = (
        P("comp", None, "gy", "gx"),
        P("gy", "gx"),
        P(),
        P("gy", "gx", None),
        P("gy", "gx"),
        P("gy", "gx"),
        P("gy", "gx", None, None),
        P("comp", None, None, "gy", "gx"),
        P(None, "gy", "gx"),
        P(None, "gy", "gx"),
        P(),
        P(),
        P("gy", "gx"),
        P("gy", "gx"),
        P("gy", "gx"),
        P("gy", "gx", None, None),
    )
    return jax.shard_map(
        shards,
        mesh=mesh,
        in_specs=placed,
        out_specs=(
            P("comp", None, "gy", "gx"),
            P("comp", None, "gy", "gx"),
            P("comp", None, None, "gy", "gx"),
        ),
        check_vma=False,
    )
```

profile of v0, /device:TPU:1, one launch (start us, length us, event | category | flops | bytes accessed | tf_op | source)
XLA Modules:
  0.0 101.9 jit_solution(6631159740385727939)
XLA Ops:
  0.6 3.2 %pack_rows.1 = (bf16[704,128]{1,0:T(8,128)(2,1)}, bf16[704,128]{1,0:T(8,128)(2,1)}, f32[128,128]{1,0:T(8,128)}) custom-call(s32[1]{0:T(128)} %bitcast.comp, f32[2304,128]{1,0:T(8,128)} %bitcast.22, f32[2560,128]{1,0:T(8,128)} %bitcast.19, f32[32,128]{1,0:T(8,128)} %mass.3, s32[96,128]{1,0:T(8,128)} %bitcast.28, f32[96,128]{1,0:T(8,128)} %bitcast.29), custom_call_target="tpu_custom_call" | custom-call | tf_op jit(solution)/shard_map/pack_rows/pallas_call | solution.py:663
  3.8 0.0 copy-start.8
  3.8 0.0 copy-start.6
  3.9 4.0 %collective-permute-start = (bf16[704,128]{1,0:T(8,128)(2,1)}, bf16[704,128]{1,0:T(8,128)(2,1)S(1)}, u32[]{:S(2)}, u32[]{:S(2)}) collective-permute-start(bf16[704,128]{1,0:T(8,128)(2,1)} %get-tuple-element.27), channel_id=1, source_target_pairs={{0,1},{1,2},{2,3},{4,5},{5,6},{6,7},{8,9},{9,10},{10,11},{12,13},{... | collective-permute-start | bytes 540680 | tf_op jit(solution)/shard_map/ppermute | solution.py:629
  7.8 1.3 %collective-permute-start.1 = (bf16[704,128]{1,0:T(8,128)(2,1)}, bf16[704,128]{1,0:T(8,128)(2,1)S(1)}, u32[]{:S(2)}, u32[]{:S(2)}) collective-permute-start(bf16[704,128]{1,0:T(8,128)(2,1)} %get-tuple-element.28), channel_id=1, source_target_pairs={{1,0},{2,1},{3,2},{5,4},{6,5},{7,6},{9,8},{10,9},{11,10},{13,12},{... | collective-permute-start | bytes 540680 | tf_op jit(solution)/shard_map/ppermute | solution.py:629
  9.1 3.8 %pack_columns.1 = (f32[176,128]{1,0:T(8,128)}, f32[176,128]{1,0:T(8,128)}, f32[2560,128]{1,0:T(8,128)}) custom-call(s32[1]{0:T(128)} %bitcast.comp, f32[2304,128]{1,0:T(8,128)} %bitcast.23, f32[2560,128]{1,0:T(8,128)} %bitcast.20, f32[32,128]{1,0:T(8,128)} %mass.3, f32[128,128]{1,0:T(8,128)} %get-tuple-element.25.rate8), custom_call_target="tpu_custom_call" | custom-call | tf_op jit(solution)/shard_map/pack_columns/pallas_call | solution.py:671
  12.9 0.0 copy-done.8
  12.9 0.1 slice_reduce_fusion
  13.0 0.0 copy-done.6
  13.0 0.1 fusion.1
  13.2 0.0 collective-permute-done.above
  13.2 0.0 copy-start.1
  13.2 2.1 %collective-permute-done.1.below = bf16[704,128]{1,0:T(8,128)(2,1)S(1)} collective-permute-done((bf16[704,128]{1,0:T(8,128)(2,1)}, bf16[704,128]{1,0:T(8,128)(2,1)S(1)}, u32[]{:S(2)}, u32[]{:S(2)}) %collective-permute-start.1) | collective-permute-done | bytes 180256 | tf_op jit(solution)/shard_map/ppermute | solution.py:629
  15.3 0.0 copy-start.2
  15.3 0.0 copy-done.1
  15.3 0.7 copy-done.2
  16.0 1.9 %finish_columns.1 = (bf16[176,128]{1,0:T(8,128)(2,1)}, bf16[176,128]{1,0:T(8,128)(2,1)}) custom-call(s32[1]{0:T(128)} %bitcast.comp, f32[176,128]{1,0:T(8,128)} %get-tuple-element.29.raw_left, f32[176,128]{1,0:T(8,128)} %get-tuple-element.30.raw_right, bf16[704,128]{1,0:T(8,128)(2,1)} %copy-done.1, bf16[704,128]{1,0:T(8,128)(2,1)} %copy-done.2), custom_call_target="tpu_custom_call" | custom-call | tf_op jit(solution)/shard_map/finish_columns/pallas_call | solution.py:674
  17.9 3.2 %collective-permute-start.2 = (bf16[176,128]{1,0:T(8,128)(2,1)}, bf16[176,128]{1,0:T(8,128)(2,1)S(1)}, u32[]{:S(2)}, u32[]{:S(2)}) collective-permute-start(bf16[176,128]{1,0:T(8,128)(2,1)} %get-tuple-element.31), channel_id=1, source_target_pairs={{0,4},{4,8},{8,12},{12,16},{16,20},{20,24},{24,28},{28,32},{32,36}... | collective-permute-start | bytes 135176 | tf_op jit(solution)/shard_map/ppermute | solution.py:629
  21.1 1.3 %collective-permute-start.3 = (bf16[176,128]{1,0:T(8,128)(2,1)}, bf16[176,128]{1,0:T(8,128)(2,1)S(1)}, u32[]{:S(2)}, u32[]{:S(2)}) collective-permute-start(bf16[176,128]{1,0:T(8,128)(2,1)} %get-tuple-element.32), channel_id=1, source_target_pairs={{4,0},{8,4},{12,8},{16,12},{20,16},{24,20},{28,24},{32,28},{36,32}... | collective-permute-start | bytes 135176 | tf_op jit(solution)/shard_map/ppermute | solution.py:629
  22.4 0.6 pad_maximum_fusion.lhs
  23.0 0.0 collective-permute-done.2.halo_l
  23.0 0.0 copy-start.3
  23.0 3.1 %collective-permute-done.3.halo_r = bf16[176,128]{1,0:T(8,128)(2,1)S(1)} collective-permute-done((bf16[176,128]{1,0:T(8,128)(2,1)}, bf16[176,128]{1,0:T(8,128)(2,1)S(1)}, u32[]{:S(2)}, u32[]{:S(2)}) %collective-permute-start.3) | collective-permute-done | bytes 45088 | tf_op jit(solution)/shard_map/ppermute | solution.py:629
  26.1 0.0 copy-start.4
  26.1 0.0 copy-done.3
  26.1 0.6 copy-done.4
  26.7 4.3 %assemble.1 = (f32[2304,128]{1,0:T(8,128)}, bf16[32,32,128]{2,1,0:T(8,128)(2,1)}, bf16[32,16,128]{2,1,0:T(8,128)(2,1)}, bf16[2,16,128]{2,1,0:T(8,128)(2,1)}, f32[384,128]{1,0:T(8,128)}, /*index=5*/f32[384,128]{1,0:T(8,128)}) custom-call(s32[1]{0:T(128)} %bitcast.comp, f32[80]{0:T(128)} %lev_speed.3, f32[2560,128]{1,0:T(8,128)} %get-tuple-element.26.turned, ...), custom_call_target="tpu_custom_call" | custom-call | tf_op jit(solution)/shard_map/assemble/pallas_call | solution.py:690
  30.9 1.3 %collective-permute-start.4 = (bf16[32,16,128]{2,1,0:T(8,128)(2,1)}, bf16[32,16,128]{2,1,0:T(8,128)(2,1)S(1)}, u32[]{:S(2)}, u32[]{:S(2)}) collective-permute-start(bf16[32,16,128]{2,1,0:T(8,128)(2,1)} %get-tuple-element.35), channel_id=1, source_target_pairs={{0,128},{1,129},{2,130},{3,131},{4,132},{5,133},{6,134},{7,135},{8... | collective-permute-start | bytes 393224 | tf_op jit(solution)/shard_map/ppermute | solution.py:629
  32.2 5.6 %collective-permute-done.4.arrived = bf16[32,16,128]{2,1,0:T(8,128)(2,1)S(1)} collective-permute-done((bf16[32,16,128]{2,1,0:T(8,128)(2,1)}, bf16[32,16,128]{2,1,0:T(8,128)(2,1)S(1)}, u32[]{:S(2)}, u32[]{:S(2)}) %collective-permute-start.4) | collective-permute-done | bytes 131104 | tf_op jit(solution)/shard_map/ppermute | solution.py:629
  37.9 0.0 copy-start.5
  37.9 0.7 copy-done.5
  38.5 4.5 %tile_products.1 = bf16[288,16,128]{2,1,0:T(8,128)(2,1)} custom-call(s32[1]{0:T(128)} %bitcast.comp, s32[1]{0:T(128)} %bitcast.5.me, s32[1,64]{1,0:T(1,128)} %src.1, s32[1,64]{1,0:T(1,128)} %bitcast.31, s32[1,64]{1,0:T(1,128)} %dst.1, bf16[32,32,128]{2,1,0:T(8,128)(2,1)} %get-tuple-element.34.own, bf16[32,16,128]{2,1,0:T(8,128)(2,1)} %copy-done.5, ...), custom_call_target="tpu_custom_call" | custom-call | tf_op jit(solution)/shard_map/tile_products/pallas_call | solution.py:709
  43.0 13.0 %all-to-all-start = ((bf16[32,9,16,128]{3,2,1,0:T(8,128)(2,1)}), bf16[32,9,16,128]{3,2,1,0:T(8,128)(2,1)S(1)}, u32[]{:S(2)}, u32[]{:S(2)}) async-start(bf16[32,9,16,128]{3,2,1,0:T(8,128)(2,1)} %bitcast.21), calls=%async_computation | async-start | bytes 2359296 | tf_op jit(solution)/shard_map/all_to_all | solution.py:723
  56.0 0.7 copy.20
  56.7 16.9 %advect_all.1 = (f32[2560,128]{1,0:T(8,128)}, f32[2304,128]{1,0:T(8,128)}) custom-call(s32[1]{0:T(128)} %bitcast.comp, f32[80]{0:T(128)} %lev_speed.3, f32[2560,128]{1,0:T(8,128)} %get-tuple-element.26.turned, f32[2304,128]{1,0:T(8,128)} %get-tuple-element.33.fields, bf16[704,128]{1,0:T(8,128)(2,1)} %copy-done.1, bf16[704,128]{1,0:T(8,128)(2,1)} %copy-done.2, ...), custom_call_target="tpu_custom_call" | custom-call | tf_op jit(solution)/shard_map/advect_all/pallas_call | solution.py:727
  73.6 12.3 %all-to-all-done = bf16[32,9,16,128]{3,2,1,0:T(8,128)(2,1)S(1)} async-done(((bf16[32,9,16,128]{3,2,1,0:T(8,128)(2,1)}), bf16[32,9,16,128]{3,2,1,0:T(8,128)(2,1)S(1)}, u32[]{:S(2)}, u32[]{:S(2)}) %all-to-all-start) | async-done | bytes 1179680 | tf_op jit(solution)/shard_map/all_to_all | solution.py:723
  85.9 0.0 copy-start
  85.9 1.0 copy-done
  86.9 2.8 %surface_select.1.mine = f32[128,128]{1,0:T(8,128)} custom-call(s32[1,64]{1,0:T(1,128)} %back_owner.1, s32[1,64]{1,0:T(1,128)} %back_src.1, bf16[288,16,128]{2,1,0:T(8,128)(2,1)} %bitcast.17), custom_call_target="tpu_custom_call" | custom-call | tf_op jit(solution)/shard_map/surface_select/pallas_call | solution.py:735
  89.7 3.8 %collective-permute-start.5 = (f32[128,128]{1,0:T(8,128)}, f32[128,128]{1,0:T(8,128)S(1)}, u32[]{:S(2)}, u32[]{:S(2)}) collective-permute-start(f32[128,128]{1,0:T(8,128)} %surface_select.1.mine), channel_id=1, source_target_pairs={{128,0},{129,1},{130,2},{131,3},{132,4},{133,5},{134,6},{135,7},{1... | collective-permute-start | bytes 196616 | tf_op jit(solution)/shard_map/ppermute | solution.py:629
  93.5 6.2 %force.1 = f32[2560,128]{1,0:T(8,128)} custom-call(s32[1]{0:T(128)} %bitcast.comp, f32[2560,128]{1,0:T(8,128)} %get-tuple-element.45.advected_ref, bf16[288,16,128]{2,1,0:T(8,128)(2,1)} %bitcast.18, f32[160,16]{1,0:T(8,128)} %bitcast.27), custom_call_target="tpu_custom_call" | custom-call | tf_op jit(solution)/shard_map/force/pallas_call | solution.py:739
  99.7 0.0 collective-permute-done.5.other
  99.7 0.0 copy-start.7
  99.7 0.6 copy-done.7
  100.3 1.5 %surface_product.1 = f32[64,128]{1,0:T(8,128)} custom-call(s32[1]{0:T(128)} %bitcast.comp, s32[1,64]{1,0:T(1,128)} %back_dst.1, bf16[64,128,128]{2,1,0:T(8,128)(2,1)} %bitcast.25, f32[128,128]{1,0:T(8,128)} %surface_select.1.mine, f32[128,128]{1,0:T(8,128)} %copy-done.7), custom_call_target="tpu_custom_call" | custom-call | tf_op jit(solution)/shard_map/surface_product/pallas_call | solution.py:743
  (2 shorter events, 0.0 us)
Async XLA Ops:
  3.8 9.1 %copy-start.8 = (f32[2,80,16]{1,2,0:T(8,128)S(1)}, f32[2,80,16]{1,2,0:T(8,128)}, u32[]{:S(2)}) copy-start(f32[2,80,16]{1,2,0:T(8,128)} %param.27) | copy-start | bytes 30724
  3.8 9.2 %copy-start.6 = (f32[16,72]{1,0:T(8,128)S(1)}, f32[16,72]{1,0:T(8,128)}, u32[]{:S(2)}) copy-start(f32[16,72]{1,0:T(8,128)} %param.18) | copy-start | bytes 13828
  3.9 9.3 %collective-permute-start = (bf16[704,128]{1,0:T(8,128)(2,1)}, bf16[704,128]{1,0:T(8,128)(2,1)S(1)}, u32[]{:S(2)}, u32[]{:S(2)}) collective-permute-start(bf16[704,128]{1,0:T(8,128)(2,1)} %get-tuple-element.27), channel_id=1, source_target_pairs={{0,1},{1,2},{2,3},{4,5},{5,6},{6,7},{8,9},{9,10},{10,11},{12,13},{... | collective-permute-start | bytes 540680 | tf_op jit(solution)/shard_map/ppermute | solution.py:629
  7.8 7.5 %collective-permute-start.1 = (bf16[704,128]{1,0:T(8,128)(2,1)}, bf16[704,128]{1,0:T(8,128)(2,1)S(1)}, u32[]{:S(2)}, u32[]{:S(2)}) collective-permute-start(bf16[704,128]{1,0:T(8,128)(2,1)} %get-tuple-element.28), channel_id=1, source_target_pairs={{1,0},{2,1},{3,2},{5,4},{6,5},{7,6},{9,8},{10,9},{11,10},{13,12},{... | collective-permute-start | bytes 540680 | tf_op jit(solution)/shard_map/ppermute | solution.py:629
  13.2 2.1 %copy-start.1 = (bf16[704,128]{1,0:T(8,128)(2,1)}, bf16[704,128]{1,0:T(8,128)(2,1)S(1)}, u32[]{:S(2)}) copy-start(bf16[704,128]{1,0:T(8,128)(2,1)S(1)} %collective-permute-done.above) | copy-start | bytes 540676
  15.3 0.7 copy-start.2
  17.9 5.1 %collective-permute-start.2 = (bf16[176,128]{1,0:T(8,128)(2,1)}, bf16[176,128]{1,0:T(8,128)(2,1)S(1)}, u32[]{:S(2)}, u32[]{:S(2)}) collective-permute-start(bf16[176,128]{1,0:T(8,128)(2,1)} %get-tuple-element.31), channel_id=1, source_target_pairs={{0,4},{4,8},{8,12},{12,16},{16,20},{20,24},{24,28},{28,32},{32,36}... | collective-permute-start | bytes 135176 | tf_op jit(solution)/shard_map/ppermute | solution.py:629
  21.1 5.0 %collective-permute-start.3 = (bf16[176,128]{1,0:T(8,128)(2,1)}, bf16[176,128]{1,0:T(8,128)(2,1)S(1)}, u32[]{:S(2)}, u32[]{:S(2)}) collective-permute-start(bf16[176,128]{1,0:T(8,128)(2,1)} %get-tuple-element.32), channel_id=1, source_target_pairs={{4,0},{8,4},{12,8},{16,12},{20,16},{24,20},{28,24},{32,28},{36,32}... | collective-permute-start | bytes 135176 | tf_op jit(solution)/shard_map/ppermute | solution.py:629
  23.0 3.1 %copy-start.3 = (bf16[176,128]{1,0:T(8,128)(2,1)}, bf16[176,128]{1,0:T(8,128)(2,1)S(1)}, u32[]{:S(2)}) copy-start(bf16[176,128]{1,0:T(8,128)(2,1)S(1)} %collective-permute-done.2.halo_l) | copy-start | bytes 135172
  26.1 0.6 copy-start.4
  30.9 7.0 %collective-permute-start.4 = (bf16[32,16,128]{2,1,0:T(8,128)(2,1)}, bf16[32,16,128]{2,1,0:T(8,128)(2,1)S(1)}, u32[]{:S(2)}, u32[]{:S(2)}) collective-permute-start(bf16[32,16,128]{2,1,0:T(8,128)(2,1)} %get-tuple-element.35), channel_id=1, source_target_pairs={{0,128},{1,129},{2,130},{3,131},{4,132},{5,133},{6,134},{7,135},{8... | collective-permute-start | bytes 393224 | tf_op jit(solution)/shard_map/ppermute | solution.py:629
  37.9 0.7 copy-start.5
  43.0 42.9 %all-to-all-start = ((bf16[32,9,16,128]{3,2,1,0:T(8,128)(2,1)}), bf16[32,9,16,128]{3,2,1,0:T(8,128)(2,1)S(1)}, u32[]{:S(2)}, u32[]{:S(2)}) async-start(bf16[32,9,16,128]{3,2,1,0:T(8,128)(2,1)} %bitcast.21), calls=%async_computation | async-start | bytes 2359296 | tf_op jit(solution)/shard_map/all_to_all | solution.py:723
  85.9 1.0 %copy-start = (bf16[32,9,16,128]{3,2,1,0:T(8,128)(2,1)}, bf16[32,9,16,128]{3,2,1,0:T(8,128)(2,1)S(1)}, u32[]{:S(2)}) copy-start(bf16[32,9,16,128]{3,2,1,0:T(8,128)(2,1)S(1)} %all-to-all-done) | copy-start | bytes 3538948
  89.7 10.0 %collective-permute-start.5 = (f32[128,128]{1,0:T(8,128)}, f32[128,128]{1,0:T(8,128)S(1)}, u32[]{:S(2)}, u32[]{:S(2)}) collective-permute-start(f32[128,128]{1,0:T(8,128)} %surface_select.1.mine), channel_id=1, source_target_pairs={{128,0},{129,1},{130,2},{131,3},{132,4},{133,5},{134,6},{135,7},{1... | collective-permute-start | bytes 196616 | tf_op jit(solution)/shard_map/ppermute | solution.py:629
  99.7 0.6 copy-start.7
where the time goes:
time: 103 us; the launch traced here: 102 us
  Pallas kernels  45 us (44%)
  starting transfers between devices  27.8 us (27%)
  waiting for transfers between devices  23.1 us (22%)
  local copies, waits for them, and re-layouts  4.41 us (4%)
    pallas_call x1, Pallas kernels, shards(): call(advect_all, [shape(16 * 160, W), shape(72 * 32, W)], 2, 2, 6, [buf,...  16.9 us
    ppermute x6, starting transfers between devices, shifted(): return lax.ppermute(array, axis, pairs)  14.8 us
    all_to_all x1, starting transfers between devices, shards(): lax.all_to_all(send.reshape(band, TILES_PER_PEER, 16, W), 'gx', 0, 0, til...  13 us
    all_to_all x1, waiting for transfers between devices, shards(): lax.all_to_all(send.reshape(band, TILES_PER_PEER, 16, W), 'gx', 0, 0, til...  12.3 us
    ppermute x6, waiting for transfers between devices, shifted(): return lax.ppermute(array, axis, pairs)  10.8 us
    pallas_call x1, Pallas kernels, shards(): call(force, [shape(2560, W)], 1, 2, 1, [buf, pltpu.VMEM((band * TILES_PER...  6.19 us
    pallas_call x1, Pallas kernels, shards(): call(tile_products, [shape(band * TILES_PER_PEER, 16, W, dtype=BF16)], 5,...  4.45 us
    unnamed x19, local copies, waits for them, and re-layouts  4.32 us
  transfers between devices with their start and end apart: 7, of which 4 were waited for; matrix products, arithmetic and copies ran while one was open for 2% of the time, Pallas kernels for 26%

commit v1 on v0

--- a/solution.py
+++ b/solution.py
@@ -13,7 +13,6 @@
 W = 128
 PR = 176
 EXT = 24
-SLOTS = 6
 TILES_PER_PEER = 9
 
 
@@ -33,7 +32,7 @@
 
 
 def params():
-    return pltpu.CompilerParams(vmem_limit_bytes=60 * 1024 * 1024)
+    return pltpu.CompilerParams(vmem_limit_bytes=16 * 1024 * 1024)
 
 
 def call(body, out_shape, n_smem, n_any, n_vmem, scratch):
@@ -53,13 +52,12 @@
     )
 
 
-def pack_rows(comp, state, tracer, mass, codes, rates, up, down, rate8, buf, sem):
+def pack_rows(comp, state, tracer, mass, codes, rates, up, down, rate8):
     @pl.when(comp[0] == 0)
     def _():
-        fetch(state, buf.at[pl.ds(0, 2304)], sem)
         for dst, y in ((up, 0), (down, 31)):
             m = jnp.broadcast_to(mass[y : y + 1, :], (8, W))
-            parts = [buf[pl.ds(g * 256 + y, 8, stride=32), :] * m for g in range(9)] + [m]
+            parts = [state[pl.ds(g * 256 + y, 8, stride=32), :] * m for g in range(9)] + [m]
             for p in range(5):
                 hi, lo = split(jnp.concatenate(parts[2 * p : 2 * p + 2], axis=0))
                 dst[16 * p : 16 * p + 16, :] = hi
@@ -67,7 +65,6 @@
 
     @pl.when(comp[0] == 1)
     def _():
-        fetch(tracer, buf, sem)
         for o in range(8):
             acc = jnp.zeros((16, W), F32)
             for k in range(6):
@@ -79,7 +76,7 @@
                 y = first + j
                 for p in range(10):
                     both = jnp.concatenate(
-                        [buf[pl.ds(g * 128 + y, 8, stride=16), :] for g in (2 * p, 2 * p + 1)],
+                        [tracer[pl.ds(g * 128 + y, 8, stride=16), :] for g in (2 * p, 2 * p + 1)],
                         axis=0,
                     )
                     dst[j * PR + 16 * p : j * PR + 16 * p + 16, :] = both.astype(BF16)
@@ -87,19 +84,18 @@
                 dst[j * PR + 160 : j * PR + 176, :] = jnp.concatenate([r, r], axis=0).astype(BF16)
 
 
-def pack_columns(comp, state, tracer, mass, rate8, left, right, turned, buf, sem):
+def pack_columns(comp, state, tracer, mass, rate8, left, right, turned):
     lane = lanes(8)
 
     @pl.when(comp[0] == 0)
     def _():
-        fetch(state, buf.at[pl.ds(0, 2304)], sem)
         for g in range(10):
             to_left = jnp.zeros((8, W), F32)
             to_right = jnp.zeros((8, W), F32)
             for y in range(32):
                 v = jnp.broadcast_to(mass[y : y + 1, :], (8, W))
                 if g < 9:
-                    v = v * buf[pl.ds(g * 256 + y, 8, stride=32), :]
+                    v = v * state[pl.ds(g * 256 + y, 8, stride=32), :]
                 turned[80 * y + 8 * g : 80 * y + 8 * g + 8, :] = v
                 v = pltpu.roll(v, y, 1)
                 to_left = jnp.where(lane == y, v, to_left)
@@ -109,14 +105,13 @@
 
     @pl.when(comp[0] == 1)
     def _():
-        fetch(tracer, buf, sem)
         for g in range(21):
             to_left = jnp.zeros((8, W), F32)
             to_right = jnp.zeros((8, W), F32)
             for y in range(16):
                 i = y + ADV
                 if g < 20:
-                    v = buf[pl.ds(g * 128 + y, 8, stride=16), :]
+                    v = tracer[pl.ds(g * 128 + y, 8, stride=16), :]
                     turned[160 * y + 8 * g : 160 * y + 8 * g + 8, :] = v
                 else:
                     v = rate8[pl.ds(y, 8, stride=16), :]
@@ -409,7 +404,7 @@
 
 
 def tile_products(
-    comp, me, src, dest, dst, own, arrived, weights, top, send, count, meta, parts
+    comp, src, dest, dst, own, arrived, weights, top, send, count, meta, parts
 ):
     band = send.shape[0] // TILES_PER_PEER
     tiles = weights.shape[0]
@@ -447,17 +442,14 @@
 
     @pl.when(comp[0] == 1)
     def _():
-        ids = jnp.where(sub8 == 0, me[0], lane8 % 16).astype(F32)
-        ids = jnp.where((sub8 == 2) | (lane8 % tiles >= 16), -1.0, ids)
-
         def clear(h, carry):
             for j in range(TILES_PER_PEER):
-                if j in (0, 4):
-                    send[h * TILES_PER_PEER + j] = top[j // 4]
+                if j < 2:
+                    send[h * TILES_PER_PEER + j] = top[j]
                 else:
                     send[h * TILES_PER_PEER + j] = jnp.zeros((16, W), BF16)
             count[h] = 0
-            meta[h] = ids
+            meta[h] = jnp.full((8, W), -1.0, F32)
             return carry
 
         lax.fori_loop(0, band, clear, 0)
@@ -465,7 +457,7 @@
             owner = dest[0, t]
             slot = count[owner]
             count[owner] = slot + 1
-            place = slot + 1 + jnp.where(slot >= SLOTS // 2, 1, 0)
+            place = slot + 2
             send[owner * TILES_PER_PEER + place] = product(arrived, t).astype(BF16)
             named = jnp.where(
                 (lane8 // 16 == place) & (sub8 == 2), dst[0, t].astype(F32), meta[owner]
@@ -509,9 +501,7 @@
         advect(((ta, tb), (tc, td)), coef_a, coef_b, speed, 20, 4, result)
 
 
-def surface_select(back_owner, back_src, received, out):
-    band = received.shape[0] // TILES_PER_PEER
-    lane = lanes(1)
+def wanted(back_owner, back_src):
     sub8 = lax.broadcasted_iota(jnp.int32, (8, W), 0)
     wants = []
     for p in range(8):
@@ -519,58 +509,70 @@
         for k in range(8):
             v = jnp.where(sub8 == k, back_owner[0, 8 * p + k] * 16 + back_src[0, 8 * p + k], v)
         wants.append(v)
-    want = jnp.concatenate(wants, axis=0).astype(F32)
-
-    def pair(q, carry):
-        h = 2 * q
-        ids = [
-            received[(h + d) * TILES_PER_PEER + 8].astype(F32) for d in range(2)
-        ]
-        named = [v[0:1, :] * 16.0 + v[1:2, :] for v in ids]
-        row = jnp.where(lane < 64, named[0], named[1])
-        hot = jnp.where(jnp.broadcast_to(row, (64, W)) == want, 1.0, 0.0).astype(BF16)
-        totals = []
+    return jnp.concatenate(wants, axis=0).astype(F32)
+
+
+def surface_select(comp, back_owner, back_src, weights, received, out):
+    band = received.shape[0] // TILES_PER_PEER
+
+    @pl.when(comp[0] == 0)
+    def _():
+        lane = lanes(1)
+        want = wanted(back_owner, back_src)
+
+        def pair(q, carry):
+            h = 2 * q
+            ids = [received[(h + d) * TILES_PER_PEER + 8].astype(F32) for d in range(2)]
+            named = [v[0:1, :] * 16.0 + v[1:2, :] for v in ids]
+            row = jnp.where(lane < 64, named[0], named[1])
+            hot = jnp.where(jnp.broadcast_to(row, (64, W)) == want, 1.0, 0.0).astype(BF16)
+            totals = []
+            for v in range(2):
+                rhs = jnp.concatenate(
+                    [
+                        received[(h + d) * TILES_PER_PEER + 4 * v + j]
+                        for d in range(2)
+                        for j in range(4)
+                    ],
+                    axis=0,
+                )
+                totals.append(carry[v] + jnp.dot(hot, rhs, preferred_element_type=F32))
+            return tuple(totals)
+
+        zero = jnp.zeros((64, W), F32)
+        sums = lax.fori_loop(0, band // 2, pair, (zero, zero), unroll=4)
         for v in range(2):
-            rhs = jnp.concatenate(
-                [
-                    received[(h + d) * TILES_PER_PEER + 4 * v + j]
-                    for d in range(2)
-                    for j in range(4)
-                ],
-                axis=0,
-            )
-            totals.append(carry[v] + jnp.dot(hot, rhs, preferred_element_type=F32))
-        return tuple(totals)
-
-    zero = jnp.zeros((64, W), F32)
-    sums = lax.fori_loop(0, band // 2, pair, (zero, zero), unroll=4)
-    for v in range(2):
-        out[64 * v : 64 * v + 64, :] = sums[v]
-
-
-def surface_product(comp, back_dst, weights, mine, other, out, store, sem, table, parts, acc):
+            out[64 * v : 64 * v + 64, :] = sums[v]
+
+
+def finish(
+    comp, back_owner, back_src, back_dst,
+    advected, received, profile, weights, mine, other,
+    ocean, surface, table, parts, acc,
+):
+    band = received.shape[0] // TILES_PER_PEER
     tiles = weights.shape[0]
 
-    @pl.when(comp[0] == 1)
-    def _():
-        out[...] = jnp.zeros(out.shape, F32)
-
     @pl.when(comp[0] == 0)
     def _():
-        copy = pltpu.make_async_copy(weights, store, sem)
-        copy.start()
+        want = wanted(back_owner, back_src)
+        sums = [mine[64 * v : 64 * v + 64, :] for v in range(2)]
+        for c in range(band // 8):
+            row = (lanes(64) + c * W).astype(F32)
+            hot = jnp.where(row == want, 1.0, 0.0).astype(BF16)
+            for v in range(2):
+                rhs = jnp.concatenate([other[(8 * c + h) * 2 + v] for h in range(8)], axis=0)
+                sums[v] = sums[v] + jnp.dot(hot, rhs, preferred_element_type=F32)
         for v in range(2):
-            rows = slice(64 * v, 64 * v + 64)
-            hi, lo = split(mine[rows, :] + other[rows, :])
+            hi, lo = split(sums[v])
             for at, part in ((v, hi.astype(F32)), (2 + v, lo.astype(F32))):
                 for p in range(8):
                     table[pl.ds(64 * p + at, 8, stride=8), :] = part[8 * p : 8 * p + 8]
         acc[...] = jnp.zeros(acc.shape, F32)
-        copy.wait()
         for t in range(tiles):
             parts[8 * t : 8 * t + 8, :] = lax.dot_general(
                 table[8 * t : 8 * t + 8, :].astype(BF16),
-                store[t],
+                weights[t],
                 (((1,), (1,)), ((), ())),
                 preferred_element_type=F32,
             )
@@ -579,24 +581,15 @@
             acc[at, :] = acc[at, :] + parts[8 * t : 8 * t + 8, :]
         for v in range(2):
             for p in range(4):
-                out[32 * v + 8 * p : 32 * v + 8 * p + 8, :] = (
+                surface[32 * v + 8 * p : 32 * v + 8 * p + 8, :] = (
                     acc[pl.ds(64 * p + v, 8, stride=8), :]
                     + acc[pl.ds(64 * p + 2 + v, 8, stride=8), :]
                 )
-
-
-def force(comp, advected_ref, received_ref, profile, out, advected, received, sem, sem2):
-    band = received.shape[0] // TILES_PER_PEER
-
-    @pl.when(comp[0] == 0)
-    def _():
-        out[...] = jnp.zeros(out.shape, F32)
+        ocean[...] = jnp.zeros(ocean.shape, F32)
 
     @pl.when(comp[0] == 1)
     def _():
-        late = pltpu.make_async_copy(advected_ref, advected, sem2)
-        late.start()
-        fetch(received_ref, received, sem)
+        surface[...] = jnp.zeros(surface.shape, F32)
         row = lax.broadcasted_iota(jnp.int32, (256, W), 0)
         point = jnp.where(row % 16 == lanes(256) % 16, row // 16, -2).astype(F32)
 
@@ -610,7 +603,6 @@
 
         total = lax.fori_loop(0, band, add, jnp.zeros((256, W), F32), unroll=4)
         level_hi, level_lo = split(profile[...])
-        late.wait()
         for y in range(16):
             hi, lo = split(total[16 * y : 16 * y + 16, :])
             more = (
@@ -620,7 +612,7 @@
             )
             new = advected[160 * y : 160 * y + 160, :] + more
             for g in range(20):
-                out[pl.ds(g * 128 + y, 8, stride=16), :] = new[8 * g : 8 * g + 8]
+                ocean[pl.ds(g * 128 + y, 8, stride=16), :] = new[8 * g : 8 * g + 8]
 
 
 def shifted(array, axis, by):
@@ -663,13 +655,13 @@
     up, down, rate8 = call(
         pack_rows,
         [shape(4 * PR, W, dtype=BF16), shape(4 * PR, W, dtype=BF16), shape(128, W)],
-        1, 2, 3,
-        [buf, dma],
+        1, 0, 5,
+        [],
     )(comp, state, tracer, atm_mass, codes, rates)
     below = shifted(up, "gy", -1)
     above = shifted(down, "gy", 1)
     raw_left, raw_right, turned = call(
-        pack_columns, [shape(PR, W), shape(PR, W), shape(2560, W)], 1, 2, 2, [buf, dma]
+        pack_columns, [shape(PR, W), shape(PR, W), shape(2560, W)], 1, 0, 4, []
     )(comp, state, tracer, atm_mass, rate8)
     left, right = call(
         finish_columns,
@@ -684,7 +676,6 @@
     lhs = jnp.pad(jnp.concatenate([coupler, top_profile], axis=0), ((0, 14), (0, 8)))
     lhs_hi, lhs_lo = split(lhs)
     lhs = jnp.concatenate([lhs_hi, lhs_lo], axis=0)
-    me = lax.axis_index("gx").astype(jnp.int32).reshape(1)
     small = pltpu.VMEM((EXT * 8, W), F32)
 
     fields, own, flux, top, coef_a, coef_b = call(
@@ -704,19 +695,21 @@
             pltpu.VMEM((80, W), F32), pltpu.VMEM((80, W), F32),
             small, small, small, small,
         ],
-    )(comp, lev_speed, turned, rate8, above, below, halo_l, halo_r, lhs)
+    )(
+        comp, lev_speed, turned, rate8, above, below, halo_l, halo_r, lhs,
+    )
     arrived = shifted(flux, "comp", 1)
     send, = call(
         tile_products,
         [shape(band * TILES_PER_PEER, 16, W, dtype=BF16)],
-        5, 0, 4,
+        4, 0, 4,
         [
             pltpu.SMEM((band,), jnp.int32),
             pltpu.VMEM((band, 8, W), F32),
             pltpu.VMEM((512, W), F32),
         ],
     )(
-        comp, me, flux_src_blk, flux_dest.reshape(1, 64), flux_dst_blk,
+        comp, flux_src_blk, flux_dest.reshape(1, 64), flux_dst_blk,
         own, arrived, conservative_flux_weights[0], top,
     )
     send, coef_a, coef_b = lax.optimization_barrier((send, coef_a, coef_b))
@@ -729,21 +722,22 @@
         [shape(16 * 160, W), shape(72 * 32, W)],
         2, 2, 6,
         [buf, dma, grid, grid, grid, grid, pltpu.VMEM((160, W), F32)],
-    )(comp, lev_speed, turned, fields, above, below, halo_l, halo_r, coef_a, coef_b)
+    )(
+        comp, lev_speed, turned, fields, above, below, halo_l, halo_r, coef_a, coef_b,
+    )
     levels = profile.reshape(160, 16)
     received, advected, levels = lax.optimization_barrier((received, advected, levels))
-    mine, = call(surface_select, [shape(128, W)], 2, 0, 1, [])(
-        back_owner, back_src_blk, received
-    )
-    other = shifted(mine, "comp", -1)
-    ocean, = call(force, [shape(2560, W)], 1, 2, 1, [
-        buf, pltpu.VMEM((band * TILES_PER_PEER, 16, W), BF16), dma, dma,
-    ])(comp, advected, received, levels)
-    tile_store = pltpu.VMEM(return_remap_weights.shape[1:], BF16)
-    surface, = call(surface_product, [shape(64, W)], 2, 1, 2, [
-        tile_store, dma,
+    tops = received.reshape(band, TILES_PER_PEER, 16, W)[:, :2].reshape(2 * band, 16, W)
+    other = shifted(tops, "comp", -1)
+    mine, = call(surface_select, [shape(128, W)], 3, 1, 1, [])(
+        comp, back_owner, back_src_blk, return_remap_weights[0], received
+    )
+    ocean, surface = call(finish, [shape(2560, W), shape(64, W)], 4, 0, 6, [
         pltpu.VMEM((512, W), F32), pltpu.VMEM((512, W), F32), pltpu.VMEM((256, W), F32),
-    ])(comp, back_dst_blk, return_remap_weights[0], mine, other)
+    ])(
+        comp, back_owner, back_src_blk, back_dst_blk,
+        advected, received, levels, return_remap_weights[0], mine, other,
+    )
     return (
         dss.reshape(1, 72, 32, W),
         surface.reshape(1, 2, 32, W),

time: 103 us -> 92 us (0.89)
  Pallas kernels: 45 us -> 24.8 us
  local copies, waits for them, and re-layouts: 4.41 us -> 15.8 us
  waiting for transfers between devices: 23.1 us -> 21.6 us
    unnamed x19 -> x65, local copies, waits for them, and re-layouts: 4.32 us -> 15.6 us
    pallas_call x5 -> x4, Pallas kernels: 18.8 us -> 8.41 us  [the longest x1 4.15 us: shards(): call(finish, [shape(2560, W), shape(64, W)], 4, 0, 6, [pltpu.VMEM((512, W...]
    all_to_all x1, waiting for transfers between devices: 12.3 us -> 7.21 us  [shards(): lax.all_to_all(send.reshape(band, TILES_PER_PEER, 16, W), 'gx', 0, 0, til...]
    ppermute x6, waiting for transfers between devices: 10.8 us -> 14.4 us  [shifted(): return lax.ppermute(array, axis, pairs)]
    pallas_call x1, Pallas kernels: 3.19 us -> 0.28 us  [shards(): call(pack_rows, [shape(4 * PR, W, dtype=BF16), shape(4 * PR, W, dtype=BF1...]
    pallas_call x1, Pallas kernels: 4.25 us -> 1.44 us  [shards(): call(assemble, [shape(72 * 32, W), shape(32, 32, W, dtype=BF16), shape(32...]
    pallas_call x1, Pallas kernels: 16.9 us -> 14.5 us  [shards(): call(advect_all, [shape(16 * 160, W), shape(72 * 32, W)], 2, 2, 6, [buf,...]
    pallas_call x1, Pallas kernels: 1.88 us -> 0.16 us  [shards(): call(finish_columns, [shape(PR, W, dtype=BF16), shape(PR, W, dtype=BF16)]...]
  transfers between devices with their start and end apart: 7 -> 7, of which waited for: 4 -> 6; matrix products, arithmetic and copies ran while one was open for 2% -> 0% of each run, Pallas kernels for 26% -> 17%
where the time goes in v1:
time: 92 us; the launch traced here: 91.2 us
  starting transfers between devices  27.9 us (30%)
  Pallas kernels  24.8 us (27%)
  waiting for transfers between devices  21.6 us (23%)
  local copies, waits for them, and re-layouts  15.8 us (17%)
  between operations  0.96 us (1%)
    unnamed x65, local copies, waits for them, and re-layouts  15.6 us
    ppermute x6, starting transfers between devices, shifted(): return lax.ppermute(array, axis, pairs)  14.9 us
    pallas_call x1, Pallas kernels, shards(): call(advect_all, [shape(16 * 160, W), shape(72 * 32, W)], 2, 2, 6, [buf,...  14.5 us
    ppermute x6, waiting for transfers between devices, shifted(): return lax.ppermute(array, axis, pairs)  14.4 us
    all_to_all x1, starting transfers between devices, shards(): lax.all_to_all(send.reshape(band, TILES_PER_PEER, 16, W), 'gx', 0, 0, til...  13 us
    all_to_all x1, waiting for transfers between devices, shards(): lax.all_to_all(send.reshape(band, TILES_PER_PEER, 16, W), 'gx', 0, 0, til...  7.21 us
    pallas_call x1, Pallas kernels, shards(): call(finish, [shape(2560, W), shape(64, W)], 4, 0, 6, [pltpu.VMEM((512, W...  4.15 us
    pallas_call x1, Pallas kernels, shards(): call(tile_products, [shape(band * TILES_PER_PEER, 16, W, dtype=BF16)], 4,...  3.19 us
  transfers between devices with their start and end apart: 7, of which 6 were waited for; matrix products, arithmetic and copies ran while one was open for 0% of the time, Pallas kernels for 17%

profile of v1, /device:TPU:1, one launch (start us, length us, event | category | flops | bytes accessed | tf_op | source)
XLA Modules:
  0.0 91.2 jit_solution(18215873722728349033)
XLA Ops:
  0.6 0.0 copy-start.3
  0.6 1.3 %copy-done.3 = f32[1,2,80,16,128]{4,3,2,1,0:T(8,128)S(1)} copy-done((f32[1,2,80,16,128]{4,3,2,1,0:T(8,128)S(1)}, f32[1,2,80,16,128]{4,3,2,1,0:T(8,128)}, u32[]{:S(2)}) %copy-start.3) | copy-done | bytes 1310744
  2.0 1.3 %copy-done.4 = f32[1,72,32,128]{3,2,1,0:T(8,128)S(1)} copy-done((f32[1,72,32,128]{3,2,1,0:T(8,128)S(1)}, f32[1,72,32,128]{3,2,1,0:T(8,128)}, u32[]{:S(2)}) %copy-start.4) | copy-done | bytes 1179672
  3.2 0.7 copy-done.20
  3.9 0.8 copy-done.21
  4.7 0.8 copy-done.22
  5.5 0.3 pack_rows.1
  5.8 0.0 copy-start.31
  5.8 0.0 copy-start.30
  5.8 4.0 %collective-permute-start = (bf16[704,128]{1,0:T(8,128)(2,1)S(1)}, bf16[704,128]{1,0:T(8,128)(2,1)S(1)}, u32[]{:S(2)}, u32[]{:S(2)}) collective-permute-start(bf16[704,128]{1,0:T(8,128)(2,1)S(1)} %get-tuple-element.29), channel_id=1, source_target_pairs={{0,1},{1,2},{2,3},{4,5},{5,6},{6,7},{8,9},{9,10},{10,11},{12,13},{... | collective-permute-start | bytes 540680 | tf_op jit(solution)/shard_map/ppermute | solution.py:621
  9.8 1.3 %collective-permute-start.1 = (bf16[704,128]{1,0:T(8,128)(2,1)S(1)}, bf16[704,128]{1,0:T(8,128)(2,1)S(1)}, u32[]{:S(2)}, u32[]{:S(2)}) collective-permute-start(bf16[704,128]{1,0:T(8,128)(2,1)S(1)} %get-tuple-element.30), channel_id=1, source_target_pairs={{1,0},{2,1},{3,2},{5,4},{6,5},{7,6},{9,8},{10,9},{11,10},{13,12},{... | collective-permute-start | bytes 540680 | tf_op jit(solution)/shard_map/ppermute | solution.py:621
  11.1 0.0 copy-start.23
  11.1 0.5 pack_columns.1
  11.6 0.0 copy-done.31
  11.7 0.0 copy-start.1
  11.7 0.0 copy-start.5
  11.7 0.0 copy-start.26
  11.7 0.0 copy-start.27
  11.7 0.0 copy-start.28
  11.7 0.1 slice_reduce_fusion
  11.8 0.0 copy-done.30
  11.8 0.1 fusion.1
  12.0 1.3 %collective-permute-done.above = bf16[704,128]{1,0:T(8,128)(2,1)S(1)} collective-permute-done((bf16[704,128]{1,0:T(8,128)(2,1)S(1)}, bf16[704,128]{1,0:T(8,128)(2,1)S(1)}, u32[]{:S(2)}, u32[]{:S(2)}) %collective-permute-start) | collective-permute-done | bytes 180256 | tf_op jit(solution)/shard_map/ppermute | solution.py:621
  13.2 3.8 %collective-permute-done.1.below = bf16[704,128]{1,0:T(8,128)(2,1)S(1)} collective-permute-done((bf16[704,128]{1,0:T(8,128)(2,1)S(1)}, bf16[704,128]{1,0:T(8,128)(2,1)S(1)}, u32[]{:S(2)}, u32[]{:S(2)}) %collective-permute-start.1) | collective-permute-done | bytes 180256 | tf_op jit(solution)/shard_map/ppermute | solution.py:621
  17.0 0.2 finish_columns.1
  17.2 3.2 %collective-permute-start.2 = (bf16[176,128]{1,0:T(8,128)(2,1)S(1)}, bf16[176,128]{1,0:T(8,128)(2,1)S(1)}, u32[]{:S(2)}, u32[]{:S(2)}) collective-permute-start(bf16[176,128]{1,0:T(8,128)(2,1)S(1)} %get-tuple-element.33), channel_id=1, source_target_pairs={{0,4},{4,8},{8,12},{12,16},{16,20},{20,24},{24,28},{28,32},{32,36}... | collective-permute-start | bytes 135176 | tf_op jit(solution)/shard_map/ppermute | solution.py:621
  20.4 1.3 %collective-permute-start.3 = (bf16[176,128]{1,0:T(8,128)(2,1)S(1)}, bf16[176,128]{1,0:T(8,128)(2,1)S(1)}, u32[]{:S(2)}, u32[]{:S(2)}) collective-permute-start(bf16[176,128]{1,0:T(8,128)(2,1)S(1)} %get-tuple-element.34), channel_id=1, source_target_pairs={{4,0},{8,4},{12,8},{16,12},{20,16},{24,20},{28,24},{32,28},{36,32}... | collective-permute-start | bytes 135176 | tf_op jit(solution)/shard_map/ppermute | solution.py:621
  21.7 0.0 collective-permute-done.2.halo_l
  21.7 0.0 copy-start.16
  21.7 3.5 %collective-permute-done.3.halo_r = bf16[176,128]{1,0:T(8,128)(2,1)S(1)} collective-permute-done((bf16[176,128]{1,0:T(8,128)(2,1)S(1)}, bf16[176,128]{1,0:T(8,128)(2,1)S(1)}, u32[]{:S(2)}, u32[]{:S(2)}) %collective-permute-start.3) | collective-permute-done | bytes 45088 | tf_op jit(solution)/shard_map/ppermute | solution.py:621
  25.2 0.0 copy-done.23
  25.2 1.4 %assemble.1 = (f32[2304,128]{1,0:T(8,128)S(1)}, bf16[32,32,128]{2,1,0:T(8,128)(2,1)S(1)}, bf16[32,16,128]{2,1,0:T(8,128)(2,1)S(1)}, bf16[2,16,128]{2,1,0:T(8,128...) custom-call(s32[1]{0:T(128)} %bitcast.comp, f32[80]{0:T(128)S(1)} %copy-done.23, ...), custom_call_target="tpu_custom_call" | custom-call | tf_op jit(solution)/shard_map/assemble/pallas_call | solution.py:681
  26.6 0.0 copy-done.16
  26.7 0.0 copy-start.10
  26.7 1.0 %copy-done.10 = f32[2304,128]{1,0:T(8,128)} copy-done((f32[2304,128]{1,0:T(8,128)}, f32[2304,128]{1,0:T(8,128)S(1)}, u32[]{:S(2)}) %copy-start.10) | copy-done | bytes 1179672
  27.7 0.7 copy-done.12
  28.4 0.7 copy-done.14
  29.0 1.3 %collective-permute-start.4 = (bf16[32,16,128]{2,1,0:T(8,128)(2,1)S(1)}, bf16[32,16,128]{2,1,0:T(8,128)(2,1)S(1)}, u32[]{:S(2)}, u32[]{:S(2)}) collective-permute-start(bf16[32,16,128]{2,1,0:T(8,128)(2,1)S(1)} %get-tuple-element.37), channel_id=1, source_target_pairs={{0,128},{1,129},{2,130},{3,131},{4,132},{5,133},{6,134},{7,135},{8... | collective-permute-start | bytes 393224 | tf_op jit(solution)/shard_map/ppermute | solution.py:621
  30.3 5.4 %collective-permute-done.4.arrived = bf16[32,16,128]{2,1,0:T(8,128)(2,1)S(1)} collective-permute-done((bf16[32,16,128]{2,1,0:T(8,128)(2,1)S(1)}, bf16[32,16,128]{2,1,0:T(8,128)(2,1)S(1)}, u32[]{:S(2)}, u32[]{:S(2)}) %collective-permute-start.4) | collective-permute-done | bytes 131104 | tf_op jit(solution)/shard_map/ppermute | solution.py:621
  35.7 0.0 copy-done.5
  35.7 0.0 copy-done.26
  35.7 0.0 copy-done.27
  35.7 3.2 %tile_products.1 = bf16[288,16,128]{2,1,0:T(8,128)(2,1)} custom-call(s32[1]{0:T(128)} %bitcast.comp, s32[1,64]{1,0:T(1,128)S(1)} %copy-done.26, s32[1,64]{1,0:T(1,128)S(1)} %bitcast.30, s32[1,64]{1,0:T(1,128)S(1)} %copy-done.28, bf16[32,32,128]{2,1,0:T(8,128)(2,1)S(1)} %get-tuple-element.36.own, bf16[32,16,128]{2,1,0:T(8,128)(2,1)S(1)} %collective-permute-done.4.arrived, ...), custom_call_target="tpu_custom_call" | custom-call | tf_op jit(solution)/shard_map/tile_products/pallas_call | solution.py:702
  38.9 0.0 copy-done.6
  38.9 13.0 %all-to-all-start = ((bf16[32,9,16,128]{3,2,1,0:T(8,128)(2,1)}), bf16[32,9,16,128]{3,2,1,0:T(8,128)(2,1)S(1)}, u32[]{:S(2)}, u32[]{:S(2)}) async-start(bf16[32,9,16,128]{3,2,1,0:T(8,128)(2,1)} %bitcast.8), calls=%async_computation | async-start | bytes 2359296 | tf_op jit(solution)/shard_map/all_to_all | solution.py:716
  51.9 0.1 copy.20
  52.0 1.3 %copy-done.2 = f32[2560,128]{1,0:T(8,128)S(1)} copy-done((f32[2560,128]{1,0:T(8,128)S(1)}, f32[2560,128]{1,0:T(8,128)}, u32[]{:S(2)}) %copy-start.2) | copy-done | bytes 1310744
  53.3 0.9 %copy-done.7 = bf16[704,128]{1,0:T(8,128)(2,1)S(1)} copy-done((bf16[704,128]{1,0:T(8,128)(2,1)S(1)}, bf16[704,128]{1,0:T(8,128)(2,1)}, u32[]{:S(2)}) %copy-start.7) | copy-done | bytes 180248
  54.3 1.3 %copy-done.11 = f32[2304,128]{1,0:T(8,128)S(1)} copy-done((f32[2304,128]{1,0:T(8,128)S(1)}, f32[2304,128]{1,0:T(8,128)}, u32[]{:S(2)}) %copy-start.11) | copy-done | bytes 1179672
  55.5 0.9 %copy-done.13 = f32[384,128]{1,0:T(8,128)S(1)} copy-done((f32[384,128]{1,0:T(8,128)S(1)}, f32[384,128]{1,0:T(8,128)}, u32[]{:S(2)}) %copy-start.13) | copy-done | bytes 196632
  56.5 0.9 %copy-done.15 = f32[384,128]{1,0:T(8,128)S(1)} copy-done((f32[384,128]{1,0:T(8,128)S(1)}, f32[384,128]{1,0:T(8,128)}, u32[]{:S(2)}) %copy-start.15) | copy-done | bytes 196632
  57.4 0.8 copy-done.17
  58.2 0.8 copy-done.19
  59.0 14.5 %advect_all.1 = (f32[2560,128]{1,0:T(8,128)S(1)}, f32[2304,128]{1,0:T(8,128)}) custom-call(s32[1]{0:T(128)} %bitcast.comp, f32[80]{0:T(128)S(1)} %copy-done.23, f32[2560,128]{1,0:T(8,128)S(1)} %copy-done.2, f32[2304,128]{1,0:T(8,128)S(1)} %copy-done.11, bf16[704,128]{1,0:T(8,128)(2,1)S(1)} %collective-permute-done.above, bf16[704,128]{1,0:T(8,128)(2,1)S(1)} %copy-done.7, ...), custom_call_target="tpu_custom_call" | custom-call | tf_op jit(solution)/shard_map/advect_all/pallas_call | solution.py:720
  73.5 0.0 copy-start.8
  73.5 1.0 %copy-done.8 = f32[2560,128]{1,0:T(8,128)} copy-done((f32[2560,128]{1,0:T(8,128)}, f32[2560,128]{1,0:T(8,128)S(1)}, u32[]{:S(2)}) %copy-start.8) | copy-done | bytes 1310744
  74.6 7.2 %all-to-all-done = bf16[32,9,16,128]{3,2,1,0:T(8,128)(2,1)S(1)} async-done(((bf16[32,9,16,128]{3,2,1,0:T(8,128)(2,1)}), bf16[32,9,16,128]{3,2,1,0:T(8,128)(2,1)S(1)}, u32[]{:S(2)}, u32[]{:S(2)}) %all-to-all-start) | async-done | bytes 1179680 | tf_op jit(solution)/shard_map/all_to_all | solution.py:716
  81.8 3.8 %collective-permute-start.5 = (bf16[64,16,128]{2,1,0:T(8,128)(2,1)S(1)}, bf16[64,16,128]{2,1,0:T(8,128)(2,1)S(1)}, u32[]{:S(2)}, u32[]{:S(2)}) collective-permute-start(bf16[64,16,128]{2,1,0:T(8,128)(2,1)S(1)} %bitcast.31), channel_id=1, source_target_pairs={{128,0},{129,1},{130,2},{131,3},{132,4},{133,5},{134,6},{135,7},{1... | collective-permute-start | bytes 786440 | tf_op jit(solution)/shard_map/ppermute | solution.py:621
  85.7 0.0 copy-start.9
  85.7 0.0 copy-start.29
  85.7 0.6 surface_select.1.mine
  86.3 0.5 collective-permute-done.5.other
  86.8 0.2 copy-done.9
  87.0 4.2 %finish.1 = (f32[2560,128]{1,0:T(8,128)}, f32[64,128]{1,0:T(8,128)}) custom-call(s32[1]{0:T(128)} %bitcast.comp, s32[1,64]{1,0:T(1,128)S(1)} %copy-done.24, s32[1,64]{1,0:T(1,128)S(1)} %copy-done.25, s32[1,64]{1,0:T(1,128)S(1)} %copy-done.29, f32[2560,128]{1,0:T(8,128)S(1)} %copy-done.9, bf16[288,16,128]{2,1,0:T(8,128)(2,1)S(1)} %bitcast.19, ...), custom_call_target="tpu_custom_call" | custom-call | tf_op jit(solution)/shard_map/finish/pallas_call | solution.py:735
  (29 shorter events, 0.1 us)
Async XLA Ops:
  0.6 1.3 %copy-start.3 = (f32[1,2,80,16,128]{4,3,2,1,0:T(8,128)S(1)}, f32[1,2,80,16,128]{4,3,2,1,0:T(8,128)}, u32[]{:S(2)}) copy-start(f32[1,2,80,16,128]{4,3,2,1,0:T(8,128)} %param.23) | copy-start | bytes 3932164
  2.0 1.3 %copy-start.4 = (f32[1,72,32,128]{3,2,1,0:T(8,128)S(1)}, f32[1,72,32,128]{3,2,1,0:T(8,128)}, u32[]{:S(2)}) copy-start(f32[1,72,32,128]{3,2,1,0:T(8,128)} %param.16) | copy-start | bytes 3538948
  3.2 0.7 copy-start.20
  3.9 0.8 copy-start.21
  4.7 0.8 copy-start.22
  5.8 5.8 %copy-start.31 = (f32[2,80,16]{1,2,0:T(8,128)S(1)}, f32[2,80,16]{1,2,0:T(8,128)}, u32[]{:S(2)}) copy-start(f32[2,80,16]{1,2,0:T(8,128)} %param.27) | copy-start | bytes 30724
  5.8 6.0 %copy-start.30 = (f32[16,72]{1,0:T(8,128)S(1)}, f32[16,72]{1,0:T(8,128)}, u32[]{:S(2)}) copy-start(f32[16,72]{1,0:T(8,128)} %param.18) | copy-start | bytes 13828
  5.8 7.4 %collective-permute-start = (bf16[704,128]{1,0:T(8,128)(2,1)S(1)}, bf16[704,128]{1,0:T(8,128)(2,1)S(1)}, u32[]{:S(2)}, u32[]{:S(2)}) collective-permute-start(bf16[704,128]{1,0:T(8,128)(2,1)S(1)} %get-tuple-element.29), channel_id=1, source_target_pairs={{0,1},{1,2},{2,3},{4,5},{5,6},{6,7},{8,9},{9,10},{10,11},{12,13},{... | collective-permute-start | bytes 540680 | tf_op jit(solution)/shard_map/ppermute | solution.py:621
  9.8 7.2 %collective-permute-start.1 = (bf16[704,128]{1,0:T(8,128)(2,1)S(1)}, bf16[704,128]{1,0:T(8,128)(2,1)S(1)}, u32[]{:S(2)}, u32[]{:S(2)}) collective-permute-start(bf16[704,128]{1,0:T(8,128)(2,1)S(1)} %get-tuple-element.30), channel_id=1, source_target_pairs={{1,0},{2,1},{3,2},{5,4},{6,5},{7,6},{9,8},{10,9},{11,10},{13,12},{... | collective-permute-start | bytes 540680 | tf_op jit(solution)/shard_map/ppermute | solution.py:621
  11.1 14.1 %copy-start.23 = (f32[80]{0:T(128)S(1)}, f32[80]{0:T(128)}, u32[]{:S(2)}) copy-start(f32[80]{0:T(128)} %lev_speed.3) | copy-start | bytes 964
  11.7 27.3 %copy-start.1 = (f32[2560,128]{1,0:T(8,128)}, f32[2560,128]{1,0:T(8,128)S(1)}, u32[]{:S(2)}) copy-start(f32[2560,128]{1,0:T(8,128)S(1)} %get-tuple-element.28.turned) | copy-start | bytes 3932164
  11.7 24.0 %copy-start.5 = (bf16[1,64,128,128]{3,2,1,0:T(8,128)(2,1)S(1)}, bf16[1,64,128,128]{3,2,1,0:T(8,128)(2,1)}, u32[]{:S(2)}) copy-start(bf16[1,64,128,128]{3,2,1,0:T(8,128)(2,1)} %param.22) | copy-start | bytes 6291460
  11.7 24.0 %copy-start.26 = (s32[1,64]{1,0:T(1,128)S(1)}, s32[1,64]{1,0:T(1,128)}, u32[]{:S(2)}) copy-start(s32[1,64]{1,0:T(1,128)} %src.1) | copy-start | bytes 772
  11.7 24.0 %copy-start.27 = (s32[1,64,1]{1,2,0:T(1,128)S(1)}, s32[1,64,1]{1,2,0:T(1,128)}, u32[]{:S(2)}) copy-start(s32[1,64,1]{1,2,0:T(1,128)} %param.19) | copy-start | bytes 772
  11.7 24.0 %copy-start.28 = (s32[1,64]{1,0:T(1,128)S(1)}, s32[1,64]{1,0:T(1,128)}, u32[]{:S(2)}) copy-start(s32[1,64]{1,0:T(1,128)} %dst.1) | copy-start | bytes 772
  17.0 21.9 %copy-start.6 = (bf16[704,128]{1,0:T(8,128)(2,1)}, bf16[704,128]{1,0:T(8,128)(2,1)S(1)}, u32[]{:S(2)}) copy-start(bf16[704,128]{1,0:T(8,128)(2,1)S(1)} %collective-permute-done.1.below) | copy-start | bytes 540676
  17.2 4.5 %collective-permute-start.2 = (bf16[176,128]{1,0:T(8,128)(2,1)S(1)}, bf16[176,128]{1,0:T(8,128)(2,1)S(1)}, u32[]{:S(2)}, u32[]{:S(2)}) collective-permute-start(bf16[176,128]{1,0:T(8,128)(2,1)S(1)} %get-tuple-element.33), channel_id=1, source_target_pairs={{0,4},{4,8},{8,12},{12,16},{16,20},{20,24},{24,28},{28,32},{32,36}... | collective-permute-start | bytes 135176 | tf_op jit(solution)/shard_map/ppermute | solution.py:621
  20.4 4.8 %collective-permute-start.3 = (bf16[176,128]{1,0:T(8,128)(2,1)S(1)}, bf16[176,128]{1,0:T(8,128)(2,1)S(1)}, u32[]{:S(2)}, u32[]{:S(2)}) collective-permute-start(bf16[176,128]{1,0:T(8,128)(2,1)S(1)} %get-tuple-element.34), channel_id=1, source_target_pairs={{4,0},{8,4},{12,8},{16,12},{20,16},{24,20},{28,24},{32,28},{36,32}... | collective-permute-start | bytes 135176 | tf_op jit(solution)/shard_map/ppermute | solution.py:621
  21.7 4.9 %copy-start.16 = (bf16[176,128]{1,0:T(8,128)(2,1)}, bf16[176,128]{1,0:T(8,128)(2,1)S(1)}, u32[]{:S(2)}) copy-start(bf16[176,128]{1,0:T(8,128)(2,1)S(1)} %collective-permute-done.2.halo_l) | copy-start | bytes 135172
  25.2 13.7 %copy-start.18 = (bf16[176,128]{1,0:T(8,128)(2,1)}, bf16[176,128]{1,0:T(8,128)(2,1)S(1)}, u32[]{:S(2)}) copy-start(bf16[176,128]{1,0:T(8,128)(2,1)S(1)} %collective-permute-done.3.halo_r) | copy-start | bytes 135172
  26.7 1.0 %copy-start.10 = (f32[2304,128]{1,0:T(8,128)}, f32[2304,128]{1,0:T(8,128)S(1)}, u32[]{:S(2)}) copy-start(f32[2304,128]{1,0:T(8,128)S(1)} %get-tuple-element.35.fields) | copy-start | bytes 3538948
  27.7 0.7 copy-start.12
  28.4 0.7 copy-start.14
  29.0 6.6 %collective-permute-start.4 = (bf16[32,16,128]{2,1,0:T(8,128)(2,1)S(1)}, bf16[32,16,128]{2,1,0:T(8,128)(2,1)S(1)}, u32[]{:S(2)}, u32[]{:S(2)}) collective-permute-start(bf16[32,16,128]{2,1,0:T(8,128)(2,1)S(1)} %get-tuple-element.37), channel_id=1, source_target_pairs={{0,128},{1,129},{2,130},{3,131},{4,132},{5,133},{6,134},{7,135},{8... | collective-permute-start | bytes 393224 | tf_op jit(solution)/shard_map/ppermute | solution.py:621
  38.9 42.9 %all-to-all-start = ((bf16[32,9,16,128]{3,2,1,0:T(8,128)(2,1)}), bf16[32,9,16,128]{3,2,1,0:T(8,128)(2,1)S(1)}, u32[]{:S(2)}, u32[]{:S(2)}) async-start(bf16[32,9,16,128]{3,2,1,0:T(8,128)(2,1)} %bitcast.8), calls=%async_computation | async-start | bytes 2359296 | tf_op jit(solution)/shard_map/all_to_all | solution.py:716
  52.0 1.3 %copy-start.2 = (f32[2560,128]{1,0:T(8,128)S(1)}, f32[2560,128]{1,0:T(8,128)}, u32[]{:S(2)}) copy-start(f32[2560,128]{1,0:T(8,128)} %copy-done.1) | copy-start | bytes 3932164
  53.3 0.9 %copy-start.7 = (bf16[704,128]{1,0:T(8,128)(2,1)S(1)}, bf16[704,128]{1,0:T(8,128)(2,1)}, u32[]{:S(2)}) copy-start(bf16[704,128]{1,0:T(8,128)(2,1)} %copy-done.6) | copy-start | bytes 540676
  54.3 1.3 %copy-start.11 = (f32[2304,128]{1,0:T(8,128)S(1)}, f32[2304,128]{1,0:T(8,128)}, u32[]{:S(2)}) copy-start(f32[2304,128]{1,0:T(8,128)} %copy-done.10) | copy-start | bytes 3538948
  55.5 0.9 %copy-start.13 = (f32[384,128]{1,0:T(8,128)S(1)}, f32[384,128]{1,0:T(8,128)}, u32[]{:S(2)}) copy-start(f32[384,128]{1,0:T(8,128)} %copy-done.12) | copy-start | bytes 589828
  56.5 0.9 %copy-start.15 = (f32[384,128]{1,0:T(8,128)S(1)}, f32[384,128]{1,0:T(8,128)}, u32[]{:S(2)}) copy-start(f32[384,128]{1,0:T(8,128)} %copy-done.14) | copy-start | bytes 589828
  57.4 0.8 copy-start.17
  58.2 0.8 copy-start.19
  59.0 26.7 %copy-start = (bf16[1,64,128,128]{3,2,1,0:T(8,128)(2,1)S(1)}, bf16[1,64,128,128]{3,2,1,0:T(8,128)(2,1)}, u32[]{:S(2)}) copy-start(bf16[1,64,128,128]{3,2,1,0:T(8,128)(2,1)} %param.31) | copy-start | bytes 6291460
  59.0 26.7 %copy-start.24 = (s32[1,64]{1,0:T(1,128)S(1)}, s32[1,64]{1,0:T(1,128)}, u32[]{:S(2)}) copy-start(s32[1,64]{1,0:T(1,128)} %back_owner.3) | copy-start | bytes 772
  59.0 26.7 %copy-start.25 = (s32[1,64]{1,0:T(1,128)S(1)}, s32[1,64]{1,0:T(1,128)}, u32[]{:S(2)}) copy-start(s32[1,64]{1,0:T(1,128)} %back_src.3) | copy-start | bytes 772
  73.5 1.1 %copy-start.8 = (f32[2560,128]{1,0:T(8,128)}, f32[2560,128]{1,0:T(8,128)S(1)}, u32[]{:S(2)}) copy-start(f32[2560,128]{1,0:T(8,128)S(1)} %get-tuple-element.46.advected) | copy-start | bytes 3932164
  81.8 5.0 %collective-permute-start.5 = (bf16[64,16,128]{2,1,0:T(8,128)(2,1)S(1)}, bf16[64,16,128]{2,1,0:T(8,128)(2,1)S(1)}, u32[]{:S(2)}, u32[]{:S(2)}) collective-permute-start(bf16[64,16,128]{2,1,0:T(8,128)(2,1)S(1)} %bitcast.31), channel_id=1, source_target_pairs={{128,0},{129,1},{130,2},{131,3},{132,4},{133,5},{134,6},{135,7},{1... | collective-permute-start | bytes 786440 | tf_op jit(solution)/shard_map/ppermute | solution.py:621
  85.7 1.3 %copy-start.9 = (f32[2560,128]{1,0:T(8,128)S(1)}, f32[2560,128]{1,0:T(8,128)}, u32[]{:S(2)}) copy-start(f32[2560,128]{1,0:T(8,128)} %copy-done.8) | copy-start | bytes 3932164
  85.7 1.3 %copy-start.29 = (s32[1,64]{1,0:T(1,128)S(1)}, s32[1,64]{1,0:T(1,128)}, u32[]{:S(2)}) copy-start(s32[1,64]{1,0:T(1,128)} %back_dst.1) | copy-start | bytes 772

commit v2 on v1

--- a/solution.py
+++ b/solution.py
@@ -20,22 +20,12 @@
     return lax.broadcasted_iota(jnp.int32, (rows, W), 1)
 
 
-def fetch(src, dst, sem):
-    copy = pltpu.make_async_copy(src, dst, sem)
-    copy.start()
-    copy.wait()
-
-
 def split(value):
     hi = value.astype(BF16)
     return hi, (value - hi.astype(F32)).astype(BF16)
 
 
-def params():
-    return pltpu.CompilerParams(vmem_limit_bytes=16 * 1024 * 1024)
-
-
-def call(body, out_shape, n_smem, n_any, n_vmem, scratch):
+def call(body, out_shape, n_smem, n_any, n_vmem, scratch, mebibytes=16):
     specs = (
         [pl.BlockSpec(memory_space=pltpu.SMEM)] * n_smem
         + [pl.BlockSpec(memory_space=pl.ANY)] * n_any
@@ -47,14 +37,29 @@
         in_specs=specs,
         out_specs=[pl.BlockSpec(memory_space=pltpu.VMEM)] * len(out_shape),
         scratch_shapes=scratch,
-        compiler_params=params(),
+        compiler_params=pltpu.CompilerParams(vmem_limit_bytes=mebibytes * 1024 * 1024),
         name=body.__name__,
     )
 
 
-def pack_rows(comp, state, tracer, mass, codes, rates, up, down, rate8):
+def pack_rows(
+    comp, state_ref, tracer_ref, mass_ref, codes_ref, rates_ref, up, down, rate8,
+    buf, mass, codes, rates, sem,
+):
+    state = tracer = buf
+
+    def fetch_all(*pairs):
+        copies = [
+            pltpu.make_async_copy(src, dst, sem.at[n]) for n, (src, dst) in enumerate(pairs)
+        ]
+        for copy in copies:
+            copy.start()
+        for copy in copies:
+            copy.wait()
+
     @pl.when(comp[0] == 0)
     def _():
+        fetch_all((state_ref, buf.at[pl.ds(0, 2304)]), (mass_ref, mass))
         for dst, y in ((up, 0), (down, 31)):
             m = jnp.broadcast_to(mass[y : y + 1, :], (8, W))
             parts = [state[pl.ds(g * 256 + y, 8, stride=32), :] * m for g in range(9)] + [m]
@@ -65,6 +70,7 @@
 
     @pl.when(comp[0] == 1)
     def _():
+        fetch_all((tracer_ref, buf), (codes_ref, codes), (rates_ref, rates))
         for o in range(8):
             acc = jnp.zeros((16, W), F32)
             for k in range(6):
@@ -293,68 +299,72 @@
         lax.fori_loop(step + 1, EXT - 1 - step, row, 0)
 
 
+def edge_sums(above, below, halo_l, halo_r, buf, edge, far_l, far_r, ready, emit):
+    lane = lanes(8)
+    for p in range(5):
+        rows = slice(16 * p, 16 * p + 16)
+        rest = slice(80 + 16 * p, 96 + 16 * p)
+        v = halo_l[rows, :].astype(F32) + halo_l[rest, :].astype(F32)
+        far_l[rows, :] = pltpu.roll(v, 2, 1)
+        far_r[rows, :] = halo_r[rows, :].astype(F32) + halo_r[rest, :].astype(F32)
+        v = above[rows, :].astype(F32) + above[rest, :].astype(F32)
+        buf[16 * p : 16 * p + 16, :] = v
+        v = below[rows, :].astype(F32) + below[rest, :].astype(F32)
+        buf[2640 + 16 * p : 2656 + 16 * p, :] = v
+    for g in range(10):
+        rows = slice(8 * g, 8 * g + 8)
+        from_l, from_r = far_l[rows, :], far_r[rows, :]
+        for y in range(32):
+            v = jnp.where(lane == y, from_r, from_l)
+            at = 80 * y + 8 * g
+            edge[at : at + 8, :] = pltpu.roll(v, (W - 1 - y) % W, 1)
+    ready()
+
+    def quad(q, carry):
+        first = lane % 4 == 0
+        final = lane % 4 == 3
+        outer = (lane == 0) | (lane == W - 1)
+
+        def at(row, g, wide=80):
+            return pl.ds(pl.multiple_of(row * wide + 8 * g, 8), 8)
+
+        for r in range(4):
+            y = 4 * q + r
+            values = []
+            for g in (9, 0, 1, 2, 3, 4, 5, 6, 7, 8):
+                v = buf[at(y + 1, g), :]
+                if r == 0:
+                    v = v + buf[at(y, g), :]
+                if r == 3:
+                    v = v + buf[at(y + 2, g), :]
+                near = jnp.where(first, pltpu.roll(v, 1, 1), pltpu.roll(v, W - 1, 1))
+                near = jnp.where(outer, edge[at(y, g), :], near)
+                v = v + jnp.where(first | final, near, 0.0)
+                if g == 9:
+                    inverse = 1.0 / v
+                else:
+                    values.append(v * inverse)
+            emit(y, values, at)
+        return carry
+
+    lax.fori_loop(0, 8, quad, 0)
+
+
 def assemble(
     comp, lev_speed, turned, rate8, above, below, halo_l, halo_r, lhs,
-    dss, own, flux, top, coef_a, coef_b,
-    buf, sem, edge, high, low, far_l, far_r, ta, tb, tc, td,
+    own, flux, top,
+    buf, sem, edge, high, low, far_l, far_r, ta, tb, tc, td, coef_a, coef_b,
 ):
-    lane = lanes(8)
-
     @pl.when(comp[0] == 0)
     def _():
+        def emit(y, values, at):
+            hi, lo = split(jnp.concatenate(values + [jnp.zeros((8, W), F32)], axis=0))
+            high[y] = hi
+            low[y] = lo
+
         copy = pltpu.make_async_copy(turned, buf.at[pl.ds(80, 2560)], sem)
         copy.start()
-        for p in range(5):
-            rows = slice(16 * p, 16 * p + 16)
-            rest = slice(80 + 16 * p, 96 + 16 * p)
-            v = halo_l[rows, :].astype(F32) + halo_l[rest, :].astype(F32)
-            far_l[rows, :] = pltpu.roll(v, 2, 1)
-            far_r[rows, :] = halo_r[rows, :].astype(F32) + halo_r[rest, :].astype(F32)
-            v = above[rows, :].astype(F32) + above[rest, :].astype(F32)
-            buf[16 * p : 16 * p + 16, :] = v
-            v = below[rows, :].astype(F32) + below[rest, :].astype(F32)
-            buf[2640 + 16 * p : 2656 + 16 * p, :] = v
-        for g in range(10):
-            rows = slice(8 * g, 8 * g + 8)
-            from_l, from_r = far_l[rows, :], far_r[rows, :]
-            for y in range(32):
-                v = jnp.where(lane == y, from_r, from_l)
-                at = 80 * y + 8 * g
-                edge[at : at + 8, :] = pltpu.roll(v, (W - 1 - y) % W, 1)
-        copy.wait()
-
-        def quad(q, carry):
-            first = lane % 4 == 0
-            final = lane % 4 == 3
-            outer = (lane == 0) | (lane == W - 1)
-
-            def at(row, g, wide=80):
-                return pl.ds(pl.multiple_of(row * wide + 8 * g, 8), 8)
-
-            for r in range(4):
-                y = 4 * q + r
-                values = []
-                for g in (9, 0, 1, 2, 3, 4, 5, 6, 7, 8):
-                    v = buf[at(y + 1, g), :]
-                    if r == 0:
-                        v = v + buf[at(y, g), :]
-                    if r == 3:
-                        v = v + buf[at(y + 2, g), :]
-                    near = jnp.where(first, pltpu.roll(v, 1, 1), pltpu.roll(v, W - 1, 1))
-                    near = jnp.where(outer, edge[at(y, g), :], near)
-                    v = v + jnp.where(first | final, near, 0.0)
-                    if g == 9:
-                        inverse = 1.0 / v
-                    else:
-                        values.append(v * inverse)
-                for g, v in enumerate(values):
-                    dss[at(y, g, 72), :] = v
-                hi, lo = split(jnp.concatenate(values + [jnp.zeros((8, W), F32)], axis=0))
-                high[y] = hi
-                low[y] = lo
-            return carry
-
-        lax.fori_loop(0, 8, quad, 0)
+        edge_sums(above, below, halo_l, halo_r, buf, edge, far_l, far_r, copy.wait, emit)
         for y in range(32):
             first = jnp.dot(lhs[...], high[y], preferred_element_type=F32)
             second = jnp.dot(lhs[0:32, :], low[y], preferred_element_type=F32)
@@ -473,25 +483,37 @@
 
 
 def advect_all(
-    comp, lev_speed, turned, fields, above, below, halo_l, halo_r, coef_a, coef_b,
-    result, dss, buf, sem, ta, tb, tc, td, speed,
+    comp, lev_speed, state, tracer, mass, rate8, above, below, halo_l, halo_r, after,
+    result, dss, buf, edge, far_l, far_r, ta, tb, tc, td, coef_a, coef_b, speed,
 ):
+    del after
+
     @pl.when(comp[0] == 0)
     def _():
-        fetch(fields, buf.at[pl.ds(0, 2304)], sem)
+        def emit(y, values, at):
+            for g, v in enumerate(values):
+                ta[at(y, g, 72), :] = v
+
+        for y in range(32):
+            m = jnp.broadcast_to(mass[y : y + 1, :], (8, W))
+            for g in range(9):
+                at = 80 + 80 * y + 8 * g
+                buf[at : at + 8, :] = m * state[pl.ds(g * 256 + y, 8, stride=32), :]
+            buf[152 + 80 * y : 160 + 80 * y, :] = m
+        edge_sums(above, below, halo_l, halo_r, buf, edge, far_l, far_r, lambda: None, emit)
         for f in range(72):
             for p in range(4):
-                dss[32 * f + 8 * p : 32 * f + 8 * p + 8, :] = buf[
+                dss[32 * f + 8 * p : 32 * f + 8 * p + 8, :] = ta[
                     pl.ds(72 * 8 * p + f, 8, stride=72), :
                 ]
 
     @pl.when(comp[0] == 1)
     def _():
-        fetch(turned, buf, sem)
         dss[...] = jnp.zeros(dss.shape, F32)
+        prepare_rates(coef_a, coef_b, rate8, above, below, halo_l, halo_r)
 
         def main(g, y):
-            return buf[160 * y + 8 * g : 160 * y + 8 * g + 8, :]
+            return tracer[pl.ds(g * 128 + y, 8, stride=16), :]
 
         groups = tuple(range(20))
         fill(groups, ta, tb, main, above, below, halo_l, halo_r)
@@ -512,7 +534,7 @@
     return jnp.concatenate(wants, axis=0).astype(F32)
 
 
-def surface_select(comp, back_owner, back_src, weights, received, out):
+def surface_select(comp, back_owner, back_src, received, out):
     band = received.shape[0] // TILES_PER_PEER
 
     @pl.when(comp[0] == 0)
@@ -655,8 +677,12 @@
     up, down, rate8 = call(
         pack_rows,
         [shape(4 * PR, W, dtype=BF16), shape(4 * PR, W, dtype=BF16), shape(128, W)],
-        1, 0, 5,
-        [],
+        1, 5, 0,
+        [
+            buf, pltpu.VMEM((32, W), F32), pltpu.VMEM((96, W), jnp.int32),
+            pltpu.VMEM((96, W), F32), dma((3,)),
+        ],
+        62,
     )(comp, state, tracer, atm_mass, codes, rates)
     below = shifted(up, "gy", -1)
     above = shifted(down, "gy", 1)
@@ -678,22 +704,21 @@
     lhs = jnp.concatenate([lhs_hi, lhs_lo], axis=0)
     small = pltpu.VMEM((EXT * 8, W), F32)
 
-    fields, own, flux, top, coef_a, coef_b = call(
+    coef = pltpu.VMEM((EXT * 16, W), F32)
+    points = pltpu.VMEM((34 * 80, W), F32)
+    rows = pltpu.VMEM((80, W), F32)
+    own, flux, top = call(
         assemble,
         [
-            shape(72 * 32, W),
             shape(32, 32, W, dtype=BF16),
             shape(32, 16, W, dtype=BF16),
             shape(2, 16, W, dtype=BF16),
-            shape(EXT * 16, W),
-            shape(EXT * 16, W),
         ],
         2, 1, 6,
         [
-            pltpu.VMEM((34 * 80, W), F32), dma, buf,
-            pltpu.VMEM((32, 80, W), BF16), pltpu.VMEM((32, 80, W), BF16),
-            pltpu.VMEM((80, W), F32), pltpu.VMEM((80, W), F32),
-            small, small, small, small,
+            points, dma, buf,
+            pltpu.VMEM((32, 80, W), BF16), pltpu.VMEM((32, 80, W), BF16), rows, rows,
+            small, small, small, small, coef, coef,
         ],
     )(
         comp, lev_speed, turned, rate8, above, below, halo_l, halo_r, lhs,
@@ -712,7 +737,7 @@
         comp, flux_src_blk, flux_dest.reshape(1, 64), flux_dst_blk,
         own, arrived, conservative_flux_weights[0], top,
     )
-    send, coef_a, coef_b = lax.optimization_barrier((send, coef_a, coef_b))
+    send, top = lax.optimization_barrier((send, top))
     received = lax.all_to_all(
         send.reshape(band, TILES_PER_PEER, 16, W), "gx", 0, 0, tiled=True
     ).reshape(band * TILES_PER_PEER, 16, W)
@@ -720,17 +745,20 @@
     advected, dss = call(
         advect_all,
         [shape(16 * 160, W), shape(72 * 32, W)],
-        2, 2, 6,
-        [buf, dma, grid, grid, grid, grid, pltpu.VMEM((160, W), F32)],
+        2, 0, 9,
+        [
+            points, buf, rows, rows, grid, grid, grid, grid, coef, coef,
+            pltpu.VMEM((160, W), F32),
+        ],
     )(
-        comp, lev_speed, turned, fields, above, below, halo_l, halo_r, coef_a, coef_b,
+        comp, lev_speed, state, tracer, atm_mass, rate8, above, below, halo_l, halo_r, top,
     )
     levels = profile.reshape(160, 16)
     received, advected, levels = lax.optimization_barrier((received, advected, levels))
     tops = received.reshape(band, TILES_PER_PEER, 16, W)[:, :2].reshape(2 * band, 16, W)
     other = shifted(tops, "comp", -1)
-    mine, = call(surface_select, [shape(128, W)], 3, 1, 1, [])(
-        comp, back_owner, back_src_blk, return_remap_weights[0], received
+    mine, = call(surface_select, [shape(128, W)], 3, 0, 1, [])(
+        comp, back_owner, back_src_blk, received
     )
     ocean, surface = call(finish, [shape(2560, W), shape(64, W)], 4, 0, 6, [
         pltpu.VMEM((512, W), F32), pltpu.VMEM((512, W), F32), pltpu.VMEM((256, W), F32),

time: 92 us -> 88.5 us (0.962)
  local copies, waits for them, and re-layouts: 15.8 us -> 7.29 us
  waiting for transfers between devices: 21.6 us -> 24.9 us
  Pallas kernels: 24.8 us -> 26.5 us
    unnamed x65 -> x41, local copies, waits for them, and re-layouts: 15.6 us -> 7.19 us
    all_to_all x1, waiting for transfers between devices: 7.21 us -> 12.3 us  [shards(): lax.all_to_all(send.reshape(band, TILES_PER_PEER, 16, W), 'gx', 0, 0, til...]
    pallas_call x1, Pallas kernels: 0.28 us -> 2.47 us  [shards(): call(pack_rows, [shape(4 * PR, W, dtype=BF16), shape(4 * PR, W, dtype=BF1...]
    ppermute x6, waiting for transfers between devices: 14.4 us -> 12.6 us  [shifted(): return lax.ppermute(array, axis, pairs)]
    pallas_call x1, Pallas kernels: 3.19 us -> 2.17 us  [shards(): call(tile_products, [shape(band * TILES_PER_PEER, 16, W, dtype=BF16)], 4,...]
  transfers between devices with their start and end apart: 7 -> 7, of which waited for: 6 -> 5; matrix products, arithmetic and copies ran while one was open for 0% -> 0% of each run, Pallas kernels for 17% -> 18%
where the time goes in v2:
time: 88.5 us; the launch traced here: 87.9 us
  starting transfers between devices  28.2 us (32%)
  Pallas kernels  26.5 us (30%)
  waiting for transfers between devices  24.9 us (28%)
  local copies, waits for them, and re-layouts  7.29 us (8%)
  between operations  0.92 us (1%)
    pallas_call x1, Pallas kernels, shards(): call(advect_all, [shape(16 * 160, W), shape(72 * 32, W)], 2, 0, 9, [point...  15.1 us
    ppermute x6, starting transfers between devices, shifted(): return lax.ppermute(array, axis, pairs)  15 us
    all_to_all x1, starting transfers between devices, shards(): lax.all_to_all(send.reshape(band, TILES_PER_PEER, 16, W), 'gx', 0, 0, til...  13.1 us
    ppermute x6, waiting for transfers between devices, shifted(): return lax.ppermute(array, axis, pairs)  12.6 us
    all_to_all x1, waiting for transfers between devices, shards(): lax.all_to_all(send.reshape(band, TILES_PER_PEER, 16, W), 'gx', 0, 0, til...  12.3 us
    unnamed x41, local copies, waits for them, and re-layouts  7.19 us
    pallas_call x1, Pallas kernels, shards(): call(finish, [shape(2560, W), shape(64, W)], 4, 0, 6, [pltpu.VMEM((512, W...  4.16 us
    pallas_call x1, Pallas kernels, shards(): call(pack_rows, [shape(4 * PR, W, dtype=BF16), shape(4 * PR, W, dtype=BF1...  2.47 us
  transfers between devices with their start and end apart: 7, of which 5 were waited for; matrix products, arithmetic and copies ran while one was open for 0% of the time, Pallas kernels for 18%

profile of v2, /device:TPU:1, one launch (start us, length us, event | category | flops | bytes accessed | tf_op | source)
XLA Modules:
  0.0 87.9 jit_solution(18061596631659079438)
XLA Ops:
  0.6 0.0 copy-start.19
  0.6 0.0 copy-start
  0.7 0.0 copy-start.10
  0.7 2.5 %pack_rows.1 = (bf16[704,128]{1,0:T(8,128)(2,1)}, bf16[704,128]{1,0:T(8,128)(2,1)}, f32[128,128]{1,0:T(8,128)}) custom-call(s32[1]{0:T(128)} %bitcast.comp, f32[2304,128]{1,0:T(8,128)} %bitcast.23, f32[2560,128]{1,0:T(8,128)} %bitcast.20, f32[32,128]{1,0:T(8,128)} %mass.3, s32[96,128]{1,0:T(8,128)} %bitcast.32, f32[96,128]{1,0:T(8,128)} %bitcast.33), custom_call_target="tpu_custom_call" | custom-call | tf_op jit(solution)/shard_map/pack_rows/pallas_call | solution.py:677
  3.1 0.0 copy-start.18
  3.2 4.0 %collective-permute-start = (bf16[704,128]{1,0:T(8,128)(2,1)}, bf16[704,128]{1,0:T(8,128)(2,1)S(1)}, u32[]{:S(2)}, u32[]{:S(2)}) collective-permute-start(bf16[704,128]{1,0:T(8,128)(2,1)} %get-tuple-element.24), channel_id=1, source_target_pairs={{0,1},{1,2},{2,3},{4,5},{5,6},{6,7},{8,9},{9,10},{10,11},{12,13},{... | collective-permute-start | bytes 540680 | tf_op jit(solution)/shard_map/ppermute | solution.py:643
  7.1 1.3 %collective-permute-start.1 = (bf16[704,128]{1,0:T(8,128)(2,1)}, bf16[704,128]{1,0:T(8,128)(2,1)S(1)}, u32[]{:S(2)}, u32[]{:S(2)}) collective-permute-start(bf16[704,128]{1,0:T(8,128)(2,1)} %get-tuple-element.25), channel_id=1, source_target_pairs={{1,0},{2,1},{3,2},{5,4},{6,5},{7,6},{9,8},{10,9},{11,10},{13,12},{... | collective-permute-start | bytes 540680 | tf_op jit(solution)/shard_map/ppermute | solution.py:643
  8.4 0.0 copy-done.19
  8.4 0.1 slice_reduce_fusion
  8.5 0.0 copy-done
  8.5 0.0 copy-done.10
  8.5 0.0 copy-start.1
  8.5 1.3 %copy-done.1 = f32[1,72,32,128]{3,2,1,0:T(8,128)S(1)} copy-done((f32[1,72,32,128]{3,2,1,0:T(8,128)S(1)}, f32[1,72,32,128]{3,2,1,0:T(8,128)}, u32[]{:S(2)}) %copy-start.1) | copy-done | bytes 1179672
  9.8 0.0 copy-start.8
  9.8 0.8 copy-done.8
  10.6 0.0 copy-start.13
  10.6 0.5 pack_columns.1
  11.1 0.0 copy-done.18
  11.2 0.0 copy-start.4
  11.2 0.0 copy-start.14
  11.2 0.0 copy-start.15
  11.2 0.0 copy-start.16
  11.2 0.1 fusion.1
  11.4 0.0 collective-permute-done.above
  11.4 3.2 %collective-permute-done.1.below = bf16[704,128]{1,0:T(8,128)(2,1)S(1)} collective-permute-done((bf16[704,128]{1,0:T(8,128)(2,1)}, bf16[704,128]{1,0:T(8,128)(2,1)S(1)}, u32[]{:S(2)}, u32[]{:S(2)}) %collective-permute-start.1) | collective-permute-done | bytes 180256 | tf_op jit(solution)/shard_map/ppermute | solution.py:643
  14.6 0.2 finish_columns.1
  14.8 3.2 %collective-permute-start.2 = (bf16[176,128]{1,0:T(8,128)(2,1)S(1)}, bf16[176,128]{1,0:T(8,128)(2,1)S(1)}, u32[]{:S(2)}, u32[]{:S(2)}) collective-permute-start(bf16[176,128]{1,0:T(8,128)(2,1)S(1)} %get-tuple-element.28), channel_id=1, source_target_pairs={{0,4},{4,8},{8,12},{12,16},{16,20},{20,24},{24,28},{28,32},{32,36}... | collective-permute-start | bytes 135176 | tf_op jit(solution)/shard_map/ppermute | solution.py:643
  18.0 1.3 %collective-permute-start.3 = (bf16[176,128]{1,0:T(8,128)(2,1)S(1)}, bf16[176,128]{1,0:T(8,128)(2,1)S(1)}, u32[]{:S(2)}, u32[]{:S(2)}) collective-permute-start(bf16[176,128]{1,0:T(8,128)(2,1)S(1)} %get-tuple-element.29), channel_id=1, source_target_pairs={{4,0},{8,4},{12,8},{16,12},{20,16},{24,20},{28,24},{32,28},{36,32}... | collective-permute-start | bytes 135176 | tf_op jit(solution)/shard_map/ppermute | solution.py:643
  19.3 0.0 collective-permute-done.2.halo_l
  19.3 3.5 %collective-permute-done.3.halo_r = bf16[176,128]{1,0:T(8,128)(2,1)S(1)} collective-permute-done((bf16[176,128]{1,0:T(8,128)(2,1)S(1)}, bf16[176,128]{1,0:T(8,128)(2,1)S(1)}, u32[]{:S(2)}, u32[]{:S(2)}) %collective-permute-start.3) | collective-permute-done | bytes 45088 | tf_op jit(solution)/shard_map/ppermute | solution.py:643
  22.8 0.0 copy-done.13
  22.8 1.4 %assemble.1 = (bf16[32,32,128]{2,1,0:T(8,128)(2,1)S(1)}, bf16[32,16,128]{2,1,0:T(8,128)(2,1)S(1)}, bf16[2,16,128]{2,1,0:T(8,128)(2,1)S(1)}) custom-call(s32[1]{0:T(128)} %bitcast.comp, f32[80]{0:T(128)S(1)} %copy-done.13, f32[2560,128]{1,0:T(8,128)S(1)} %get-tuple-element.30.turned, f32[128,128]{1,0:T(8,128)S(1)} %copy-done.8, ...), custom_call_target="tpu_custom_call" | custom-call | tf_op jit(solution)/shard_map/assemble/pallas_call | solution.py:710
  24.2 1.3 %collective-permute-start.4 = (bf16[32,16,128]{2,1,0:T(8,128)(2,1)S(1)}, bf16[32,16,128]{2,1,0:T(8,128)(2,1)S(1)}, u32[]{:S(2)}, u32[]{:S(2)}) collective-permute-start(bf16[32,16,128]{2,1,0:T(8,128)(2,1)S(1)} %get-tuple-element.32), channel_id=1, source_target_pairs={{0,128},{1,129},{2,130},{3,131},{4,132},{5,133},{6,134},{7,135},{8... | collective-permute-start | bytes 393224 | tf_op jit(solution)/shard_map/ppermute | solution.py:643
  25.5 5.3 %collective-permute-done.4.arrived = bf16[32,16,128]{2,1,0:T(8,128)(2,1)S(1)} collective-permute-done((bf16[32,16,128]{2,1,0:T(8,128)(2,1)S(1)}, bf16[32,16,128]{2,1,0:T(8,128)(2,1)S(1)}, u32[]{:S(2)}, u32[]{:S(2)}) %collective-permute-start.4) | collective-permute-done | bytes 131104 | tf_op jit(solution)/shard_map/ppermute | solution.py:643
  30.8 0.0 copy-done.4
  30.8 0.0 copy-done.14
  30.8 0.0 copy-done.15
  30.8 0.0 copy-done.16
  30.9 2.2 %tile_products.1 = bf16[288,16,128]{2,1,0:T(8,128)(2,1)S(1)} custom-call(s32[1]{0:T(128)} %bitcast.comp, s32[1,64]{1,0:T(1,128)S(1)} %copy-done.14, s32[1,64]{1,0:T(1,128)S(1)} %bitcast.30, s32[1,64]{1,0:T(1,128)S(1)} %copy-done.16, bf16[32,32,128]{2,1,0:T(8,128)(2,1)S(1)} %get-tuple-element.31.own, bf16[32,16,128]{2,1,0:T(8,128)(2,1)S(1)} %collective-permute-done.4.arrived, ...), custom_call_target="tpu_custom_call" | custom-call | tf_op jit(solution)/shard_map/tile_products/pallas_call | solution.py:727
  33.0 0.0 copy-start.3
  33.0 1.0 %copy-done.3 = bf16[288,16,128]{2,1,0:T(8,128)(2,1)} copy-done((bf16[288,16,128]{2,1,0:T(8,128)(2,1)}, bf16[288,16,128]{2,1,0:T(8,128)(2,1)S(1)}, u32[]{:S(2)}) %copy-start.3) | copy-done | bytes 1179672
  34.1 0.0 copy-start.9
  34.1 13.1 %all-to-all-start = ((bf16[32,9,16,128]{3,2,1,0:T(8,128)(2,1)}), bf16[32,9,16,128]{3,2,1,0:T(8,128)(2,1)S(1)}, u32[]{:S(2)}, u32[]{:S(2)}) async-start(bf16[32,9,16,128]{3,2,1,0:T(8,128)(2,1)} %bitcast.26), calls=%async_computation | async-start | bytes 2359296 | tf_op jit(solution)/shard_map/all_to_all | solution.py:741
  47.2 0.1 copy.20
  47.3 0.0 copy-done.9
  47.3 0.0 copy-start.2
  47.3 1.3 %copy-done.2 = f32[1,72,32,128]{3,2,1,0:T(8,128)S(1)} copy-done((f32[1,72,32,128]{3,2,1,0:T(8,128)S(1)}, f32[1,72,32,128]{3,2,1,0:T(8,128)}, u32[]{:S(2)}) %copy-start.2) | copy-done | bytes 1179672
  48.6 0.0 copy-start.11
  48.6 0.0 copy-start.12
  48.6 15.1 %advect_all.1 = (f32[2560,128]{1,0:T(8,128)S(1)}, f32[2304,128]{1,0:T(8,128)}) custom-call(s32[1]{0:T(128)} %bitcast.comp, f32[80]{0:T(128)S(1)} %copy-done.13, f32[2304,128]{1,0:T(8,128)S(1)} %bitcast.25, f32[2560,128]{1,0:T(8,128)S(1)} %bitcast.22, f32[32,128]{1,0:T(8,128)S(1)} %copy-done.10, f32[128,128]{1,0:T(8,128)S(1)} %copy-done.9, ...), custom_call_target="tpu_custom_call" | custom-call | tf_op jit(solution)/shard_map/advect_all/pallas_call | solution.py:745
  63.6 0.0 copy-start.6
  63.6 1.1 %copy-done.6 = f32[2560,128]{1,0:T(8,128)} copy-done((f32[2560,128]{1,0:T(8,128)}, f32[2560,128]{1,0:T(8,128)S(1)}, u32[]{:S(2)}) %copy-start.6) | copy-done | bytes 1310744
  64.7 0.0 copy-start.17
  64.7 12.3 %all-to-all-done = bf16[32,9,16,128]{3,2,1,0:T(8,128)(2,1)S(1)} async-done(((bf16[32,9,16,128]{3,2,1,0:T(8,128)(2,1)}), bf16[32,9,16,128]{3,2,1,0:T(8,128)(2,1)S(1)}, u32[]{:S(2)}, u32[]{:S(2)}) %all-to-all-start) | async-done | bytes 1179680 | tf_op jit(solution)/shard_map/all_to_all | solution.py:741
  77.0 0.0 copy-start.7
  77.0 4.0 %collective-permute-start.5 = (bf16[64,16,128]{2,1,0:T(8,128)(2,1)S(1)}, bf16[64,16,128]{2,1,0:T(8,128)(2,1)S(1)}, u32[]{:S(2)}, u32[]{:S(2)}) collective-permute-start(bf16[64,16,128]{2,1,0:T(8,128)(2,1)S(1)} %bitcast.31), channel_id=1, source_target_pairs={{128,0},{129,1},{130,2},{131,3},{132,4},{133,5},{134,6},{135,7},{1... | collective-permute-start | bytes 786440 | tf_op jit(solution)/shard_map/ppermute | solution.py:643
  81.0 0.0 copy-done.11
  81.1 0.0 copy-done.12
  81.1 0.6 surface_select.1.mine
  81.6 0.6 collective-permute-done.5.other
  82.2 0.0 copy-done.17
  82.2 0.0 copy-done.7
  82.2 1.6 %copy-done.5 = bf16[1,64,128,128]{3,2,1,0:T(8,128)(2,1)S(1)} copy-done((bf16[1,64,128,128]{3,2,1,0:T(8,128)(2,1)S(1)}, bf16[1,64,128,128]{3,2,1,0:T(8,128)(2,1)}, u32[]{:S(2)}) %copy-start.5) | copy-done | bytes 2097176
  83.8 4.2 %finish.1 = (f32[2560,128]{1,0:T(8,128)}, f32[64,128]{1,0:T(8,128)}) custom-call(s32[1]{0:T(128)} %bitcast.comp, s32[1,64]{1,0:T(1,128)S(1)} %copy-done.11, s32[1,64]{1,0:T(1,128)S(1)} %copy-done.12, s32[1,64]{1,0:T(1,128)S(1)} %copy-done.17, f32[2560,128]{1,0:T(8,128)S(1)} %copy-done.7, bf16[288,16,128]{2,1,0:T(8,128)(2,1)S(1)} %bitcast.19, ...), custom_call_target="tpu_custom_call" | custom-call | tf_op jit(solution)/shard_map/finish/pallas_call | solution.py:763
  (5 shorter events, 0.1 us)
Async XLA Ops:
  0.6 7.8 %copy-start.19 = (f32[2,80,16]{1,2,0:T(8,128)S(1)}, f32[2,80,16]{1,2,0:T(8,128)}, u32[]{:S(2)}) copy-start(f32[2,80,16]{1,2,0:T(8,128)} %param.27) | copy-start | bytes 30724
  0.6 7.9 %copy-start = (f32[1,2,80,16,128]{4,3,2,1,0:T(8,128)S(1)}, f32[1,2,80,16,128]{4,3,2,1,0:T(8,128)}, u32[]{:S(2)}) copy-start(f32[1,2,80,16,128]{4,3,2,1,0:T(8,128)} %param.23) | copy-start | bytes 3932164
  0.7 7.9 %copy-start.10 = (f32[32,128]{1,0:T(8,128)S(1)}, f32[32,128]{1,0:T(8,128)}, u32[]{:S(2)}) copy-start(f32[32,128]{1,0:T(8,128)} %mass.3) | copy-start | bytes 49156
  3.1 8.0 %copy-start.18 = (f32[16,72]{1,0:T(8,128)S(1)}, f32[16,72]{1,0:T(8,128)}, u32[]{:S(2)}) copy-start(f32[16,72]{1,0:T(8,128)} %param.18) | copy-start | bytes 13828
  3.2 8.2 %collective-permute-start = (bf16[704,128]{1,0:T(8,128)(2,1)}, bf16[704,128]{1,0:T(8,128)(2,1)S(1)}, u32[]{:S(2)}, u32[]{:S(2)}) collective-permute-start(bf16[704,128]{1,0:T(8,128)(2,1)} %get-tuple-element.24), channel_id=1, source_target_pairs={{0,1},{1,2},{2,3},{4,5},{5,6},{6,7},{8,9},{9,10},{10,11},{12,13},{... | collective-permute-start | bytes 540680 | tf_op jit(solution)/shard_map/ppermute | solution.py:643
  7.1 7.5 %collective-permute-start.1 = (bf16[704,128]{1,0:T(8,128)(2,1)}, bf16[704,128]{1,0:T(8,128)(2,1)S(1)}, u32[]{:S(2)}, u32[]{:S(2)}) collective-permute-start(bf16[704,128]{1,0:T(8,128)(2,1)} %get-tuple-element.25), channel_id=1, source_target_pairs={{1,0},{2,1},{3,2},{5,4},{6,5},{7,6},{9,8},{10,9},{11,10},{13,12},{... | collective-permute-start | bytes 540680 | tf_op jit(solution)/shard_map/ppermute | solution.py:643
  8.5 1.3 %copy-start.1 = (f32[1,72,32,128]{3,2,1,0:T(8,128)S(1)}, f32[1,72,32,128]{3,2,1,0:T(8,128)}, u32[]{:S(2)}) copy-start(f32[1,72,32,128]{3,2,1,0:T(8,128)} %param.16) | copy-start | bytes 3538948
  9.8 0.8 copy-start.8
  10.6 12.1 %copy-start.13 = (f32[80]{0:T(128)S(1)}, f32[80]{0:T(128)}, u32[]{:S(2)}) copy-start(f32[80]{0:T(128)} %lev_speed.3) | copy-start | bytes 964
  11.2 19.7 %copy-start.4 = (bf16[1,64,128,128]{3,2,1,0:T(8,128)(2,1)S(1)}, bf16[1,64,128,128]{3,2,1,0:T(8,128)(2,1)}, u32[]{:S(2)}) copy-start(bf16[1,64,128,128]{3,2,1,0:T(8,128)(2,1)} %param.22) | copy-start | bytes 6291460
  11.2 19.7 %copy-start.14 = (s32[1,64]{1,0:T(1,128)S(1)}, s32[1,64]{1,0:T(1,128)}, u32[]{:S(2)}) copy-start(s32[1,64]{1,0:T(1,128)} %src.1) | copy-start | bytes 772
  11.2 19.7 %copy-start.15 = (s32[1,64,1]{1,2,0:T(1,128)S(1)}, s32[1,64,1]{1,2,0:T(1,128)}, u32[]{:S(2)}) copy-start(s32[1,64,1]{1,2,0:T(1,128)} %param.19) | copy-start | bytes 772
  11.2 19.7 %copy-start.16 = (s32[1,64]{1,0:T(1,128)S(1)}, s32[1,64]{1,0:T(1,128)}, u32[]{:S(2)}) copy-start(s32[1,64]{1,0:T(1,128)} %dst.1) | copy-start | bytes 772
  14.8 4.5 %collective-permute-start.2 = (bf16[176,128]{1,0:T(8,128)(2,1)S(1)}, bf16[176,128]{1,0:T(8,128)(2,1)S(1)}, u32[]{:S(2)}, u32[]{:S(2)}) collective-permute-start(bf16[176,128]{1,0:T(8,128)(2,1)S(1)} %get-tuple-element.28), channel_id=1, source_target_pairs={{0,4},{4,8},{8,12},{12,16},{16,20},{20,24},{24,28},{28,32},{32,36}... | collective-permute-start | bytes 135176 | tf_op jit(solution)/shard_map/ppermute | solution.py:643
  18.0 4.8 %collective-permute-start.3 = (bf16[176,128]{1,0:T(8,128)(2,1)S(1)}, bf16[176,128]{1,0:T(8,128)(2,1)S(1)}, u32[]{:S(2)}, u32[]{:S(2)}) collective-permute-start(bf16[176,128]{1,0:T(8,128)(2,1)S(1)} %get-tuple-element.29), channel_id=1, source_target_pairs={{4,0},{8,4},{12,8},{16,12},{20,16},{24,20},{28,24},{32,28},{36,32}... | collective-permute-start | bytes 135176 | tf_op jit(solution)/shard_map/ppermute | solution.py:643
  24.2 6.6 %collective-permute-start.4 = (bf16[32,16,128]{2,1,0:T(8,128)(2,1)S(1)}, bf16[32,16,128]{2,1,0:T(8,128)(2,1)S(1)}, u32[]{:S(2)}, u32[]{:S(2)}) collective-permute-start(bf16[32,16,128]{2,1,0:T(8,128)(2,1)S(1)} %get-tuple-element.32), channel_id=1, source_target_pairs={{0,128},{1,129},{2,130},{3,131},{4,132},{5,133},{6,134},{7,135},{8... | collective-permute-start | bytes 393224 | tf_op jit(solution)/shard_map/ppermute | solution.py:643
  33.0 1.0 %copy-start.3 = (bf16[288,16,128]{2,1,0:T(8,128)(2,1)}, bf16[288,16,128]{2,1,0:T(8,128)(2,1)S(1)}, u32[]{:S(2)}) copy-start(bf16[288,16,128]{2,1,0:T(8,128)(2,1)S(1)} %tile_products.1) | copy-start | bytes 3538948
  34.1 13.2 %copy-start.9 = (f32[128,128]{1,0:T(8,128)S(1)}, f32[128,128]{1,0:T(8,128)}, u32[]{:S(2)}) copy-start(f32[128,128]{1,0:T(8,128)} %get-tuple-element.23.rate8) | copy-start | bytes 196612
  34.1 43.0 %all-to-all-start = ((bf16[32,9,16,128]{3,2,1,0:T(8,128)(2,1)}), bf16[32,9,16,128]{3,2,1,0:T(8,128)(2,1)S(1)}, u32[]{:S(2)}, u32[]{:S(2)}) async-start(bf16[32,9,16,128]{3,2,1,0:T(8,128)(2,1)} %bitcast.26), calls=%async_computation | async-start | bytes 2359296 | tf_op jit(solution)/shard_map/all_to_all | solution.py:741
  47.3 1.3 %copy-start.2 = (f32[1,72,32,128]{3,2,1,0:T(8,128)S(1)}, f32[1,72,32,128]{3,2,1,0:T(8,128)}, u32[]{:S(2)}) copy-start(f32[1,72,32,128]{3,2,1,0:T(8,128)} %param.16) | copy-start | bytes 3538948
  48.6 32.5 %copy-start.11 = (s32[1,64]{1,0:T(1,128)S(1)}, s32[1,64]{1,0:T(1,128)}, u32[]{:S(2)}) copy-start(s32[1,64]{1,0:T(1,128)} %back_owner.3) | copy-start | bytes 772
  48.6 32.5 %copy-start.12 = (s32[1,64]{1,0:T(1,128)S(1)}, s32[1,64]{1,0:T(1,128)}, u32[]{:S(2)}) copy-start(s32[1,64]{1,0:T(1,128)} %back_src.3) | copy-start | bytes 772
  63.6 1.1 %copy-start.6 = (f32[2560,128]{1,0:T(8,128)}, f32[2560,128]{1,0:T(8,128)S(1)}, u32[]{:S(2)}) copy-start(f32[2560,128]{1,0:T(8,128)S(1)} %get-tuple-element.38.advected) | copy-start | bytes 3932164
  64.7 17.5 %copy-start.17 = (s32[1,64]{1,0:T(1,128)S(1)}, s32[1,64]{1,0:T(1,128)}, u32[]{:S(2)}) copy-start(s32[1,64]{1,0:T(1,128)} %back_dst.1) | copy-start | bytes 772
  77.0 5.2 %copy-start.7 = (f32[2560,128]{1,0:T(8,128)S(1)}, f32[2560,128]{1,0:T(8,128)}, u32[]{:S(2)}) copy-start(f32[2560,128]{1,0:T(8,128)} %copy-done.6) | copy-start | bytes 3932164
  77.0 5.1 %collective-permute-start.5 = (bf16[64,16,128]{2,1,0:T(8,128)(2,1)S(1)}, bf16[64,16,128]{2,1,0:T(8,128)(2,1)S(1)}, u32[]{:S(2)}, u32[]{:S(2)}) collective-permute-start(bf16[64,16,128]{2,1,0:T(8,128)(2,1)S(1)} %bitcast.31), channel_id=1, source_target_pairs={{128,0},{129,1},{130,2},{131,3},{132,4},{133,5},{134,6},{135,7},{1... | collective-permute-start | bytes 786440 | tf_op jit(solution)/shard_map/ppermute | solution.py:643
  82.2 1.6 %copy-start.5 = (bf16[1,64,128,128]{3,2,1,0:T(8,128)(2,1)S(1)}, bf16[1,64,128,128]{3,2,1,0:T(8,128)(2,1)}, u32[]{:S(2)}) copy-start(bf16[1,64,128,128]{3,2,1,0:T(8,128)(2,1)} %param.31) | copy-start | bytes 6291460

commit v3 on v2

--- a/solution.py
+++ b/solution.py
@@ -14,10 +14,24 @@
 PR = 176
 EXT = 24
 TILES_PER_PEER = 9
+CHUNKS = 8
 
 
 def lanes(rows):
     return lax.broadcasted_iota(jnp.int32, (rows, W), 1)
+
+
+def in_hbm(array):
+    return pltpu.with_memory_space_constraint(array, pltpu.HBM)
+
+
+def in_pieces(src, dst, sem):
+    size = src.shape[0] // CHUNKS
+    spans = [pl.ds(size * n, size) for n in range(CHUNKS)]
+    return [
+        pltpu.make_async_copy(src.at[span], dst.at[span], sem.at[n])
+        for n, span in enumerate(spans)
+    ]
 
 
 def split(value):
@@ -48,6 +62,10 @@
 ):
     state = tracer = buf
 
+    def pieces(ref, rows):
+        spans = [pl.ds(rows // CHUNKS * n, rows // CHUNKS) for n in range(CHUNKS)]
+        return [(ref.at[span], buf.at[span]) for span in spans]
+
     def fetch_all(*pairs):
         copies = [
             pltpu.make_async_copy(src, dst, sem.at[n]) for n, (src, dst) in enumerate(pairs)
@@ -59,7 +77,7 @@
 
     @pl.when(comp[0] == 0)
     def _():
-        fetch_all((state_ref, buf.at[pl.ds(0, 2304)]), (mass_ref, mass))
+        fetch_all(*pieces(state_ref, 2304), (mass_ref, mass))
         for dst, y in ((up, 0), (down, 31)):
             m = jnp.broadcast_to(mass[y : y + 1, :], (8, W))
             parts = [state[pl.ds(g * 256 + y, 8, stride=32), :] * m for g in range(9)] + [m]
@@ -70,7 +88,7 @@
 
     @pl.when(comp[0] == 1)
     def _():
-        fetch_all((tracer_ref, buf), (codes_ref, codes), (rates_ref, rates))
+        fetch_all(*pieces(tracer_ref, 2560), (codes_ref, codes), (rates_ref, rates))
         for o in range(8):
             acc = jnp.zeros((16, W), F32)
             for k in range(6):
@@ -534,8 +552,14 @@
     return jnp.concatenate(wants, axis=0).astype(F32)
 
 
-def surface_select(comp, back_owner, back_src, received, out):
+def select_or_force(
+    comp, back_owner, back_src, received_ref, advected_ref, profile, out, ocean,
+    received, advected, sem, sem2,
+):
     band = received.shape[0] // TILES_PER_PEER
+    arrivals = in_pieces(received_ref, received, sem)
+    for copy in arrivals:
+        copy.start()
 
     @pl.when(comp[0] == 0)
     def _():
@@ -562,21 +586,64 @@
             return tuple(totals)
 
         zero = jnp.zeros((64, W), F32)
-        sums = lax.fori_loop(0, band // 2, pair, (zero, zero), unroll=4)
+        sums = (zero, zero)
+        for n, copy in enumerate(arrivals):
+            copy.wait()
+            for q in range(n * band // (2 * CHUNKS), (n + 1) * band // (2 * CHUNKS)):
+                sums = pair(q, sums)
         for v in range(2):
             out[64 * v : 64 * v + 64, :] = sums[v]
+        ocean[...] = jnp.zeros(ocean.shape, F32)
+
+    @pl.when(comp[0] == 1)
+    def _():
+        others = in_pieces(advected_ref, advected, sem2)
+        for copy in others:
+            copy.start()
+        row = lax.broadcasted_iota(jnp.int32, (256, W), 0)
+        point = jnp.where(row % 16 == lanes(256) % 16, row // 16, -2).astype(F32)
+
+        def add(h, total):
+            named = received[h * TILES_PER_PEER + 8].astype(F32)[2:3, :]
+            hot = jnp.where(jnp.broadcast_to(named, (256, W)) == point, 1.0, 0.0)
+            rhs = jnp.concatenate(
+                [received[h * TILES_PER_PEER + j] for j in range(8)], axis=0
+            )
+            return total + jnp.dot(hot.astype(BF16), rhs, preferred_element_type=F32)
+
+        total = jnp.zeros((256, W), F32)
+        for n, copy in enumerate(arrivals):
+            copy.wait()
+            for h in range(n * band // CHUNKS, (n + 1) * band // CHUNKS):
+                total = add(h, total)
+        level_hi, level_lo = split(profile[...])
+        for y in range(16):
+            if y % 2 == 0:
+                others[y // 2].wait()
+            hi, lo = split(total[16 * y : 16 * y + 16, :])
+            more = (
+                jnp.dot(level_hi, hi, preferred_element_type=F32)
+                + jnp.dot(level_hi, lo, preferred_element_type=F32)
+                + jnp.dot(level_lo, hi, preferred_element_type=F32)
+            )
+            new = advected[160 * y : 160 * y + 160, :] + more
+            for g in range(20):
+                ocean[pl.ds(g * 128 + y, 8, stride=16), :] = new[8 * g : 8 * g + 8]
 
 
 def finish(
-    comp, back_owner, back_src, back_dst,
-    advected, received, profile, weights, mine, other,
-    ocean, surface, table, parts, acc,
+    comp, back_owner, back_src, back_dst, weights_ref, mine, other,
+    surface, weights, sem, table, parts, acc,
 ):
-    band = received.shape[0] // TILES_PER_PEER
+    band = other.shape[0] // 2
     tiles = weights.shape[0]
 
     @pl.when(comp[0] == 0)
     def _():
+        chunk = tiles // CHUNKS
+        copies = in_pieces(weights_ref, weights, sem)
+        for copy in copies:
+            copy.start()
         want = wanted(back_owner, back_src)
         sums = [mine[64 * v : 64 * v + 64, :] for v in range(2)]
         for c in range(band // 8):
@@ -592,6 +659,8 @@
                     table[pl.ds(64 * p + at, 8, stride=8), :] = part[8 * p : 8 * p + 8]
         acc[...] = jnp.zeros(acc.shape, F32)
         for t in range(tiles):
+            if t % chunk == 0:
+                copies[t // chunk].wait()
             parts[8 * t : 8 * t + 8, :] = lax.dot_general(
                 table[8 * t : 8 * t + 8, :].astype(BF16),
                 weights[t],
@@ -607,34 +676,10 @@
                     acc[pl.ds(64 * p + v, 8, stride=8), :]
                     + acc[pl.ds(64 * p + 2 + v, 8, stride=8), :]
                 )
-        ocean[...] = jnp.zeros(ocean.shape, F32)
 
     @pl.when(comp[0] == 1)
     def _():
         surface[...] = jnp.zeros(surface.shape, F32)
-        row = lax.broadcasted_iota(jnp.int32, (256, W), 0)
-        point = jnp.where(row % 16 == lanes(256) % 16, row // 16, -2).astype(F32)
-
-        def add(h, total):
-            named = received[h * TILES_PER_PEER + 8].astype(F32)[2:3, :]
-            hot = jnp.where(jnp.broadcast_to(named, (256, W)) == point, 1.0, 0.0)
-            rhs = jnp.concatenate(
-                [received[h * TILES_PER_PEER + j] for j in range(8)], axis=0
-            )
-            return total + jnp.dot(hot.astype(BF16), rhs, preferred_element_type=F32)
-
-        total = lax.fori_loop(0, band, add, jnp.zeros((256, W), F32), unroll=4)
-        level_hi, level_lo = split(profile[...])
-        for y in range(16):
-            hi, lo = split(total[16 * y : 16 * y + 16, :])
-            more = (
-                jnp.dot(level_hi, hi, preferred_element_type=F32)
-                + jnp.dot(level_hi, lo, preferred_element_type=F32)
-                + jnp.dot(level_lo, hi, preferred_element_type=F32)
-            )
-            new = advected[160 * y : 160 * y + 160, :] + more
-            for g in range(20):
-                ocean[pl.ds(g * 128 + y, 8, stride=16), :] = new[8 * g : 8 * g + 8]
 
 
 def shifted(array, axis, by):
@@ -680,7 +725,7 @@
         1, 5, 0,
         [
             buf, pltpu.VMEM((32, W), F32), pltpu.VMEM((96, W), jnp.int32),
-            pltpu.VMEM((96, W), F32), dma((3,)),
+            pltpu.VMEM((96, W), F32), dma((CHUNKS + 2,)),
         ],
         62,
     )(comp, state, tracer, atm_mass, codes, rates)
@@ -757,14 +802,17 @@
     received, advected, levels = lax.optimization_barrier((received, advected, levels))
     tops = received.reshape(band, TILES_PER_PEER, 16, W)[:, :2].reshape(2 * band, 16, W)
     other = shifted(tops, "comp", -1)
-    mine, = call(surface_select, [shape(128, W)], 3, 0, 1, [])(
-        comp, back_owner, back_src_blk, received
-    )
-    ocean, surface = call(finish, [shape(2560, W), shape(64, W)], 4, 0, 6, [
+    mine, ocean = call(select_or_force, [shape(128, W), shape(2560, W)], 3, 2, 1, [
+        pltpu.VMEM((band * TILES_PER_PEER, 16, W), BF16), buf,
+        dma((CHUNKS,)), dma((CHUNKS,)),
+    ])(
+        comp, back_owner, back_src_blk, in_hbm(received), in_hbm(advected), levels
+    )
+    surface, = call(finish, [shape(64, W)], 4, 1, 2, [
+        pltpu.VMEM(return_remap_weights.shape[1:], BF16), dma((CHUNKS,)),
         pltpu.VMEM((512, W), F32), pltpu.VMEM((512, W), F32), pltpu.VMEM((256, W), F32),
     ])(
-        comp, back_owner, back_src_blk, back_dst_blk,
-        advected, received, levels, return_remap_weights[0], mine, other,
+        comp, back_owner, back_src_blk, back_dst_blk, in_hbm(return_remap_weights[0]), mine, other,
     )
     return (
         dss.reshape(1, 72, 32, W),

time: 88.5 us -> 90.1 us (1.018)
  Pallas kernels: 26.5 us -> 29.3 us
  local copies, waits for them, and re-layouts: 7.29 us -> 5.41 us
    unnamed x41 -> x37, local copies, waits for them, and re-layouts: 7.19 us -> 4.36 us
    pallas_call x2, Pallas kernels: 4.71 us -> 7.43 us  [the longest x1 6.17 us: shards(): call(select_or_force, [shape(128, W), shape(2560, W)], 3, 2, 1, [pltpu.VM...]
    all_to_all x1, waiting for transfers between devices: 12.3 us -> 13.5 us  [shards(): lax.all_to_all(send.reshape(band, TILES_PER_PEER, 16, W), 'gx', 0, 0, til...]
    slice x1, local copies, waits for them, and re-layouts: 0.02 us -> 0.97 us  [shards(): received.reshape(band, TILES_PER_PEER, 16, W)[:, :2]]
  transfers between devices with their start and end apart: 7 -> 7, of which waited for: 5 -> 4; matrix products, arithmetic and copies ran while one was open for 0% -> 0% of each run, Pallas kernels for 18% -> 24%
where the time goes in v3:
time: 90.1 us; the launch traced here: 89.6 us
  Pallas kernels  29.3 us (33%)
  starting transfers between devices  28.1 us (31%)
  waiting for transfers between devices  25.6 us (28%)
  local copies, waits for them, and re-layouts  5.41 us (6%)
  between operations  0.95 us (1%)
    pallas_call x1, Pallas kernels, shards(): call(advect_all, [shape(16 * 160, W), shape(72 * 32, W)], 2, 0, 9, [point...  15.1 us
    ppermute x6, starting transfers between devices, shifted(): return lax.ppermute(array, axis, pairs)  14.9 us
    all_to_all x1, waiting for transfers between devices, shards(): lax.all_to_all(send.reshape(band, TILES_PER_PEER, 16, W), 'gx', 0, 0, til...  13.5 us
    all_to_all x1, starting transfers between devices, shards(): lax.all_to_all(send.reshape(band, TILES_PER_PEER, 16, W), 'gx', 0, 0, til...  13.2 us
    ppermute x6, waiting for transfers between devices, shifted(): return lax.ppermute(array, axis, pairs)  12 us
    pallas_call x1, Pallas kernels, shards(): call(select_or_force, [shape(128, W), shape(2560, W)], 3, 2, 1, [pltpu.VM...  6.17 us
    unnamed x37, local copies, waits for them, and re-layouts  4.36 us
    pallas_call x1, Pallas kernels, shards(): call(pack_rows, [shape(4 * PR, W, dtype=BF16), shape(4 * PR, W, dtype=BF1...  2.6 us
  transfers between devices with their start and end apart: 7, of which 4 were waited for; matrix products, arithmetic and copies ran while one was open for 0% of the time, Pallas kernels for 24%

profile of v3, /device:TPU:1, one launch (start us, length us, event | category | flops | bytes accessed | tf_op | source)
XLA Modules:
  0.0 89.6 jit_solution(8999182998761667018)
XLA Ops:
  0.6 0.0 copy-start.17
  0.6 0.0 copy-start
  0.7 0.0 copy-start.8
  0.7 2.6 %pack_rows.1 = (bf16[704,128]{1,0:T(8,128)(2,1)}, bf16[704,128]{1,0:T(8,128)(2,1)}, f32[128,128]{1,0:T(8,128)}) custom-call(s32[1]{0:T(128)} %bitcast.comp, f32[2304,128]{1,0:T(8,128)} %bitcast.21, f32[2560,128]{1,0:T(8,128)} %bitcast.18, f32[32,128]{1,0:T(8,128)} %mass.3, s32[96,128]{1,0:T(8,128)} %bitcast.30, f32[96,128]{1,0:T(8,128)} %bitcast.31), custom_call_target="tpu_custom_call" | custom-call | tf_op jit(solution)/shard_map/pack_rows/pallas_call | solution.py:722
  3.3 0.0 copy-start.16
  3.3 4.0 %collective-permute-start = (bf16[704,128]{1,0:T(8,128)(2,1)}, bf16[704,128]{1,0:T(8,128)(2,1)S(1)}, u32[]{:S(2)}, u32[]{:S(2)}) collective-permute-start(bf16[704,128]{1,0:T(8,128)(2,1)} %get-tuple-element.24), channel_id=1, source_target_pairs={{0,1},{1,2},{2,3},{4,5},{5,6},{6,7},{8,9},{9,10},{10,11},{12,13},{... | collective-permute-start | bytes 540680 | tf_op jit(solution)/shard_map/ppermute | solution.py:688
  7.2 1.3 %collective-permute-start.1 = (bf16[704,128]{1,0:T(8,128)(2,1)}, bf16[704,128]{1,0:T(8,128)(2,1)S(1)}, u32[]{:S(2)}, u32[]{:S(2)}) collective-permute-start(bf16[704,128]{1,0:T(8,128)(2,1)} %get-tuple-element.25), channel_id=1, source_target_pairs={{1,0},{2,1},{3,2},{5,4},{6,5},{7,6},{9,8},{10,9},{11,10},{13,12},{... | collective-permute-start | bytes 540680 | tf_op jit(solution)/shard_map/ppermute | solution.py:688
  8.5 0.0 copy-done.17
  8.6 0.1 slice_reduce_fusion
  8.6 0.0 copy-done
  8.6 0.0 copy-done.8
  8.6 0.0 copy-start.1
  8.7 1.3 %copy-done.1 = f32[1,72,32,128]{3,2,1,0:T(8,128)S(1)} copy-done((f32[1,72,32,128]{3,2,1,0:T(8,128)S(1)}, f32[1,72,32,128]{3,2,1,0:T(8,128)}, u32[]{:S(2)}) %copy-start.1) | copy-done | bytes 1179672
  9.9 0.0 copy-start.6
  9.9 0.8 copy-done.6
  10.8 0.0 copy-start.9
  10.8 0.5 pack_columns.1
  11.3 0.0 copy-done.16
  11.3 0.0 copy-start.4
  11.3 0.0 copy-start.12
  11.3 0.0 copy-start.13
  11.3 0.0 copy-start.14
  11.3 0.1 fusion.1
  11.5 0.0 collective-permute-done.above
  11.5 3.2 %collective-permute-done.1.below = bf16[704,128]{1,0:T(8,128)(2,1)S(1)} collective-permute-done((bf16[704,128]{1,0:T(8,128)(2,1)}, bf16[704,128]{1,0:T(8,128)(2,1)S(1)}, u32[]{:S(2)}, u32[]{:S(2)}) %collective-permute-start.1) | collective-permute-done | bytes 180256 | tf_op jit(solution)/shard_map/ppermute | solution.py:688
  14.7 0.2 finish_columns.1
  14.9 3.2 %collective-permute-start.2 = (bf16[176,128]{1,0:T(8,128)(2,1)S(1)}, bf16[176,128]{1,0:T(8,128)(2,1)S(1)}, u32[]{:S(2)}, u32[]{:S(2)}) collective-permute-start(bf16[176,128]{1,0:T(8,128)(2,1)S(1)} %get-tuple-element.28), channel_id=1, source_target_pairs={{0,4},{4,8},{8,12},{12,16},{16,20},{20,24},{24,28},{28,32},{32,36}... | collective-permute-start | bytes 135176 | tf_op jit(solution)/shard_map/ppermute | solution.py:688
  18.1 1.3 %collective-permute-start.3 = (bf16[176,128]{1,0:T(8,128)(2,1)S(1)}, bf16[176,128]{1,0:T(8,128)(2,1)S(1)}, u32[]{:S(2)}, u32[]{:S(2)}) collective-permute-start(bf16[176,128]{1,0:T(8,128)(2,1)S(1)} %get-tuple-element.29), channel_id=1, source_target_pairs={{4,0},{8,4},{12,8},{16,12},{20,16},{24,20},{28,24},{32,28},{36,32}... | collective-permute-start | bytes 135176 | tf_op jit(solution)/shard_map/ppermute | solution.py:688
  19.4 0.0 collective-permute-done.2.halo_l
  19.4 3.5 %collective-permute-done.3.halo_r = bf16[176,128]{1,0:T(8,128)(2,1)S(1)} collective-permute-done((bf16[176,128]{1,0:T(8,128)(2,1)S(1)}, bf16[176,128]{1,0:T(8,128)(2,1)S(1)}, u32[]{:S(2)}, u32[]{:S(2)}) %collective-permute-start.3) | collective-permute-done | bytes 45088 | tf_op jit(solution)/shard_map/ppermute | solution.py:688
  22.9 0.0 copy-done.9
  22.9 1.4 %assemble.1 = (bf16[32,32,128]{2,1,0:T(8,128)(2,1)S(1)}, bf16[32,16,128]{2,1,0:T(8,128)(2,1)S(1)}, bf16[2,16,128]{2,1,0:T(8,128)(2,1)S(1)}) custom-call(s32[1]{0:T(128)} %bitcast.comp, f32[80]{0:T(128)S(1)} %copy-done.9, f32[2560,128]{1,0:T(8,128)S(1)} %get-tuple-element.30.turned, f32[128,128]{1,0:T(8,128)S(1)} %copy-done.6, ...), custom_call_target="tpu_custom_call" | custom-call | tf_op jit(solution)/shard_map/assemble/pallas_call | solution.py:755
  24.3 1.3 %collective-permute-start.4 = (bf16[32,16,128]{2,1,0:T(8,128)(2,1)S(1)}, bf16[32,16,128]{2,1,0:T(8,128)(2,1)S(1)}, u32[]{:S(2)}, u32[]{:S(2)}) collective-permute-start(bf16[32,16,128]{2,1,0:T(8,128)(2,1)S(1)} %get-tuple-element.32), channel_id=1, source_target_pairs={{0,128},{1,129},{2,130},{3,131},{4,132},{5,133},{6,134},{7,135},{8... | collective-permute-start | bytes 393224 | tf_op jit(solution)/shard_map/ppermute | solution.py:688
  25.6 5.3 %collective-permute-done.4.arrived = bf16[32,16,128]{2,1,0:T(8,128)(2,1)S(1)} collective-permute-done((bf16[32,16,128]{2,1,0:T(8,128)(2,1)S(1)}, bf16[32,16,128]{2,1,0:T(8,128)(2,1)S(1)}, u32[]{:S(2)}, u32[]{:S(2)}) %collective-permute-start.4) | collective-permute-done | bytes 131104 | tf_op jit(solution)/shard_map/ppermute | solution.py:688
  31.0 0.0 copy-done.4
  31.0 0.0 copy-done.12
  31.0 0.0 copy-done.13
  31.0 0.0 copy-done.14
  31.0 2.2 %tile_products.1 = bf16[288,16,128]{2,1,0:T(8,128)(2,1)S(1)} custom-call(s32[1]{0:T(128)} %bitcast.comp, s32[1,64]{1,0:T(1,128)S(1)} %copy-done.12, s32[1,64]{1,0:T(1,128)S(1)} %bitcast.27, s32[1,64]{1,0:T(1,128)S(1)} %copy-done.14, bf16[32,32,128]{2,1,0:T(8,128)(2,1)S(1)} %get-tuple-element.31.own, bf16[32,16,128]{2,1,0:T(8,128)(2,1)S(1)} %collective-permute-done.4.arrived, ...), custom_call_target="tpu_custom_call" | custom-call | tf_op jit(solution)/shard_map/tile_products/pallas_call | solution.py:772
  33.2 0.0 copy-start.3
  33.2 1.0 %copy-done.3 = bf16[288,16,128]{2,1,0:T(8,128)(2,1)} copy-done((bf16[288,16,128]{2,1,0:T(8,128)(2,1)}, bf16[288,16,128]{2,1,0:T(8,128)(2,1)S(1)}, u32[]{:S(2)}) %copy-start.3) | copy-done | bytes 1179672
  34.2 0.0 copy-start.2
  34.2 0.0 copy-start.7
  34.2 13.2 %all-to-all-start = ((bf16[32,9,16,128]{3,2,1,0:T(8,128)(2,1)}), bf16[32,9,16,128]{3,2,1,0:T(8,128)(2,1)}, u32[]{:S(2)}, u32[]{:S(2)}) async-start(bf16[32,9,16,128]{3,2,1,0:T(8,128)(2,1)} %bitcast.24), calls=%async_computation | async-start | bytes 2359296 | tf_op jit(solution)/shard_map/all_to_all | solution.py:786
  47.4 0.1 copy.20
  47.5 0.0 copy-done.2
  47.5 0.0 copy-done.7
  47.5 0.0 copy-start.10
  47.5 0.0 copy-start.11
  47.6 15.1 %advect_all.1 = (f32[2560,128]{1,0:T(8,128)S(1)}, f32[2304,128]{1,0:T(8,128)}) custom-call(s32[1]{0:T(128)} %bitcast.comp, f32[80]{0:T(128)S(1)} %copy-done.9, f32[2304,128]{1,0:T(8,128)S(1)} %bitcast.23, f32[2560,128]{1,0:T(8,128)S(1)} %bitcast.20, f32[32,128]{1,0:T(8,128)S(1)} %copy-done.8, f32[128,128]{1,0:T(8,128)S(1)} %copy-done.7, ...), custom_call_target="tpu_custom_call" | custom-call | tf_op jit(solution)/shard_map/advect_all/pallas_call | solution.py:790
  62.6 0.0 copy-start.5
  62.6 1.1 %copy-done.5 = f32[2560,128]{1,0:T(8,128)} copy-done((f32[2560,128]{1,0:T(8,128)}, f32[2560,128]{1,0:T(8,128)S(1)}, u32[]{:S(2)}) %copy-start.5) | copy-done | bytes 1310744
  63.7 13.5 %all-to-all-done = bf16[32,9,16,128]{3,2,1,0:T(8,128)(2,1)} async-done(((bf16[32,9,16,128]{3,2,1,0:T(8,128)(2,1)}), bf16[32,9,16,128]{3,2,1,0:T(8,128)(2,1)}, u32[]{:S(2)}, u32[]{:S(2)}) %all-to-all-start) | async-done | bytes 1179680 | tf_op jit(solution)/shard_map/all_to_all | solution.py:786
  77.2 1.0 %slice.8 = bf16[32,2,16,128]{3,2,1,0:T(8,128)(2,1)S(1)} slice(bf16[32,9,16,128]{3,2,1,0:T(8,128)(2,1)} %bitcast.12), slice={[0:32], [0:2], [0:16], [0:128]} | slice | bytes 524288 | tf_op jit(solution)/shard_map/slice | solution.py:803
  78.2 0.0 copy-start.15
  78.2 3.9 %collective-permute-start.5 = (bf16[64,16,128]{2,1,0:T(8,128)(2,1)S(1)}, bf16[64,16,128]{2,1,0:T(8,128)(2,1)S(1)}, u32[]{:S(2)}, u32[]{:S(2)}) collective-permute-start(bf16[64,16,128]{2,1,0:T(8,128)(2,1)S(1)} %bitcast.29), channel_id=1, source_target_pairs={{128,0},{129,1},{130,2},{131,3},{132,4},{133,5},{134,6},{135,7},{1... | collective-permute-start | bytes 786440 | tf_op jit(solution)/shard_map/ppermute | solution.py:688
  82.1 0.0 copy-done.10
  82.1 0.0 copy-done.11
  82.1 6.2 %select_or_force.1 = (f32[128,128]{1,0:T(8,128)S(1)}, f32[2560,128]{1,0:T(8,128)}) custom-call(s32[1]{0:T(128)} %bitcast.comp, s32[1,64]{1,0:T(1,128)S(1)} %copy-done.10, s32[1,64]{1,0:T(1,128)S(1)} %copy-done.11, bf16[288,16,128]{2,1,0:T(8,128)(2,1)} %bitcast.10.received_ref, f32[2560,128]{1,0:T(8,128)} %copy-done.5, f32[160,16]{1,0:T(8,128)S(1)} %bitcast.26), custom_call_target="tpu_custom_call" | custom-call | tf_op jit(solution)/shard_map/select_or_force/pallas_call | solution.py:805
  88.3 0.0 collective-permute-done.5.other
  88.3 0.0 copy-done.15
  88.3 1.3 %finish.1 = f32[64,128]{1,0:T(8,128)} custom-call(s32[1]{0:T(128)} %bitcast.comp, s32[1,64]{1,0:T(1,128)S(1)} %copy-done.10, s32[1,64]{1,0:T(1,128)S(1)} %copy-done.11, s32[1,64]{1,0:T(1,128)S(1)} %copy-done.15, bf16[64,128,128]{2,1,0:T(8,128)(2,1)} %bitcast.28, f32[128,128]{1,0:T(8,128)S(1)} %get-tuple-element.41.mine, ...), custom_call_target="tpu_custom_call" | custom-call | tf_op jit(solution)/shard_map/finish/pallas_call | solution.py:811
  (3 shorter events, 0.0 us)
Async XLA Ops:
  0.6 7.9 %copy-start.17 = (f32[2,80,16]{1,2,0:T(8,128)S(1)}, f32[2,80,16]{1,2,0:T(8,128)}, u32[]{:S(2)}) copy-start(f32[2,80,16]{1,2,0:T(8,128)} %param.27) | copy-start | bytes 30724
  0.6 8.0 %copy-start = (f32[1,2,80,16,128]{4,3,2,1,0:T(8,128)S(1)}, f32[1,2,80,16,128]{4,3,2,1,0:T(8,128)}, u32[]{:S(2)}) copy-start(f32[1,2,80,16,128]{4,3,2,1,0:T(8,128)} %param.23) | copy-start | bytes 3932164
  0.7 8.0 %copy-start.8 = (f32[32,128]{1,0:T(8,128)S(1)}, f32[32,128]{1,0:T(8,128)}, u32[]{:S(2)}) copy-start(f32[32,128]{1,0:T(8,128)} %mass.3) | copy-start | bytes 49156
  3.3 8.0 %copy-start.16 = (f32[16,72]{1,0:T(8,128)S(1)}, f32[16,72]{1,0:T(8,128)}, u32[]{:S(2)}) copy-start(f32[16,72]{1,0:T(8,128)} %param.18) | copy-start | bytes 13828
  3.3 8.2 %collective-permute-start = (bf16[704,128]{1,0:T(8,128)(2,1)}, bf16[704,128]{1,0:T(8,128)(2,1)S(1)}, u32[]{:S(2)}, u32[]{:S(2)}) collective-permute-start(bf16[704,128]{1,0:T(8,128)(2,1)} %get-tuple-element.24), channel_id=1, source_target_pairs={{0,1},{1,2},{2,3},{4,5},{5,6},{6,7},{8,9},{9,10},{10,11},{12,13},{... | collective-permute-start | bytes 540680 | tf_op jit(solution)/shard_map/ppermute | solution.py:688
  7.2 7.5 %collective-permute-start.1 = (bf16[704,128]{1,0:T(8,128)(2,1)}, bf16[704,128]{1,0:T(8,128)(2,1)S(1)}, u32[]{:S(2)}, u32[]{:S(2)}) collective-permute-start(bf16[704,128]{1,0:T(8,128)(2,1)} %get-tuple-element.25), channel_id=1, source_target_pairs={{1,0},{2,1},{3,2},{5,4},{6,5},{7,6},{9,8},{10,9},{11,10},{13,12},{... | collective-permute-start | bytes 540680 | tf_op jit(solution)/shard_map/ppermute | solution.py:688
  8.6 1.3 %copy-start.1 = (f32[1,72,32,128]{3,2,1,0:T(8,128)S(1)}, f32[1,72,32,128]{3,2,1,0:T(8,128)}, u32[]{:S(2)}) copy-start(f32[1,72,32,128]{3,2,1,0:T(8,128)} %param.16) | copy-start | bytes 3538948
  9.9 0.8 copy-start.6
  10.8 12.1 %copy-start.9 = (f32[80]{0:T(128)S(1)}, f32[80]{0:T(128)}, u32[]{:S(2)}) copy-start(f32[80]{0:T(128)} %lev_speed.3) | copy-start | bytes 964
  11.3 19.7 %copy-start.4 = (bf16[1,64,128,128]{3,2,1,0:T(8,128)(2,1)S(1)}, bf16[1,64,128,128]{3,2,1,0:T(8,128)(2,1)}, u32[]{:S(2)}) copy-start(bf16[1,64,128,128]{3,2,1,0:T(8,128)(2,1)} %param.22) | copy-start | bytes 6291460
  11.3 19.7 %copy-start.12 = (s32[1,64]{1,0:T(1,128)S(1)}, s32[1,64]{1,0:T(1,128)}, u32[]{:S(2)}) copy-start(s32[1,64]{1,0:T(1,128)} %src.1) | copy-start | bytes 772
  11.3 19.7 %copy-start.13 = (s32[1,64,1]{1,2,0:T(1,128)S(1)}, s32[1,64,1]{1,2,0:T(1,128)}, u32[]{:S(2)}) copy-start(s32[1,64,1]{1,2,0:T(1,128)} %param.19) | copy-start | bytes 772
  11.3 19.6 %copy-start.14 = (s32[1,64]{1,0:T(1,128)S(1)}, s32[1,64]{1,0:T(1,128)}, u32[]{:S(2)}) copy-start(s32[1,64]{1,0:T(1,128)} %dst.1) | copy-start | bytes 772
  14.9 4.5 %collective-permute-start.2 = (bf16[176,128]{1,0:T(8,128)(2,1)S(1)}, bf16[176,128]{1,0:T(8,128)(2,1)S(1)}, u32[]{:S(2)}, u32[]{:S(2)}) collective-permute-start(bf16[176,128]{1,0:T(8,128)(2,1)S(1)} %get-tuple-element.28), channel_id=1, source_target_pairs={{0,4},{4,8},{8,12},{12,16},{16,20},{20,24},{24,28},{28,32},{32,36}... | collective-permute-start | bytes 135176 | tf_op jit(solution)/shard_map/ppermute | solution.py:688
  18.1 4.8 %collective-permute-start.3 = (bf16[176,128]{1,0:T(8,128)(2,1)S(1)}, bf16[176,128]{1,0:T(8,128)(2,1)S(1)}, u32[]{:S(2)}, u32[]{:S(2)}) collective-permute-start(bf16[176,128]{1,0:T(8,128)(2,1)S(1)} %get-tuple-element.29), channel_id=1, source_target_pairs={{4,0},{8,4},{12,8},{16,12},{20,16},{24,20},{28,24},{32,28},{36,32}... | collective-permute-start | bytes 135176 | tf_op jit(solution)/shard_map/ppermute | solution.py:688
  24.3 6.6 %collective-permute-start.4 = (bf16[32,16,128]{2,1,0:T(8,128)(2,1)S(1)}, bf16[32,16,128]{2,1,0:T(8,128)(2,1)S(1)}, u32[]{:S(2)}, u32[]{:S(2)}) collective-permute-start(bf16[32,16,128]{2,1,0:T(8,128)(2,1)S(1)} %get-tuple-element.32), channel_id=1, source_target_pairs={{0,128},{1,129},{2,130},{3,131},{4,132},{5,133},{6,134},{7,135},{8... | collective-permute-start | bytes 393224 | tf_op jit(solution)/shard_map/ppermute | solution.py:688
  33.2 1.0 %copy-start.3 = (bf16[288,16,128]{2,1,0:T(8,128)(2,1)}, bf16[288,16,128]{2,1,0:T(8,128)(2,1)S(1)}, u32[]{:S(2)}) copy-start(bf16[288,16,128]{2,1,0:T(8,128)(2,1)S(1)} %tile_products.1) | copy-start | bytes 3538948
  34.2 13.4 %copy-start.2 = (f32[1,72,32,128]{3,2,1,0:T(8,128)S(1)}, f32[1,72,32,128]{3,2,1,0:T(8,128)}, u32[]{:S(2)}) copy-start(f32[1,72,32,128]{3,2,1,0:T(8,128)} %param.16) | copy-start | bytes 3538948
  34.2 13.4 %copy-start.7 = (f32[128,128]{1,0:T(8,128)S(1)}, f32[128,128]{1,0:T(8,128)}, u32[]{:S(2)}) copy-start(f32[128,128]{1,0:T(8,128)} %get-tuple-element.23.rate8) | copy-start | bytes 196612
  34.2 43.1 %all-to-all-start = ((bf16[32,9,16,128]{3,2,1,0:T(8,128)(2,1)}), bf16[32,9,16,128]{3,2,1,0:T(8,128)(2,1)}, u32[]{:S(2)}, u32[]{:S(2)}) async-start(bf16[32,9,16,128]{3,2,1,0:T(8,128)(2,1)} %bitcast.24), calls=%async_computation | async-start | bytes 2359296 | tf_op jit(solution)/shard_map/all_to_all | solution.py:786
  47.5 34.6 %copy-start.10 = (s32[1,64]{1,0:T(1,128)S(1)}, s32[1,64]{1,0:T(1,128)}, u32[]{:S(2)}) copy-start(s32[1,64]{1,0:T(1,128)} %back_owner.3) | copy-start | bytes 772
  47.5 34.6 %copy-start.11 = (s32[1,64]{1,0:T(1,128)S(1)}, s32[1,64]{1,0:T(1,128)}, u32[]{:S(2)}) copy-start(s32[1,64]{1,0:T(1,128)} %back_src.3) | copy-start | bytes 772
  62.6 1.1 %copy-start.5 = (f32[2560,128]{1,0:T(8,128)}, f32[2560,128]{1,0:T(8,128)S(1)}, u32[]{:S(2)}) copy-start(f32[2560,128]{1,0:T(8,128)S(1)} %get-tuple-element.39.advected_ref) | copy-start | bytes 3932164
  78.2 10.1 %copy-start.15 = (s32[1,64]{1,0:T(1,128)S(1)}, s32[1,64]{1,0:T(1,128)}, u32[]{:S(2)}) copy-start(s32[1,64]{1,0:T(1,128)} %back_dst.1) | copy-start | bytes 772
  78.2 10.1 %collective-permute-start.5 = (bf16[64,16,128]{2,1,0:T(8,128)(2,1)S(1)}, bf16[64,16,128]{2,1,0:T(8,128)(2,1)S(1)}, u32[]{:S(2)}, u32[]{:S(2)}) collective-permute-start(bf16[64,16,128]{2,1,0:T(8,128)(2,1)S(1)} %bitcast.29), channel_id=1, source_target_pairs={{128,0},{129,1},{130,2},{131,3},{132,4},{133,5},{134,6},{135,7},{1... | collective-permute-start | bytes 786440 | tf_op jit(solution)/shard_map/ppermute | solution.py:688

commit v4 on v2

--- a/solution.py
+++ b/solution.py
@@ -569,15 +569,26 @@
 
 def finish(
     comp, back_owner, back_src, back_dst,
-    advected, received, profile, weights, mine, other,
-    ocean, surface, table, parts, acc,
+    weights_ref, advected, received, profile, mine, other,
+    ocean, surface, weights, sem, table, parts, acc,
 ):
     band = received.shape[0] // TILES_PER_PEER
     tiles = weights.shape[0]
 
     @pl.when(comp[0] == 0)
     def _():
+        half = tiles // 2
+        copies = [
+            pltpu.make_async_copy(
+                weights_ref.at[pl.ds(half * n, half)], weights.at[pl.ds(half * n, half)],
+                sem.at[n],
+            )
+            for n in range(2)
+        ]
+        for copy in copies:
+            copy.start()
         want = wanted(back_owner, back_src)
+        ocean[...] = jnp.zeros(ocean.shape, F32)
         sums = [mine[64 * v : 64 * v + 64, :] for v in range(2)]
         for c in range(band // 8):
             row = (lanes(64) + c * W).astype(F32)
@@ -592,6 +603,8 @@
                     table[pl.ds(64 * p + at, 8, stride=8), :] = part[8 * p : 8 * p + 8]
         acc[...] = jnp.zeros(acc.shape, F32)
         for t in range(tiles):
+            if t % half == 0:
+                copies[t // half].wait()
             parts[8 * t : 8 * t + 8, :] = lax.dot_general(
                 table[8 * t : 8 * t + 8, :].astype(BF16),
                 weights[t],
@@ -607,7 +620,6 @@
                     acc[pl.ds(64 * p + v, 8, stride=8), :]
                     + acc[pl.ds(64 * p + 2 + v, 8, stride=8), :]
                 )
-        ocean[...] = jnp.zeros(ocean.shape, F32)
 
     @pl.when(comp[0] == 1)
     def _():
@@ -760,11 +772,13 @@
     mine, = call(surface_select, [shape(128, W)], 3, 0, 1, [])(
         comp, back_owner, back_src_blk, received
     )
-    ocean, surface = call(finish, [shape(2560, W), shape(64, W)], 4, 0, 6, [
+    return_weights = pltpu.with_memory_space_constraint(return_remap_weights[0], pltpu.HBM)
+    ocean, surface = call(finish, [shape(2560, W), shape(64, W)], 4, 1, 5, [
+        pltpu.VMEM(return_remap_weights.shape[1:], BF16), dma((2,)),
         pltpu.VMEM((512, W), F32), pltpu.VMEM((512, W), F32), pltpu.VMEM((256, W), F32),
     ])(
         comp, back_owner, back_src_blk, back_dst_blk,
-        advected, received, levels, return_remap_weights[0], mine, other,
+        return_weights, advected, received, levels, mine, other,
     )
     return (
         dss.reshape(1, 72, 32, W),

time: 88.5 us -> 86.9 us (0.982)
  local copies, waits for them, and re-layouts: 7.29 us -> 5.71 us
    unnamed x41 -> x39, local copies, waits for them, and re-layouts: 7.19 us -> 5.6 us
  transfers between devices with their start and end apart: 7 -> 7, of which waited for: 5 -> 5; matrix products, arithmetic and copies ran while one was open for 0% -> 0% of each run, Pallas kernels for 18% -> 19%
where the time goes in v4:
time: 86.9 us; the launch traced here: 86.4 us
  starting transfers between devices  28.2 us (32%)
  Pallas kernels  26.5 us (30%)
  waiting for transfers between devices  24.9 us (29%)
  local copies, waits for them, and re-layouts  5.71 us (7%)
  between operations  0.92 us (1%)
    pallas_call x1, Pallas kernels, shards(): call(advect_all, [shape(16 * 160, W), shape(72 * 32, W)], 2, 0, 9, [point...  15.1 us
    ppermute x6, starting transfers between devices, shifted(): return lax.ppermute(array, axis, pairs)  15 us
    all_to_all x1, starting transfers between devices, shards(): lax.all_to_all(send.reshape(band, TILES_PER_PEER, 16, W), 'gx', 0, 0, til...  13.1 us
    ppermute x6, waiting for transfers between devices, shifted(): return lax.ppermute(array, axis, pairs)  12.6 us
    all_to_all x1, waiting for transfers between devices, shards(): lax.all_to_all(send.reshape(band, TILES_PER_PEER, 16, W), 'gx', 0, 0, til...  12.3 us
    unnamed x39, local copies, waits for them, and re-layouts  5.6 us
    pallas_call x1, Pallas kernels, shards(): call(finish, [shape(2560, W), shape(64, W)], 4, 1, 5, [pltpu.VMEM(return_...  4.19 us
    pallas_call x1, Pallas kernels, shards(): call(pack_rows, [shape(4 * PR, W, dtype=BF16), shape(4 * PR, W, dtype=BF1...  2.48 us
  transfers between devices with their start and end apart: 7, of which 5 were waited for; matrix products, arithmetic and copies ran while one was open for 0% of the time, Pallas kernels for 19%

profile of v4, /device:TPU:1, one launch (start us, length us, event | category | flops | bytes accessed | tf_op | source)
XLA Modules:
  0.0 86.4 jit_solution(9372980907958717974)
XLA Ops:
  0.6 0.0 copy-start.18
  0.6 0.0 copy-start
  0.7 0.0 copy-start.9
  0.7 2.5 %pack_rows.1 = (bf16[704,128]{1,0:T(8,128)(2,1)}, bf16[704,128]{1,0:T(8,128)(2,1)}, f32[128,128]{1,0:T(8,128)}) custom-call(s32[1]{0:T(128)} %bitcast.comp, f32[2304,128]{1,0:T(8,128)} %bitcast.23, f32[2560,128]{1,0:T(8,128)} %bitcast.20, f32[32,128]{1,0:T(8,128)} %mass.3, s32[96,128]{1,0:T(8,128)} %bitcast.32, f32[96,128]{1,0:T(8,128)} %bitcast.33), custom_call_target="tpu_custom_call" | custom-call | tf_op jit(solution)/shard_map/pack_rows/pallas_call | solution.py:689
  3.2 0.0 copy-start.17
  3.2 4.0 %collective-permute-start = (bf16[704,128]{1,0:T(8,128)(2,1)}, bf16[704,128]{1,0:T(8,128)(2,1)S(1)}, u32[]{:S(2)}, u32[]{:S(2)}) collective-permute-start(bf16[704,128]{1,0:T(8,128)(2,1)} %get-tuple-element.24), channel_id=1, source_target_pairs={{0,1},{1,2},{2,3},{4,5},{5,6},{6,7},{8,9},{9,10},{10,11},{12,13},{... | collective-permute-start | bytes 540680 | tf_op jit(solution)/shard_map/ppermute | solution.py:655
  7.1 1.3 %collective-permute-start.1 = (bf16[704,128]{1,0:T(8,128)(2,1)}, bf16[704,128]{1,0:T(8,128)(2,1)S(1)}, u32[]{:S(2)}, u32[]{:S(2)}) collective-permute-start(bf16[704,128]{1,0:T(8,128)(2,1)} %get-tuple-element.25), channel_id=1, source_target_pairs={{1,0},{2,1},{3,2},{5,4},{6,5},{7,6},{9,8},{10,9},{11,10},{13,12},{... | collective-permute-start | bytes 540680 | tf_op jit(solution)/shard_map/ppermute | solution.py:655
  8.4 0.0 copy-done.18
  8.4 0.1 slice_reduce_fusion
  8.5 0.0 copy-done
  8.5 0.0 copy-done.9
  8.5 0.0 copy-start.1
  8.5 1.3 %copy-done.1 = f32[1,72,32,128]{3,2,1,0:T(8,128)S(1)} copy-done((f32[1,72,32,128]{3,2,1,0:T(8,128)S(1)}, f32[1,72,32,128]{3,2,1,0:T(8,128)}, u32[]{:S(2)}) %copy-start.1) | copy-done | bytes 1179672
  9.8 0.0 copy-start.7
  9.8 0.8 copy-done.7
  10.6 0.0 copy-start.12
  10.6 0.5 pack_columns.1
  11.2 0.0 copy-done.17
  11.2 0.0 copy-start.4
  11.2 0.0 copy-start.13
  11.2 0.0 copy-start.14
  11.2 0.0 copy-start.15
  11.2 0.1 fusion.1
  11.4 0.0 collective-permute-done.above
  11.4 3.2 %collective-permute-done.1.below = bf16[704,128]{1,0:T(8,128)(2,1)S(1)} collective-permute-done((bf16[704,128]{1,0:T(8,128)(2,1)}, bf16[704,128]{1,0:T(8,128)(2,1)S(1)}, u32[]{:S(2)}, u32[]{:S(2)}) %collective-permute-start.1) | collective-permute-done | bytes 180256 | tf_op jit(solution)/shard_map/ppermute | solution.py:655
  14.6 0.2 finish_columns.1
  14.8 3.2 %collective-permute-start.2 = (bf16[176,128]{1,0:T(8,128)(2,1)S(1)}, bf16[176,128]{1,0:T(8,128)(2,1)S(1)}, u32[]{:S(2)}, u32[]{:S(2)}) collective-permute-start(bf16[176,128]{1,0:T(8,128)(2,1)S(1)} %get-tuple-element.28), channel_id=1, source_target_pairs={{0,4},{4,8},{8,12},{12,16},{16,20},{20,24},{24,28},{28,32},{32,36}... | collective-permute-start | bytes 135176 | tf_op jit(solution)/shard_map/ppermute | solution.py:655
  18.0 1.3 %collective-permute-start.3 = (bf16[176,128]{1,0:T(8,128)(2,1)S(1)}, bf16[176,128]{1,0:T(8,128)(2,1)S(1)}, u32[]{:S(2)}, u32[]{:S(2)}) collective-permute-start(bf16[176,128]{1,0:T(8,128)(2,1)S(1)} %get-tuple-element.29), channel_id=1, source_target_pairs={{4,0},{8,4},{12,8},{16,12},{20,16},{24,20},{28,24},{32,28},{36,32}... | collective-permute-start | bytes 135176 | tf_op jit(solution)/shard_map/ppermute | solution.py:655
  19.3 0.0 collective-permute-done.2.halo_l
  19.3 3.5 %collective-permute-done.3.halo_r = bf16[176,128]{1,0:T(8,128)(2,1)S(1)} collective-permute-done((bf16[176,128]{1,0:T(8,128)(2,1)S(1)}, bf16[176,128]{1,0:T(8,128)(2,1)S(1)}, u32[]{:S(2)}, u32[]{:S(2)}) %collective-permute-start.3) | collective-permute-done | bytes 45088 | tf_op jit(solution)/shard_map/ppermute | solution.py:655
  22.8 0.0 copy-done.12
  22.8 1.4 %assemble.1 = (bf16[32,32,128]{2,1,0:T(8,128)(2,1)S(1)}, bf16[32,16,128]{2,1,0:T(8,128)(2,1)S(1)}, bf16[2,16,128]{2,1,0:T(8,128)(2,1)S(1)}) custom-call(s32[1]{0:T(128)} %bitcast.comp, f32[80]{0:T(128)S(1)} %copy-done.12, f32[2560,128]{1,0:T(8,128)S(1)} %get-tuple-element.30.turned, f32[128,128]{1,0:T(8,128)S(1)} %copy-done.7, ...), custom_call_target="tpu_custom_call" | custom-call | tf_op jit(solution)/shard_map/assemble/pallas_call | solution.py:722
  24.2 1.3 %collective-permute-start.4 = (bf16[32,16,128]{2,1,0:T(8,128)(2,1)S(1)}, bf16[32,16,128]{2,1,0:T(8,128)(2,1)S(1)}, u32[]{:S(2)}, u32[]{:S(2)}) collective-permute-start(bf16[32,16,128]{2,1,0:T(8,128)(2,1)S(1)} %get-tuple-element.32), channel_id=1, source_target_pairs={{0,128},{1,129},{2,130},{3,131},{4,132},{5,133},{6,134},{7,135},{8... | collective-permute-start | bytes 393224 | tf_op jit(solution)/shard_map/ppermute | solution.py:655
  25.5 5.3 %collective-permute-done.4.arrived = bf16[32,16,128]{2,1,0:T(8,128)(2,1)S(1)} collective-permute-done((bf16[32,16,128]{2,1,0:T(8,128)(2,1)S(1)}, bf16[32,16,128]{2,1,0:T(8,128)(2,1)S(1)}, u32[]{:S(2)}, u32[]{:S(2)}) %collective-permute-start.4) | collective-permute-done | bytes 131104 | tf_op jit(solution)/shard_map/ppermute | solution.py:655
  30.8 0.0 copy-done.4
  30.8 0.0 copy-done.13
  30.8 0.0 copy-done.14
  30.8 0.0 copy-done.15
  30.9 2.2 %tile_products.1 = bf16[288,16,128]{2,1,0:T(8,128)(2,1)S(1)} custom-call(s32[1]{0:T(128)} %bitcast.comp, s32[1,64]{1,0:T(1,128)S(1)} %copy-done.13, s32[1,64]{1,0:T(1,128)S(1)} %bitcast.29, s32[1,64]{1,0:T(1,128)S(1)} %copy-done.15, bf16[32,32,128]{2,1,0:T(8,128)(2,1)S(1)} %get-tuple-element.31.own, bf16[32,16,128]{2,1,0:T(8,128)(2,1)S(1)} %collective-permute-done.4.arrived, ...), custom_call_target="tpu_custom_call" | custom-call | tf_op jit(solution)/shard_map/tile_products/pallas_call | solution.py:739
  33.0 0.0 copy-start.3
  33.0 1.0 %copy-done.3 = bf16[288,16,128]{2,1,0:T(8,128)(2,1)} copy-done((bf16[288,16,128]{2,1,0:T(8,128)(2,1)}, bf16[288,16,128]{2,1,0:T(8,128)(2,1)S(1)}, u32[]{:S(2)}) %copy-start.3) | copy-done | bytes 1179672
  34.1 0.0 copy-start.8
  34.1 13.1 %all-to-all-start = ((bf16[32,9,16,128]{3,2,1,0:T(8,128)(2,1)}), bf16[32,9,16,128]{3,2,1,0:T(8,128)(2,1)S(1)}, u32[]{:S(2)}, u32[]{:S(2)}) async-start(bf16[32,9,16,128]{3,2,1,0:T(8,128)(2,1)} %bitcast.26), calls=%async_computation | async-start | bytes 2359296 | tf_op jit(solution)/shard_map/all_to_all | solution.py:753
  47.2 0.1 copy.20
  47.3 0.0 copy-done.8
  47.3 0.0 copy-start.2
  47.3 1.3 %copy-done.2 = f32[1,72,32,128]{3,2,1,0:T(8,128)S(1)} copy-done((f32[1,72,32,128]{3,2,1,0:T(8,128)S(1)}, f32[1,72,32,128]{3,2,1,0:T(8,128)}, u32[]{:S(2)}) %copy-start.2) | copy-done | bytes 1179672
  48.6 0.0 copy-start.10
  48.6 0.0 copy-start.11
  48.6 15.1 %advect_all.1 = (f32[2560,128]{1,0:T(8,128)S(1)}, f32[2304,128]{1,0:T(8,128)}) custom-call(s32[1]{0:T(128)} %bitcast.comp, f32[80]{0:T(128)S(1)} %copy-done.12, f32[2304,128]{1,0:T(8,128)S(1)} %bitcast.25, f32[2560,128]{1,0:T(8,128)S(1)} %bitcast.22, f32[32,128]{1,0:T(8,128)S(1)} %copy-done.9, f32[128,128]{1,0:T(8,128)S(1)} %copy-done.8, ...), custom_call_target="tpu_custom_call" | custom-call | tf_op jit(solution)/shard_map/advect_all/pallas_call | solution.py:757
  63.6 0.0 copy-start.5
  63.6 1.1 %copy-done.5 = f32[2560,128]{1,0:T(8,128)} copy-done((f32[2560,128]{1,0:T(8,128)}, f32[2560,128]{1,0:T(8,128)S(1)}, u32[]{:S(2)}) %copy-start.5) | copy-done | bytes 1310744
  64.7 0.0 copy-start.16
  64.7 12.3 %all-to-all-done = bf16[32,9,16,128]{3,2,1,0:T(8,128)(2,1)S(1)} async-done(((bf16[32,9,16,128]{3,2,1,0:T(8,128)(2,1)}), bf16[32,9,16,128]{3,2,1,0:T(8,128)(2,1)S(1)}, u32[]{:S(2)}, u32[]{:S(2)}) %all-to-all-start) | async-done | bytes 1179680 | tf_op jit(solution)/shard_map/all_to_all | solution.py:753
  77.0 0.0 copy-start.6
  77.0 4.0 %collective-permute-start.5 = (bf16[64,16,128]{2,1,0:T(8,128)(2,1)S(1)}, bf16[64,16,128]{2,1,0:T(8,128)(2,1)S(1)}, u32[]{:S(2)}, u32[]{:S(2)}) collective-permute-start(bf16[64,16,128]{2,1,0:T(8,128)(2,1)S(1)} %bitcast.31), channel_id=1, source_target_pairs={{128,0},{129,1},{130,2},{131,3},{132,4},{133,5},{134,6},{135,7},{1... | collective-permute-start | bytes 786440 | tf_op jit(solution)/shard_map/ppermute | solution.py:655
  81.0 0.0 copy-done.10
  81.1 0.0 copy-done.11
  81.1 0.6 surface_select.1.mine
  81.6 0.6 collective-permute-done.5.other
  82.2 0.0 copy-done.16
  82.2 0.0 copy-done.6
  82.2 4.2 %finish.1 = (f32[2560,128]{1,0:T(8,128)}, f32[64,128]{1,0:T(8,128)}) custom-call(s32[1]{0:T(128)} %bitcast.comp, s32[1,64]{1,0:T(1,128)S(1)} %copy-done.10, s32[1,64]{1,0:T(1,128)S(1)} %copy-done.11, s32[1,64]{1,0:T(1,128)S(1)} %copy-done.16, bf16[64,128,128]{2,1,0:T(8,128)(2,1)} %bitcast.30, f32[2560,128]{1,0:T(8,128)S(1)} %copy-done.6, ...), custom_call_target="tpu_custom_call" | custom-call | tf_op jit(solution)/shard_map/finish/pallas_call | solution.py:776
  (4 shorter events, 0.1 us)
Async XLA Ops:
  0.6 7.8 %copy-start.18 = (f32[2,80,16]{1,2,0:T(8,128)S(1)}, f32[2,80,16]{1,2,0:T(8,128)}, u32[]{:S(2)}) copy-start(f32[2,80,16]{1,2,0:T(8,128)} %param.27) | copy-start | bytes 30724
  0.6 7.9 %copy-start = (f32[1,2,80,16,128]{4,3,2,1,0:T(8,128)S(1)}, f32[1,2,80,16,128]{4,3,2,1,0:T(8,128)}, u32[]{:S(2)}) copy-start(f32[1,2,80,16,128]{4,3,2,1,0:T(8,128)} %param.23) | copy-start | bytes 3932164
  0.7 7.9 %copy-start.9 = (f32[32,128]{1,0:T(8,128)S(1)}, f32[32,128]{1,0:T(8,128)}, u32[]{:S(2)}) copy-start(f32[32,128]{1,0:T(8,128)} %mass.3) | copy-start | bytes 49156
  3.2 8.0 %copy-start.17 = (f32[16,72]{1,0:T(8,128)S(1)}, f32[16,72]{1,0:T(8,128)}, u32[]{:S(2)}) copy-start(f32[16,72]{1,0:T(8,128)} %param.18) | copy-start | bytes 13828
  3.2 8.2 %collective-permute-start = (bf16[704,128]{1,0:T(8,128)(2,1)}, bf16[704,128]{1,0:T(8,128)(2,1)S(1)}, u32[]{:S(2)}, u32[]{:S(2)}) collective-permute-start(bf16[704,128]{1,0:T(8,128)(2,1)} %get-tuple-element.24), channel_id=1, source_target_pairs={{0,1},{1,2},{2,3},{4,5},{5,6},{6,7},{8,9},{9,10},{10,11},{12,13},{... | collective-permute-start | bytes 540680 | tf_op jit(solution)/shard_map/ppermute | solution.py:655
  7.1 7.5 %collective-permute-start.1 = (bf16[704,128]{1,0:T(8,128)(2,1)}, bf16[704,128]{1,0:T(8,128)(2,1)S(1)}, u32[]{:S(2)}, u32[]{:S(2)}) collective-permute-start(bf16[704,128]{1,0:T(8,128)(2,1)} %get-tuple-element.25), channel_id=1, source_target_pairs={{1,0},{2,1},{3,2},{5,4},{6,5},{7,6},{9,8},{10,9},{11,10},{13,12},{... | collective-permute-start | bytes 540680 | tf_op jit(solution)/shard_map/ppermute | solution.py:655
  8.5 1.3 %copy-start.1 = (f32[1,72,32,128]{3,2,1,0:T(8,128)S(1)}, f32[1,72,32,128]{3,2,1,0:T(8,128)}, u32[]{:S(2)}) copy-start(f32[1,72,32,128]{3,2,1,0:T(8,128)} %param.16) | copy-start | bytes 3538948
  9.8 0.8 copy-start.7
  10.6 12.1 %copy-start.12 = (f32[80]{0:T(128)S(1)}, f32[80]{0:T(128)}, u32[]{:S(2)}) copy-start(f32[80]{0:T(128)} %lev_speed.3) | copy-start | bytes 964
  11.2 19.7 %copy-start.4 = (bf16[1,64,128,128]{3,2,1,0:T(8,128)(2,1)S(1)}, bf16[1,64,128,128]{3,2,1,0:T(8,128)(2,1)}, u32[]{:S(2)}) copy-start(bf16[1,64,128,128]{3,2,1,0:T(8,128)(2,1)} %param.22) | copy-start | bytes 6291460
  11.2 19.7 %copy-start.13 = (s32[1,64]{1,0:T(1,128)S(1)}, s32[1,64]{1,0:T(1,128)}, u32[]{:S(2)}) copy-start(s32[1,64]{1,0:T(1,128)} %src.1) | copy-start | bytes 772
  11.2 19.7 %copy-start.14 = (s32[1,64,1]{1,2,0:T(1,128)S(1)}, s32[1,64,1]{1,2,0:T(1,128)}, u32[]{:S(2)}) copy-start(s32[1,64,1]{1,2,0:T(1,128)} %param.19) | copy-start | bytes 772
  11.2 19.6 %copy-start.15 = (s32[1,64]{1,0:T(1,128)S(1)}, s32[1,64]{1,0:T(1,128)}, u32[]{:S(2)}) copy-start(s32[1,64]{1,0:T(1,128)} %dst.1) | copy-start | bytes 772
  14.8 4.5 %collective-permute-start.2 = (bf16[176,128]{1,0:T(8,128)(2,1)S(1)}, bf16[176,128]{1,0:T(8,128)(2,1)S(1)}, u32[]{:S(2)}, u32[]{:S(2)}) collective-permute-start(bf16[176,128]{1,0:T(8,128)(2,1)S(1)} %get-tuple-element.28), channel_id=1, source_target_pairs={{0,4},{4,8},{8,12},{12,16},{16,20},{20,24},{24,28},{28,32},{32,36}... | collective-permute-start | bytes 135176 | tf_op jit(solution)/shard_map/ppermute | solution.py:655
  18.0 4.8 %collective-permute-start.3 = (bf16[176,128]{1,0:T(8,128)(2,1)S(1)}, bf16[176,128]{1,0:T(8,128)(2,1)S(1)}, u32[]{:S(2)}, u32[]{:S(2)}) collective-permute-start(bf16[176,128]{1,0:T(8,128)(2,1)S(1)} %get-tuple-element.29), channel_id=1, source_target_pairs={{4,0},{8,4},{12,8},{16,12},{20,16},{24,20},{28,24},{32,28},{36,32}... | collective-permute-start | bytes 135176 | tf_op jit(solution)/shard_map/ppermute | solution.py:655
  24.2 6.6 %collective-permute-start.4 = (bf16[32,16,128]{2,1,0:T(8,128)(2,1)S(1)}, bf16[32,16,128]{2,1,0:T(8,128)(2,1)S(1)}, u32[]{:S(2)}, u32[]{:S(2)}) collective-permute-start(bf16[32,16,128]{2,1,0:T(8,128)(2,1)S(1)} %get-tuple-element.32), channel_id=1, source_target_pairs={{0,128},{1,129},{2,130},{3,131},{4,132},{5,133},{6,134},{7,135},{8... | collective-permute-start | bytes 393224 | tf_op jit(solution)/shard_map/ppermute | solution.py:655
  33.0 1.0 %copy-start.3 = (bf16[288,16,128]{2,1,0:T(8,128)(2,1)}, bf16[288,16,128]{2,1,0:T(8,128)(2,1)S(1)}, u32[]{:S(2)}) copy-start(bf16[288,16,128]{2,1,0:T(8,128)(2,1)S(1)} %tile_products.1) | copy-start | bytes 3538948
  34.1 13.2 %copy-start.8 = (f32[128,128]{1,0:T(8,128)S(1)}, f32[128,128]{1,0:T(8,128)}, u32[]{:S(2)}) copy-start(f32[128,128]{1,0:T(8,128)} %get-tuple-element.23.rate8) | copy-start | bytes 196612
  34.1 43.0 %all-to-all-start = ((bf16[32,9,16,128]{3,2,1,0:T(8,128)(2,1)}), bf16[32,9,16,128]{3,2,1,0:T(8,128)(2,1)S(1)}, u32[]{:S(2)}, u32[]{:S(2)}) async-start(bf16[32,9,16,128]{3,2,1,0:T(8,128)(2,1)} %bitcast.26), calls=%async_computation | async-start | bytes 2359296 | tf_op jit(solution)/shard_map/all_to_all | solution.py:753
  47.3 1.3 %copy-start.2 = (f32[1,72,32,128]{3,2,1,0:T(8,128)S(1)}, f32[1,72,32,128]{3,2,1,0:T(8,128)}, u32[]{:S(2)}) copy-start(f32[1,72,32,128]{3,2,1,0:T(8,128)} %param.16) | copy-start | bytes 3538948
  48.6 32.5 %copy-start.10 = (s32[1,64]{1,0:T(1,128)S(1)}, s32[1,64]{1,0:T(1,128)}, u32[]{:S(2)}) copy-start(s32[1,64]{1,0:T(1,128)} %back_owner.3) | copy-start | bytes 772
  48.6 32.5 %copy-start.11 = (s32[1,64]{1,0:T(1,128)S(1)}, s32[1,64]{1,0:T(1,128)}, u32[]{:S(2)}) copy-start(s32[1,64]{1,0:T(1,128)} %back_src.3) | copy-start | bytes 772
  63.6 1.1 %copy-start.5 = (f32[2560,128]{1,0:T(8,128)}, f32[2560,128]{1,0:T(8,128)S(1)}, u32[]{:S(2)}) copy-start(f32[2560,128]{1,0:T(8,128)S(1)} %get-tuple-element.38.advected) | copy-start | bytes 3932164
  64.7 17.5 %copy-start.16 = (s32[1,64]{1,0:T(1,128)S(1)}, s32[1,64]{1,0:T(1,128)}, u32[]{:S(2)}) copy-start(s32[1,64]{1,0:T(1,128)} %back_dst.1) | copy-start | bytes 772
  77.0 5.2 %copy-start.6 = (f32[2560,128]{1,0:T(8,128)S(1)}, f32[2560,128]{1,0:T(8,128)}, u32[]{:S(2)}) copy-start(f32[2560,128]{1,0:T(8,128)} %copy-done.5) | copy-start | bytes 3932164
  77.0 5.1 %collective-permute-start.5 = (bf16[64,16,128]{2,1,0:T(8,128)(2,1)S(1)}, bf16[64,16,128]{2,1,0:T(8,128)(2,1)S(1)}, u32[]{:S(2)}, u32[]{:S(2)}) collective-permute-start(bf16[64,16,128]{2,1,0:T(8,128)(2,1)S(1)} %bitcast.31), channel_id=1, source_target_pairs={{128,0},{129,1},{130,2},{131,3},{132,4},{133,5},{134,6},{135,7},{1... | collective-permute-start | bytes 786440 | tf_op jit(solution)/shard_map/ppermute | solution.py:655

commit v5 on v4

--- a/solution.py
+++ b/solution.py
@@ -20,12 +20,16 @@
     return lax.broadcasted_iota(jnp.int32, (rows, W), 1)
 
 
+def in_hbm(array):
+    return pltpu.with_memory_space_constraint(array, pltpu.HBM)
+
+
 def split(value):
     hi = value.astype(BF16)
     return hi, (value - hi.astype(F32)).astype(BF16)
 
 
-def call(body, out_shape, n_smem, n_any, n_vmem, scratch, mebibytes=16):
+def call(body, out_shape, n_smem, n_any, n_vmem, scratch):
     specs = (
         [pl.BlockSpec(memory_space=pltpu.SMEM)] * n_smem
         + [pl.BlockSpec(memory_space=pl.ANY)] * n_any
@@ -37,7 +41,7 @@
         in_specs=specs,
         out_specs=[pl.BlockSpec(memory_space=pltpu.VMEM)] * len(out_shape),
         scratch_shapes=scratch,
-        compiler_params=pltpu.CompilerParams(vmem_limit_bytes=mebibytes * 1024 * 1024),
+        compiler_params=pltpu.CompilerParams(vmem_limit_bytes=16 * 1024 * 1024),
         name=body.__name__,
     )
 
@@ -694,8 +698,7 @@
             buf, pltpu.VMEM((32, W), F32), pltpu.VMEM((96, W), jnp.int32),
             pltpu.VMEM((96, W), F32), dma((3,)),
         ],
-        62,
-    )(comp, state, tracer, atm_mass, codes, rates)
+    )(comp, *(in_hbm(array) for array in (state, tracer, atm_mass, codes, rates)))
     below = shifted(up, "gy", -1)
     above = shifted(down, "gy", 1)
     raw_left, raw_right, turned = call(
@@ -772,13 +775,12 @@
     mine, = call(surface_select, [shape(128, W)], 3, 0, 1, [])(
         comp, back_owner, back_src_blk, received
     )
-    return_weights = pltpu.with_memory_space_constraint(return_remap_weights[0], pltpu.HBM)
     ocean, surface = call(finish, [shape(2560, W), shape(64, W)], 4, 1, 5, [
         pltpu.VMEM(return_remap_weights.shape[1:], BF16), dma((2,)),
         pltpu.VMEM((512, W), F32), pltpu.VMEM((512, W), F32), pltpu.VMEM((256, W), F32),
     ])(
         comp, back_owner, back_src_blk, back_dst_blk,
-        return_weights, advected, received, levels, mine, other,
+        in_hbm(return_remap_weights[0]), advected, received, levels, mine, other,
     )
     return (
         dss.reshape(1, 72, 32, W),

time: 86.9 us -> 85.8 us (0.987)
  local copies, waits for them, and re-layouts: 5.71 us -> 3.62 us
  waiting for transfers between devices: 24.9 us -> 26.8 us
    unnamed x39 -> x35, local copies, waits for them, and re-layouts: 5.6 us -> 3.52 us
    ppermute x6, waiting for transfers between devices: 12.6 us -> 14.5 us  [shifted(): return lax.ppermute(array, axis, pairs)]
  transfers between devices with their start and end apart: 7 -> 7, of which waited for: 5 -> 6; matrix products, arithmetic and copies ran while one was open for 0% -> 0% of each run, Pallas kernels for 19% -> 19%
where the time goes in v5:
time: 85.8 us; the launch traced here: 85.4 us
  starting transfers between devices  28 us (33%)
  waiting for transfers between devices  26.8 us (31%)
  Pallas kernels  25.9 us (30%)
  local copies, waits for them, and re-layouts  3.62 us (4%)
  between operations  0.92 us (1%)
    pallas_call x1, Pallas kernels, shards(): call(advect_all, [shape(16 * 160, W), shape(72 * 32, W)], 2, 0, 9, [point...  15.1 us
    ppermute x6, starting transfers between devices, shifted(): return lax.ppermute(array, axis, pairs)  15 us
    ppermute x6, waiting for transfers between devices, shifted(): return lax.ppermute(array, axis, pairs)  14.5 us
    all_to_all x1, starting transfers between devices, shards(): lax.all_to_all(send.reshape(band, TILES_PER_PEER, 16, W), 'gx', 0, 0, til...  13 us
    all_to_all x1, waiting for transfers between devices, shards(): lax.all_to_all(send.reshape(band, TILES_PER_PEER, 16, W), 'gx', 0, 0, til...  12.3 us
    pallas_call x1, Pallas kernels, shards(): call(finish, [shape(2560, W), shape(64, W)], 4, 1, 5, [pltpu.VMEM(return_...  4.19 us
    unnamed x35, local copies, waits for them, and re-layouts  3.52 us
    pallas_call x1, Pallas kernels, shards(): call(tile_products, [shape(band * TILES_PER_PEER, 16, W, dtype=BF16)], 4,...  2.17 us
  transfers between devices with their start and end apart: 7, of which 6 were waited for; matrix products, arithmetic and copies ran while one was open for 0% of the time, Pallas kernels for 19%

profile of v5, /device:TPU:1, one launch (start us, length us, event | category | flops | bytes accessed | tf_op | source)
XLA Modules:
  0.0 85.4 jit_solution(10760811047623793392)
XLA Ops:
  0.6 0.0 copy-start.16
  0.6 0.0 copy-start
  0.7 0.0 copy-start.1
  0.7 0.0 copy-start.7
  0.7 1.8 %pack_rows.1 = (bf16[704,128]{1,0:T(8,128)(2,1)S(1)}, bf16[704,128]{1,0:T(8,128)(2,1)S(1)}, f32[128,128]{1,0:T(8,128)S(1)}) custom-call(s32[1]{0:T(128)} %bitcast.comp, f32[2304,128]{1,0:T(8,128)} %bitcast.23, f32[2560,128]{1,0:T(8,128)} %bitcast.20, f32[32,128]{1,0:T(8,128)} %mass.3, s32[96,128]{1,0:T(8,128)} %bitcast.32, f32[96,128]{1,0:T(8,128)} %bitcast.33), custom_call_target="tpu_custom_call" | custom-call | tf_op jit(solution)/shard_map/pack_rows/pallas_call | solution.py:693
  2.5 0.0 copy-start.15
  2.5 4.0 %collective-permute-start = (bf16[704,128]{1,0:T(8,128)(2,1)S(1)}, bf16[704,128]{1,0:T(8,128)(2,1)S(1)}, u32[]{:S(2)}, u32[]{:S(2)}) collective-permute-start(bf16[704,128]{1,0:T(8,128)(2,1)S(1)} %get-tuple-element.24), channel_id=1, source_target_pairs={{0,1},{1,2},{2,3},{4,5},{5,6},{6,7},{8,9},{9,10},{10,11},{12,13},{... | collective-permute-start | bytes 540680 | tf_op jit(solution)/shard_map/ppermute | solution.py:659
  6.5 1.3 %collective-permute-start.1 = (bf16[704,128]{1,0:T(8,128)(2,1)S(1)}, bf16[704,128]{1,0:T(8,128)(2,1)S(1)}, u32[]{:S(2)}, u32[]{:S(2)}) collective-permute-start(bf16[704,128]{1,0:T(8,128)(2,1)S(1)} %get-tuple-element.25), channel_id=1, source_target_pairs={{1,0},{2,1},{3,2},{5,4},{6,5},{7,6},{9,8},{10,9},{11,10},{13,12},{... | collective-permute-start | bytes 540680 | tf_op jit(solution)/shard_map/ppermute | solution.py:659
  7.8 0.0 copy-done.16
  7.8 0.1 slice_reduce_fusion
  7.8 0.0 copy-done
  7.8 0.0 copy-done.1
  7.9 0.0 copy-done.7
  7.9 0.0 copy-start.10
  7.9 0.5 pack_columns.1
  8.4 0.0 copy-done.15
  8.4 0.0 copy-start.4
  8.4 0.0 copy-start.11
  8.4 0.0 copy-start.12
  8.4 0.0 copy-start.13
  8.4 0.1 fusion.1
  8.6 1.3 %collective-permute-done.above = bf16[704,128]{1,0:T(8,128)(2,1)S(1)} collective-permute-done((bf16[704,128]{1,0:T(8,128)(2,1)S(1)}, bf16[704,128]{1,0:T(8,128)(2,1)S(1)}, u32[]{:S(2)}, u32[]{:S(2)}) %collective-permute-start) | collective-permute-done | bytes 180256 | tf_op jit(solution)/shard_map/ppermute | solution.py:659
  9.9 3.8 %collective-permute-done.1.below = bf16[704,128]{1,0:T(8,128)(2,1)S(1)} collective-permute-done((bf16[704,128]{1,0:T(8,128)(2,1)S(1)}, bf16[704,128]{1,0:T(8,128)(2,1)S(1)}, u32[]{:S(2)}, u32[]{:S(2)}) %collective-permute-start.1) | collective-permute-done | bytes 180256 | tf_op jit(solution)/shard_map/ppermute | solution.py:659
  13.7 0.2 finish_columns.1
  13.9 3.2 %collective-permute-start.2 = (bf16[176,128]{1,0:T(8,128)(2,1)S(1)}, bf16[176,128]{1,0:T(8,128)(2,1)S(1)}, u32[]{:S(2)}, u32[]{:S(2)}) collective-permute-start(bf16[176,128]{1,0:T(8,128)(2,1)S(1)} %get-tuple-element.28), channel_id=1, source_target_pairs={{0,4},{4,8},{8,12},{12,16},{16,20},{20,24},{24,28},{28,32},{32,36}... | collective-permute-start | bytes 135176 | tf_op jit(solution)/shard_map/ppermute | solution.py:659
  17.1 1.3 %collective-permute-start.3 = (bf16[176,128]{1,0:T(8,128)(2,1)S(1)}, bf16[176,128]{1,0:T(8,128)(2,1)S(1)}, u32[]{:S(2)}, u32[]{:S(2)}) collective-permute-start(bf16[176,128]{1,0:T(8,128)(2,1)S(1)} %get-tuple-element.29), channel_id=1, source_target_pairs={{4,0},{8,4},{12,8},{16,12},{20,16},{24,20},{28,24},{32,28},{36,32}... | collective-permute-start | bytes 135176 | tf_op jit(solution)/shard_map/ppermute | solution.py:659
  18.4 0.0 collective-permute-done.2.halo_l
  18.4 3.5 %collective-permute-done.3.halo_r = bf16[176,128]{1,0:T(8,128)(2,1)S(1)} collective-permute-done((bf16[176,128]{1,0:T(8,128)(2,1)S(1)}, bf16[176,128]{1,0:T(8,128)(2,1)S(1)}, u32[]{:S(2)}, u32[]{:S(2)}) %collective-permute-start.3) | collective-permute-done | bytes 45088 | tf_op jit(solution)/shard_map/ppermute | solution.py:659
  21.9 0.0 copy-done.10
  21.9 1.4 %assemble.1 = (bf16[32,32,128]{2,1,0:T(8,128)(2,1)S(1)}, bf16[32,16,128]{2,1,0:T(8,128)(2,1)S(1)}, bf16[2,16,128]{2,1,0:T(8,128)(2,1)S(1)}) custom-call(s32[1]{0:T(128)} %bitcast.comp, f32[80]{0:T(128)S(1)} %copy-done.10, f32[2560,128]{1,0:T(8,128)S(1)} %get-tuple-element.30.turned, f32[128,128]{1,0:T(8,128)S(1)} %get-tuple-element.23.rate8, ...), custom_call_target="tpu_custom_call" | custom-call | tf_op jit(solution)/shard_map/assemble/pallas_call | solution.py:725
  23.3 1.3 %collective-permute-start.4 = (bf16[32,16,128]{2,1,0:T(8,128)(2,1)S(1)}, bf16[32,16,128]{2,1,0:T(8,128)(2,1)S(1)}, u32[]{:S(2)}, u32[]{:S(2)}) collective-permute-start(bf16[32,16,128]{2,1,0:T(8,128)(2,1)S(1)} %get-tuple-element.32), channel_id=1, source_target_pairs={{0,128},{1,129},{2,130},{3,131},{4,132},{5,133},{6,134},{7,135},{8... | collective-permute-start | bytes 393224 | tf_op jit(solution)/shard_map/ppermute | solution.py:659
  24.6 5.3 %collective-permute-done.4.arrived = bf16[32,16,128]{2,1,0:T(8,128)(2,1)S(1)} collective-permute-done((bf16[32,16,128]{2,1,0:T(8,128)(2,1)S(1)}, bf16[32,16,128]{2,1,0:T(8,128)(2,1)S(1)}, u32[]{:S(2)}, u32[]{:S(2)}) %collective-permute-start.4) | collective-permute-done | bytes 131104 | tf_op jit(solution)/shard_map/ppermute | solution.py:659
  30.0 0.0 copy-done.4
  30.0 0.0 copy-done.11
  30.0 0.0 copy-done.12
  30.0 0.0 copy-done.13
  30.0 2.2 %tile_products.1 = bf16[288,16,128]{2,1,0:T(8,128)(2,1)S(1)} custom-call(s32[1]{0:T(128)} %bitcast.comp, s32[1,64]{1,0:T(1,128)S(1)} %copy-done.11, s32[1,64]{1,0:T(1,128)S(1)} %bitcast.29, s32[1,64]{1,0:T(1,128)S(1)} %copy-done.13, bf16[32,32,128]{2,1,0:T(8,128)(2,1)S(1)} %get-tuple-element.31.own, bf16[32,16,128]{2,1,0:T(8,128)(2,1)S(1)} %collective-permute-done.4.arrived, ...), custom_call_target="tpu_custom_call" | custom-call | tf_op jit(solution)/shard_map/tile_products/pallas_call | solution.py:742
  32.1 0.0 copy-start.3
  32.2 1.0 %copy-done.3 = bf16[288,16,128]{2,1,0:T(8,128)(2,1)} copy-done((bf16[288,16,128]{2,1,0:T(8,128)(2,1)}, bf16[288,16,128]{2,1,0:T(8,128)(2,1)S(1)}, u32[]{:S(2)}) %copy-start.3) | copy-done | bytes 1179672
  33.2 13.0 %all-to-all-start = ((bf16[32,9,16,128]{3,2,1,0:T(8,128)(2,1)}), bf16[32,9,16,128]{3,2,1,0:T(8,128)(2,1)S(1)}, u32[]{:S(2)}, u32[]{:S(2)}) async-start(bf16[32,9,16,128]{3,2,1,0:T(8,128)(2,1)} %bitcast.26), calls=%async_computation | async-start | bytes 2359296 | tf_op jit(solution)/shard_map/all_to_all | solution.py:756
  46.2 0.1 copy.20
  46.3 0.0 copy-start.2
  46.3 1.3 %copy-done.2 = f32[1,72,32,128]{3,2,1,0:T(8,128)S(1)} copy-done((f32[1,72,32,128]{3,2,1,0:T(8,128)S(1)}, f32[1,72,32,128]{3,2,1,0:T(8,128)}, u32[]{:S(2)}) %copy-start.2) | copy-done | bytes 1179672
  47.6 0.0 copy-start.8
  47.6 0.0 copy-start.9
  47.6 15.1 %advect_all.1 = (f32[2560,128]{1,0:T(8,128)S(1)}, f32[2304,128]{1,0:T(8,128)}) custom-call(s32[1]{0:T(128)} %bitcast.comp, f32[80]{0:T(128)S(1)} %copy-done.10, f32[2304,128]{1,0:T(8,128)S(1)} %bitcast.25, f32[2560,128]{1,0:T(8,128)S(1)} %bitcast.22, f32[32,128]{1,0:T(8,128)S(1)} %copy-done.7, f32[128,128]{1,0:T(8,128)S(1)} %get-tuple-element.23.rate8, ...), custom_call_target="tpu_custom_call" | custom-call | tf_op jit(solution)/shard_map/advect_all/pallas_call | solution.py:760
  62.6 0.0 copy-start.5
  62.6 1.1 %copy-done.5 = f32[2560,128]{1,0:T(8,128)} copy-done((f32[2560,128]{1,0:T(8,128)}, f32[2560,128]{1,0:T(8,128)S(1)}, u32[]{:S(2)}) %copy-start.5) | copy-done | bytes 1310744
  63.7 0.0 copy-start.14
  63.7 12.3 %all-to-all-done = bf16[32,9,16,128]{3,2,1,0:T(8,128)(2,1)S(1)} async-done(((bf16[32,9,16,128]{3,2,1,0:T(8,128)(2,1)}), bf16[32,9,16,128]{3,2,1,0:T(8,128)(2,1)S(1)}, u32[]{:S(2)}, u32[]{:S(2)}) %all-to-all-start) | async-done | bytes 1179680 | tf_op jit(solution)/shard_map/all_to_all | solution.py:756
  76.0 0.0 copy-start.6
  76.0 4.0 %collective-permute-start.5 = (bf16[64,16,128]{2,1,0:T(8,128)(2,1)S(1)}, bf16[64,16,128]{2,1,0:T(8,128)(2,1)S(1)}, u32[]{:S(2)}, u32[]{:S(2)}) collective-permute-start(bf16[64,16,128]{2,1,0:T(8,128)(2,1)S(1)} %bitcast.31), channel_id=1, source_target_pairs={{128,0},{129,1},{130,2},{131,3},{132,4},{133,5},{134,6},{135,7},{1... | collective-permute-start | bytes 786440 | tf_op jit(solution)/shard_map/ppermute | solution.py:659
  80.0 0.0 copy-done.8
  80.1 0.0 copy-done.9
  80.1 0.6 surface_select.1.mine
  80.6 0.6 collective-permute-done.5.other
  81.2 0.0 copy-done.14
  81.2 0.0 copy-done.6
  81.2 4.2 %finish.1 = (f32[2560,128]{1,0:T(8,128)}, f32[64,128]{1,0:T(8,128)}) custom-call(s32[1]{0:T(128)} %bitcast.comp, s32[1,64]{1,0:T(1,128)S(1)} %copy-done.8, s32[1,64]{1,0:T(1,128)S(1)} %copy-done.9, s32[1,64]{1,0:T(1,128)S(1)} %copy-done.14, bf16[64,128,128]{2,1,0:T(8,128)(2,1)} %bitcast.30, f32[2560,128]{1,0:T(8,128)S(1)} %copy-done.6, ...), custom_call_target="tpu_custom_call" | custom-call | tf_op jit(solution)/shard_map/finish/pallas_call | solution.py:778
  (4 shorter events, 0.1 us)
Async XLA Ops:
  0.6 7.1 %copy-start.16 = (f32[2,80,16]{1,2,0:T(8,128)S(1)}, f32[2,80,16]{1,2,0:T(8,128)}, u32[]{:S(2)}) copy-start(f32[2,80,16]{1,2,0:T(8,128)} %param.27) | copy-start | bytes 30724
  0.6 7.2 %copy-start = (f32[1,2,80,16,128]{4,3,2,1,0:T(8,128)S(1)}, f32[1,2,80,16,128]{4,3,2,1,0:T(8,128)}, u32[]{:S(2)}) copy-start(f32[1,2,80,16,128]{4,3,2,1,0:T(8,128)} %param.23) | copy-start | bytes 3932164
  0.7 7.2 %copy-start.1 = (f32[1,72,32,128]{3,2,1,0:T(8,128)S(1)}, f32[1,72,32,128]{3,2,1,0:T(8,128)}, u32[]{:S(2)}) copy-start(f32[1,72,32,128]{3,2,1,0:T(8,128)} %param.16) | copy-start | bytes 3538948
  0.7 7.2 %copy-start.7 = (f32[32,128]{1,0:T(8,128)S(1)}, f32[32,128]{1,0:T(8,128)}, u32[]{:S(2)}) copy-start(f32[32,128]{1,0:T(8,128)} %mass.3) | copy-start | bytes 49156
  2.5 5.9 %copy-start.15 = (f32[16,72]{1,0:T(8,128)S(1)}, f32[16,72]{1,0:T(8,128)}, u32[]{:S(2)}) copy-start(f32[16,72]{1,0:T(8,128)} %param.18) | copy-start | bytes 13828
  2.5 7.4 %collective-permute-start = (bf16[704,128]{1,0:T(8,128)(2,1)S(1)}, bf16[704,128]{1,0:T(8,128)(2,1)S(1)}, u32[]{:S(2)}, u32[]{:S(2)}) collective-permute-start(bf16[704,128]{1,0:T(8,128)(2,1)S(1)} %get-tuple-element.24), channel_id=1, source_target_pairs={{0,1},{1,2},{2,3},{4,5},{5,6},{6,7},{8,9},{9,10},{10,11},{12,13},{... | collective-permute-start | bytes 540680 | tf_op jit(solution)/shard_map/ppermute | solution.py:659
  6.5 7.3 %collective-permute-start.1 = (bf16[704,128]{1,0:T(8,128)(2,1)S(1)}, bf16[704,128]{1,0:T(8,128)(2,1)S(1)}, u32[]{:S(2)}, u32[]{:S(2)}) collective-permute-start(bf16[704,128]{1,0:T(8,128)(2,1)S(1)} %get-tuple-element.25), channel_id=1, source_target_pairs={{1,0},{2,1},{3,2},{5,4},{6,5},{7,6},{9,8},{10,9},{11,10},{13,12},{... | collective-permute-start | bytes 540680 | tf_op jit(solution)/shard_map/ppermute | solution.py:659
  7.9 14.0 %copy-start.10 = (f32[80]{0:T(128)S(1)}, f32[80]{0:T(128)}, u32[]{:S(2)}) copy-start(f32[80]{0:T(128)} %lev_speed.3) | copy-start | bytes 964
  8.4 21.6 %copy-start.4 = (bf16[1,64,128,128]{3,2,1,0:T(8,128)(2,1)S(1)}, bf16[1,64,128,128]{3,2,1,0:T(8,128)(2,1)}, u32[]{:S(2)}) copy-start(bf16[1,64,128,128]{3,2,1,0:T(8,128)(2,1)} %param.22) | copy-start | bytes 6291460
  8.4 21.5 %copy-start.11 = (s32[1,64]{1,0:T(1,128)S(1)}, s32[1,64]{1,0:T(1,128)}, u32[]{:S(2)}) copy-start(s32[1,64]{1,0:T(1,128)} %src.1) | copy-start | bytes 772
  8.4 21.5 %copy-start.12 = (s32[1,64,1]{1,2,0:T(1,128)S(1)}, s32[1,64,1]{1,2,0:T(1,128)}, u32[]{:S(2)}) copy-start(s32[1,64,1]{1,2,0:T(1,128)} %param.19) | copy-start | bytes 772
  8.4 21.5 %copy-start.13 = (s32[1,64]{1,0:T(1,128)S(1)}, s32[1,64]{1,0:T(1,128)}, u32[]{:S(2)}) copy-start(s32[1,64]{1,0:T(1,128)} %dst.1) | copy-start | bytes 772
  13.9 4.5 %collective-permute-start.2 = (bf16[176,128]{1,0:T(8,128)(2,1)S(1)}, bf16[176,128]{1,0:T(8,128)(2,1)S(1)}, u32[]{:S(2)}, u32[]{:S(2)}) collective-permute-start(bf16[176,128]{1,0:T(8,128)(2,1)S(1)} %get-tuple-element.28), channel_id=1, source_target_pairs={{0,4},{4,8},{8,12},{12,16},{16,20},{20,24},{24,28},{28,32},{32,36}... | collective-permute-start | bytes 135176 | tf_op jit(solution)/shard_map/ppermute | solution.py:659
  17.1 4.8 %collective-permute-start.3 = (bf16[176,128]{1,0:T(8,128)(2,1)S(1)}, bf16[176,128]{1,0:T(8,128)(2,1)S(1)}, u32[]{:S(2)}, u32[]{:S(2)}) collective-permute-start(bf16[176,128]{1,0:T(8,128)(2,1)S(1)} %get-tuple-element.29), channel_id=1, source_target_pairs={{4,0},{8,4},{12,8},{16,12},{20,16},{24,20},{28,24},{32,28},{36,32}... | collective-permute-start | bytes 135176 | tf_op jit(solution)/shard_map/ppermute | solution.py:659
  23.3 6.6 %collective-permute-start.4 = (bf16[32,16,128]{2,1,0:T(8,128)(2,1)S(1)}, bf16[32,16,128]{2,1,0:T(8,128)(2,1)S(1)}, u32[]{:S(2)}, u32[]{:S(2)}) collective-permute-start(bf16[32,16,128]{2,1,0:T(8,128)(2,1)S(1)} %get-tuple-element.32), channel_id=1, source_target_pairs={{0,128},{1,129},{2,130},{3,131},{4,132},{5,133},{6,134},{7,135},{8... | collective-permute-start | bytes 393224 | tf_op jit(solution)/shard_map/ppermute | solution.py:659
  32.1 1.0 %copy-start.3 = (bf16[288,16,128]{2,1,0:T(8,128)(2,1)}, bf16[288,16,128]{2,1,0:T(8,128)(2,1)S(1)}, u32[]{:S(2)}) copy-start(bf16[288,16,128]{2,1,0:T(8,128)(2,1)S(1)} %tile_products.1) | copy-start | bytes 3538948
  33.2 42.8 %all-to-all-start = ((bf16[32,9,16,128]{3,2,1,0:T(8,128)(2,1)}), bf16[32,9,16,128]{3,2,1,0:T(8,128)(2,1)S(1)}, u32[]{:S(2)}, u32[]{:S(2)}) async-start(bf16[32,9,16,128]{3,2,1,0:T(8,128)(2,1)} %bitcast.26), calls=%async_computation | async-start | bytes 2359296 | tf_op jit(solution)/shard_map/all_to_all | solution.py:756
  46.3 1.3 %copy-start.2 = (f32[1,72,32,128]{3,2,1,0:T(8,128)S(1)}, f32[1,72,32,128]{3,2,1,0:T(8,128)}, u32[]{:S(2)}) copy-start(f32[1,72,32,128]{3,2,1,0:T(8,128)} %param.16) | copy-start | bytes 3538948
  47.6 32.5 %copy-start.8 = (s32[1,64]{1,0:T(1,128)S(1)}, s32[1,64]{1,0:T(1,128)}, u32[]{:S(2)}) copy-start(s32[1,64]{1,0:T(1,128)} %back_owner.3) | copy-start | bytes 772
  47.6 32.5 %copy-start.9 = (s32[1,64]{1,0:T(1,128)S(1)}, s32[1,64]{1,0:T(1,128)}, u32[]{:S(2)}) copy-start(s32[1,64]{1,0:T(1,128)} %back_src.3) | copy-start | bytes 772
  62.6 1.1 %copy-start.5 = (f32[2560,128]{1,0:T(8,128)}, f32[2560,128]{1,0:T(8,128)S(1)}, u32[]{:S(2)}) copy-start(f32[2560,128]{1,0:T(8,128)S(1)} %get-tuple-element.38.advected) | copy-start | bytes 3932164
  63.7 17.5 %copy-start.14 = (s32[1,64]{1,0:T(1,128)S(1)}, s32[1,64]{1,0:T(1,128)}, u32[]{:S(2)}) copy-start(s32[1,64]{1,0:T(1,128)} %back_dst.1) | copy-start | bytes 772
  76.0 5.2 %copy-start.6 = (f32[2560,128]{1,0:T(8,128)S(1)}, f32[2560,128]{1,0:T(8,128)}, u32[]{:S(2)}) copy-start(f32[2560,128]{1,0:T(8,128)} %copy-done.5) | copy-start | bytes 3932164
  76.0 5.1 %collective-permute-start.5 = (bf16[64,16,128]{2,1,0:T(8,128)(2,1)S(1)}, bf16[64,16,128]{2,1,0:T(8,128)(2,1)S(1)}, u32[]{:S(2)}, u32[]{:S(2)}) collective-permute-start(bf16[64,16,128]{2,1,0:T(8,128)(2,1)S(1)} %bitcast.31), channel_id=1, source_target_pairs={{128,0},{129,1},{130,2},{131,3},{132,4},{133,5},{134,6},{135,7},{1... | collective-permute-start | bytes 786440 | tf_op jit(solution)/shard_map/ppermute | solution.py:659
